TPU v7x, 512 devices: a whole 4x8x8 slice. The times are simulated.
512 devices in a mesh: pages: 16 (over y, core), row: 8 (over z), col: 4 (over x).
Axes of the slice: x: 4, y: 8, z: 8, core: 2. Of those that a mesh axis runs over, the one named last changes fastest.
Arguments:
- residual: bfloat16 [512, 2, 2048], P('pages', None, ('row', 'col')), may hold values from -6 to 6
- fresh_qkv: bfloat16 [512, 2, 3, 2048], P('pages', None, None, 'col'), may hold values from -27 to 27
- prefix_pages: bfloat16 [256, 2, 128, 2048], P('pages', None, 'row', 'col'), may hold values from -6 to 6
- tail_pages: bfloat16 [512, 2, 128, 2048], P('pages', None, 'row', 'col'), may hold values from -6 to 6
- prefix_item: int32 [256], replicated, may hold values from 0 to 255, as said below
- tail_item: int32 [512], replicated, may hold values from 0 to 511, as said below
- prefix_length: int32 [32], replicated, may hold values from 1 to 1024, 20480 in all
- tail_length: int32 [512], replicated, may hold values from 1 to 128, 40960 in all
- out_weight: bfloat16 [2048, 2048], P('col', 'row'), may hold values from -0.125 to 0.125
- out_bias: bfloat16 [2048], P(('row', 'col')), may hold values from -4 to 4
- mlp_gain: bfloat16 [2048], P('row'), may hold values from 0.25 to 1.75
- mlp_shift: bfloat16 [2048], P('row'), may hold values from -4 to 4
- up_weight: bfloat16 [2048, 8192], P('row', 'col'), may hold values from -0.125 to 0.125
- up_bias: bfloat16 [8192], P(('col', 'row')), may hold values from -4 to 4
- down_weight: bfloat16 [8192, 2048], P('col', 'row'), may hold values from -0.0625 to 0.0625
- down_bias: bfloat16 [2048], P(('row', 'col')), may hold values from -4 to 4
- next_gain: bfloat16 [2048], P('row'), may hold values from 0.25 to 1.75
- next_shift: bfloat16 [2048], P('row'), may hold values from -4 to 4
- score_weight: bfloat16 [2048], P('row'), may hold values from -0.125 to 0.125
- qkv_weight: bfloat16 [2048, 6144], P('row', 'col'), may hold values from -0.125 to 0.125
- qkv_bias: bfloat16 [6144], P(('col', 'row')), may hold values from -4 to 4
Outputs:
- layer_out: bfloat16 [512, 2, 2048], P('pages', None, ('row', 'col'))
- score_out: float32 [512, 2], P('pages')
- projected_next: bfloat16 [512, 2, 6144], P('pages', None, ('col', 'row'))
Inputs may be any that keep to these rules, and one draw needn't show every extreme that they name: `prefix_item`: each of the 256 prompt pages is held by exactly one slot; slot h * 16 + g + k (k < 1) holds a page of one of the prompts g * 2 to (g + 1) * 2 - 1. `tail_item`: each continuation's tail is held by exactly one slot; slot h * 32 + g * 2 + k (k < 2) holds the tail of one of the continuations g * 32 to (g + 1) * 32 - 1. `prefix_length`: some prompt has exactly 1024 cached tokens. `tail_length`: some continuation has exactly 128 tail tokens.
All inputs are finite; a program needn't handle non-finite values.
Results may differ from a plain program's by a relative error of at most 0.023.
Values may be sent and summed in bfloat16 or wider, within the bound.
No kernel may reach another device: no remote copies, remote signals or barrier semaphores. Data moves between devices by JAX's collectives and lax.ppermute only.
A program may use at most 64 MiB of HBM per device.

v0:
```python
import math

import jax
import jax.numpy as jnp
from jax import lax
from jax.sharding import PartitionSpec as P

D = 2048
H = 16
HD = 128
PAGE = 128
MAXPAGES = 8
CONT = 16


masked_score = -1e30
norm_eps = 1e-05


def combined_all(shard, axis, combine):
    everything = jax.tree.map(lambda part: lax.all_gather(part, axis), shard)
    first = jax.tree.map(lambda part: part[0], everything)

    def step(k, so_far):
        return combine(so_far, jax.tree.map(lambda part: part[k], everything))

    return lax.fori_loop(1, lax.axis_size(axis), step, first)


def head_slopes(first_head, how_many):
    head_index = first_head + jnp.arange(how_many, dtype=jnp.int32)
    return jnp.exp2(-8.0 * (head_index + 1).astype(jnp.float32) / H)


def slot_partials(queries, page_keys, page_values, usable, offset, slopes):
    scores = jnp.einsum(
        "sqhd,skhd->sqhk", queries, page_keys, preferred_element_type=jnp.float32
    ) / math.sqrt(HD)
    scores = scores + slopes[None, None, :, None] * offset[:, :, None, :]
    usable_full = usable[:, :, None, :]
    scores = jnp.where(usable_full, scores, masked_score)
    maxima = jnp.max(scores, axis=3)
    weights = jnp.where(usable_full, jnp.exp(scores - maxima[..., None]), 0.0)
    totals = jnp.sum(weights, axis=3)
    outputs = jnp.einsum(
        "sqhk,skhd->sqhd", weights, page_values.astype(jnp.float32), precision=lax.Precision.HIGHEST
    )
    return (maxima, totals, outputs)


def merge_pair(left_part, right_part):
    left_max, left_total, left_out = left_part
    right_max, right_total, right_out = right_part
    joined = jnp.maximum(left_max, right_max)
    left_scale = jnp.exp(left_max - joined)
    right_scale = jnp.exp(right_max - joined)
    return (
        joined,
        left_scale * left_total + right_scale * right_total,
        left_scale[..., None] * left_out + right_scale[..., None] * right_out,
    )


def fold_sources(maxima, totals, outputs):
    joined = jnp.max(maxima, axis=0)
    rescale = jnp.exp(maxima - joined[None])
    return (
        joined,
        jnp.sum(rescale * totals, axis=0),
        jnp.sum(rescale[..., None] * outputs, axis=0),
    )


def cache_partials(
    queries,
    page_block,
    page_item,
    tail_block,
    tail_owner,
    prefix_length,
    tail_length,
    row_index,
    slopes,
):
    cont_count = queries.shape[0]
    prompts = cont_count // CONT
    head_count = queries.shape[2]
    slot_count = page_block.shape[0]
    tokens = page_block.shape[2]
    token_index = row_index * tokens + jnp.arange(tokens, dtype=jnp.int32)
    step_index = jnp.arange(2, dtype=jnp.int32)
    slot_prompt = page_item // MAXPAGES
    slot_page = page_item % MAXPAGES
    by_prompt = queries.reshape(prompts, CONT * 2, head_count, HD)
    key_pos = slot_page[:, None] * PAGE + token_index[None, :]
    slot_len = prefix_length[slot_prompt]
    slot_tails = tail_length.reshape(prompts, CONT)[slot_prompt]
    query_pos = (
        slot_len[:, None, None] + slot_tails[:, :, None] + step_index[None, None, :]
    ).reshape(slot_count, CONT * 2)
    offset = (key_pos[:, None, :] - query_pos[:, :, None]).astype(jnp.float32)
    usable = jnp.broadcast_to((key_pos < slot_len[:, None])[:, None, :], offset.shape)
    page_keys = page_block[:, 0].reshape(slot_count, tokens, head_count, HD)
    page_values = page_block[:, 1].reshape(slot_count, tokens, head_count, HD)
    maxima, totals, outputs = slot_partials(
        by_prompt[slot_prompt], page_keys, page_values, usable, offset, slopes
    )
    prompt_max = (
        jnp.full((prompts, CONT * 2, head_count), masked_score, jnp.float32)
        .at[slot_prompt]
        .max(maxima)
    )
    rescale = jnp.exp(maxima - prompt_max[slot_prompt])
    prompt_total = (
        jnp.zeros((prompts, CONT * 2, head_count), jnp.float32)
        .at[slot_prompt]
        .add(rescale * totals)
    )
    prompt_out = (
        jnp.zeros((prompts, CONT * 2, head_count, HD), jnp.float32)
        .at[slot_prompt]
        .add(rescale[..., None] * outputs)
    )
    prefix_part = (
        prompt_max.reshape(cont_count, 2, head_count),
        prompt_total.reshape(cont_count, 2, head_count),
        prompt_out.reshape(cont_count, 2, head_count, HD),
    )
    tail_count = tail_block.shape[0]
    tail_lens = tail_length[tail_owner]
    tail_usable = jnp.broadcast_to(
        (token_index[None, :] < tail_lens[:, None])[:, None, :], (tail_count, 2, tokens)
    )
    tail_offset = (
        token_index[None, None, :] - tail_lens[:, None, None] - step_index[None, :, None]
    ).astype(jnp.float32)
    tail_keys = tail_block[:, 0].reshape(tail_count, tokens, head_count, HD)
    tail_values = tail_block[:, 1].reshape(tail_count, tokens, head_count, HD)
    tail_max, tail_total, tail_out = slot_partials(
        queries[tail_owner], tail_keys, tail_values, tail_usable, tail_offset, slopes
    )
    cont_max = (
        jnp.full((cont_count, 2, head_count), masked_score, jnp.float32)
        .at[tail_owner]
        .set(tail_max)
    )
    cont_total = jnp.zeros((cont_count, 2, head_count), jnp.float32).at[tail_owner].set(tail_total)
    cont_out = jnp.zeros((cont_count, 2, head_count, HD), jnp.float32).at[tail_owner].set(tail_out)
    return merge_pair(prefix_part, (cont_max, cont_total, cont_out))


def normalize(values, sum_one, sum_two, gain, shift):
    center = sum_one / D
    spread = sum_two / D - center * center
    return (
        (values - center[:, None])
        * lax.rsqrt(spread + norm_eps)[:, None]
        * gain.astype(jnp.float32)
        + shift.astype(jnp.float32)
    ).astype(jnp.bfloat16)


def shards(
    residual,
    fresh_qkv,
    prefix_pages,
    tail_pages,
    prefix_item,
    tail_item,
    prefix_length,
    tail_length,
    out_weight,
    out_bias,
    mlp_gain,
    mlp_shift,
    up_weight,
    up_bias,
    down_weight,
    down_bias,
    next_gain,
    next_shift,
    score_weight,
    qkv_weight,
    qkv_bias,
):
    group_index = lax.axis_index("pages")
    row_index = lax.axis_index("row")
    col_index = lax.axis_index("col")
    group_count = lax.axis_size("pages")
    cont_local = residual.shape[0]
    row_total = cont_local * 2
    share = residual.shape[2]
    head_count = fresh_qkv.shape[3] // HD
    slopes = head_slopes(col_index * head_count, head_count)
    fresh_rows = fresh_qkv.reshape(cont_local, 2, 3, head_count, HD)
    slot_count = prefix_pages.shape[0]
    tail_slots = tail_pages.shape[0]
    everyone = lax.all_gather(fresh_qkv[:, :, 0], "pages", axis=0, tiled=True)
    page_item = lax.dynamic_slice_in_dim(prefix_item, group_index * slot_count, slot_count)
    tail_owner = lax.dynamic_slice_in_dim(tail_item, group_index * tail_slots, tail_slots)
    maxima, totals, outputs = cache_partials(
        everyone.reshape(everyone.shape[0], 2, head_count, HD),
        prefix_pages,
        page_item,
        tail_pages,
        tail_owner,
        prefix_length,
        tail_length,
        row_index,
        slopes,
    )
    maxima, totals, outputs = (
        lax.all_to_all(
            maxima.reshape(group_count, row_total, head_count),
            "pages",
            split_axis=0,
            concat_axis=0,
            tiled=True,
        ),
        lax.all_to_all(
            totals.reshape(group_count, row_total, head_count),
            "pages",
            split_axis=0,
            concat_axis=0,
            tiled=True,
        ),
        lax.all_to_all(
            outputs.reshape(group_count, row_total, head_count, HD),
            "pages",
            split_axis=0,
            concat_axis=0,
            tiled=True,
        ),
    )
    cache_max, cache_total, cache_out = fold_sources(maxima, totals, outputs)
    cache_max, cache_total, cache_out = combined_all(
        (cache_max, cache_total, cache_out), "row", merge_pair
    )
    step_index = jnp.arange(2, dtype=jnp.int32)
    new_usable = jnp.broadcast_to(
        (step_index[None, :] <= step_index[:, None])[None], (cont_local, 2, 2)
    )
    new_offset = jnp.broadcast_to(
        (step_index[None, :] - step_index[:, None]).astype(jnp.float32)[None], (cont_local, 2, 2)
    )
    new_part = slot_partials(
        fresh_rows[:, :, 0],
        fresh_rows[:, :, 1],
        fresh_rows[:, :, 2],
        new_usable,
        new_offset,
        slopes,
    )
    joined_max, joined_total, joined_out = merge_pair(
        (
            cache_max.reshape(cont_local, 2, head_count),
            cache_total.reshape(cont_local, 2, head_count),
            cache_out.reshape(cont_local, 2, head_count, HD),
        ),
        new_part,
    )
    attended = (
        (joined_out / joined_total[..., None])
        .astype(jnp.bfloat16)
        .reshape(row_total, head_count * HD)
    )
    head_term = jnp.dot(attended, out_weight, preferred_element_type=jnp.float32)
    hidden_one = (
        residual.reshape(row_total, share).astype(jnp.float32)
        + lax.psum_scatter(head_term, "col", scatter_dimension=1, tiled=True)
        + out_bias.astype(jnp.float32)
    )
    gain_part = lax.dynamic_slice_in_dim(mlp_gain, col_index * share, share)
    shift_part = lax.dynamic_slice_in_dim(mlp_shift, col_index * share, share)
    sum_one, sum_two = lax.psum(
        (jnp.sum(hidden_one, axis=1), jnp.sum(hidden_one * hidden_one, axis=1)), ("row", "col")
    )
    normed_a = lax.all_gather(
        normalize(hidden_one, sum_one, sum_two, gain_part, shift_part), "col", axis=1, tiled=True
    )
    up_share = lax.psum_scatter(
        jnp.dot(normed_a, up_weight, preferred_element_type=jnp.float32),
        "row",
        scatter_dimension=1,
        tiled=True,
    )
    hidden_two = jax.nn.gelu(up_share + up_bias.astype(jnp.float32), approximate=True).astype(
        jnp.bfloat16
    )
    down_sum = jnp.dot(
        lax.all_gather(hidden_two, "row", axis=1, tiled=True),
        down_weight,
        preferred_element_type=jnp.float32,
    )
    down_share = lax.psum_scatter(
        down_sum.astype(jnp.bfloat16), "col", scatter_dimension=1, tiled=True
    ).astype(jnp.float32)
    layer_out = (hidden_one + down_share + down_bias.astype(jnp.float32)).astype(jnp.bfloat16)
    out_wide = layer_out.astype(jnp.float32)
    gain_part = lax.dynamic_slice_in_dim(next_gain, col_index * share, share)
    shift_part = lax.dynamic_slice_in_dim(next_shift, col_index * share, share)
    score_part = lax.dynamic_slice_in_dim(score_weight, col_index * share, share).astype(
        jnp.float32
    )
    sum_one, sum_two, score_sum = lax.psum(
        (
            jnp.sum(out_wide, axis=1),
            jnp.sum(out_wide * out_wide, axis=1),
            jnp.sum(out_wide * score_part, axis=1),
        ),
        ("row", "col"),
    )
    normed_b = lax.all_gather(
        normalize(out_wide, sum_one, sum_two, gain_part, shift_part), "col", axis=1, tiled=True
    )
    qkv_share = lax.psum_scatter(
        jnp.dot(normed_b, qkv_weight, preferred_element_type=jnp.float32).astype(jnp.bfloat16),
        "row",
        scatter_dimension=1,
        tiled=True,
    ).astype(jnp.float32)
    projected_next = (qkv_share + qkv_bias.astype(jnp.float32)).astype(jnp.bfloat16)
    return (
        layer_out.reshape(cont_local, 2, share),
        score_sum.reshape(cont_local, 2),
        projected_next.reshape(cont_local, 2, qkv_share.shape[1]),
    )


def solution(mesh):
    in_specs = (
        P("pages", None, ("row", "col")),
        P("pages", None, None, "col"),
        P("pages", None, "row", "col"),
        P("pages", None, "row", "col"),
        P(),
        P(),
        P(),
        P(),
        P("col", "row"),
        P(("row", "col")),
        P("row"),
        P("row"),
        P("row", "col"),
        P(("col", "row")),
        P("col", "row"),
        P(("row", "col")),
        P("row"),
        P("row"),
        P("row"),
        P("row", "col"),
        P(("col", "row")),
    )
    out_specs = (
        P("pages", None, ("row", "col")),
        P("pages", None),
        P("pages", None, ("col", "row")),
    )
    return jax.shard_map(shards, mesh=mesh, in_specs=in_specs, out_specs=out_specs, check_vma=False)
```

profile of v0, /device:TPU:2, one launch (start us, length us, event | category | flops | bytes accessed | tf_op | source)
XLA Modules:
  0.0 629.2 jit_solution(3406723916201025579)
XLA Ops:
  7.2 1.6 slice.33
  10.9 1.5 gather_fusion.3
  12.4 1.3 fusion.57
  19.9 35.8 %all-gather.9.cloned.1.call-done = bf16[512,2,1,512]{3,1,2,0:T(2,128)(2,1)} async-done(((bf16[32,2,1,512]{3,1,2,0:T(2,128)(2,1)}), bf16[512,2,1,512]{3,1,2,0:T(2,128)(2,1)}) %all-gather.9.cloned.1.call-update) | async-done | bytes 1048592 | tf_op jit(solution)/shard_map/all_gather | solution.py:198
  55.7 1.7 reshape_reshape.3
  57.7 1.4 gather_fusion.1
  59.1 1.5 fusion.61
  60.7 1.1 scatter_fusion
  62.6 1.5 reshape.233
  64.1 2.0 gather_fusion.4
  66.1 1.6 fusion.60
  70.2 1.1 scatter_fusion.2
  71.3 1.1 copy.151
  72.5 1.5 scatter_fusion.3
  74.2 1.5 scatter_fusion.1
  75.7 2.5 multiply_add_fusion
  78.2 1.3 copy.147
  80.2 4.6 all-to-all-start
  84.8 2.9 fusion.4
  89.6 2.6 scatter_fusion.4
  92.3 1.5 copy.158
  94.5 1.5 scatter_fusion.5
  96.0 7.2 %all-to-all-start.1 = ((f32[16,1,256]{2,1,0:T(1,128)}), f32[16,1,256]{2,1,0:T(1,128)S(1)}, u32[]{:S(2)}, u32[]{:S(2)}) async-start(f32[16,1,256]{2,1,0:T(1,128)} %reshape.385), calls=%async_computation.1 | async-start | bytes 32768 | tf_op jit(solution)/shard_map/all_to_all | solution.py:220
  103.2 6.1 fusion.3
  109.3 1.5 all-to-all-done.1
  110.8 5.7 all-to-all-start.2
  119.8 45.9 %all-to-all-done.2 = f32[16,64,4,128]{3,2,1,0:T(4,128)S(1)} async-done(((f32[16,64,4,128]{3,2,1,0:T(4,128)}), f32[16,64,4,128]{3,2,1,0:T(4,128)S(1)}, u32[]{:S(2)}, u32[]{:S(2)}) %all-to-all-start.2) | async-done | bytes 2097184 | tf_op jit(solution)/shard_map/all_to_all | solution.py:227
  165.7 2.9 multiply_reduce_fusion
  170.9 24.3 %all-gather.4 = f32[8,64,4]{1,2,0:T(4,128)S(1)} all-gather(f32[1,64,4]{1,2,0:T(4,128)S(1)} %copy.149), channel_id=3, replica_groups=mesh['pages'=16,'row'=8,'col'=4] {'row'}, dimensions={0}, use_global_device_ids=true | all-gather | bytes 9216 | tf_op jit(solution)/shard_map/all_gather | solution.py:21
  195.2 21.2 %all-gather.5 = f32[8,64,4]{1,2,0:T(4,128)S(1)} all-gather(f32[1,64,4]{1,2,0:T(4,128)S(1)} %copy.155), channel_id=4, replica_groups=mesh['pages'=16,'row'=8,'col'=4] {'row'}, dimensions={0}, use_global_device_ids=true | all-gather | bytes 9216 | tf_op jit(solution)/shard_map/all_gather | solution.py:21
  217.3 10.9 %while.19 = (s32[]{:T(128)}, f32[64,4]{0,1:T(4,128)S(1)}, f32[64,4]{0,1:T(4,128)S(1)}, f32[64,4,128]{2,1,0:T(4,128)S(1)}, f32[8,64,4]{1,2,0:T(4,128)S(1)}, /*ind...) while((s32[]{:T(128)}, f32[64,4]{0,1:T(4,128)S(1)}, ...), condition=%wide.region_14.15_spmd, body=%wide.region_13.14_spmd.sunk | while | flops 99845 | bytes 407703 | solution.py:27
  217.6 1.3 fusion.75
  219.1 1.3 fusion.75
  220.7 1.3 fusion.75
  222.2 1.3 fusion.75
  223.8 1.3 fusion.75
  225.4 1.3 fusion.75
  226.9 1.3 fusion.75
  230.1 20.7 %reduce-scatter.13.cloned.1.call-done = f32[64,64]{1,0:T(8,128)} async-done(((f32[256,64]{1,0:T(8,128)}), f32[64,64]{1,0:T(8,128)}) %reduce-scatter.13.cloned.1.call-update) | async-done | bytes 16400
  251.7 71.3 %all-reduce.1 = (f32[64]{0:T(128)S(1)}, f32[64]{0:T(128)S(1)}) all-reduce(f32[64]{0:T(128)S(1)} %get-tuple-element.200, f32[64]{0:T(128)S(1)} %get-tuple-element.199), channel_id=1, replica_groups=mesh['pages'=16,'row'=8,'col'=4] {'row','col'}, use_global_device_ids=true, to_apply=%region_21.22 | all-reduce | flops 128 | bytes 1024 | tf_op jit(solution)/shard_map/psum | solution.py:275
  323.3 12.8 %all_gather.37 = bf16[64,256]{0,1:T(8,128)(2,1)S(1)} all-gather(bf16[64,64]{0,1:T(8,128)(2,1)S(1)} %copy.179), channel_id=1, replica_groups=mesh['pages'=16,'row'=8,'col'=4] {'col'}, dimensions={1}, use_global_device_ids=true | all-gather | bytes 40960 | tf_op jit(solution)/shard_map/all_gather | solution.py:278
  336.0 1.1 fusion.63
  337.4 39.6 %reduce-scatter.11.cloned.1.call-done = f32[64,256]{1,0:T(8,128)} async-done(((f32[64,2048]{1,0:T(8,128)}), f32[64,256]{1,0:T(8,128)}) %reduce-scatter.11.cloned.1.call-update) | async-done | bytes 65552 | tf_op jit(solution)/shard_map/reduce_scatter | solution.py:281
  377.9 24.8 %all_gather.38 = bf16[64,2048]{1,0:T(8,128)(2,1)S(1)} all-gather(bf16[64,256]{1,0:T(8,128)(2,1)S(1)} %fusion.32), channel_id=1, replica_groups=mesh['pages'=16,'row'=8,'col'=4] {'row'}, dimensions={1}, use_global_device_ids=true | all-gather | bytes 294912 | tf_op jit(solution)/shard_map/all_gather | solution.py:291
  403.9 22.7 %reduce-scatter.15.cloned.1.call-done = bf16[64,64]{1,0:T(8,128)(2,1)} async-done(((bf16[256,64]{1,0:T(8,128)(2,1)}), bf16[64,64]{1,0:T(8,128)(2,1)}) %reduce-scatter.15.cloned.1.call-update) | async-done | bytes 8208
  427.7 137.9 %all-reduce = (f32[32,2]{1,0:T(8,128)S(1)}, f32[64]{0:T(128)S(1)}, f32[64]{0:T(128)S(1)}) all-reduce(f32[32,2]{1,0:T(8,128)S(1)} %reshape.245, f32[64]{0:T(128)S(1)} %get-tuple-element.202, f32[64]{0:T(128)S(1)} %get-tuple-element.201), channel_id=1, replica_groups=mesh['pages'=16,'row'=8,'col'=4] {'row','col'}, use_global_device_ids=true, to_apply=%region_25.26 | all-reduce | flops 192 | bytes 1536 | tf_op jit(solution)/shard_map/psum | solution.py:305
  565.8 14.2 %all_gather.39 = bf16[64,256]{0,1:T(8,128)(2,1)S(1)} all-gather(bf16[64,64]{0,1:T(8,128)(2,1)S(1)} %copy.180), channel_id=1, replica_groups=mesh['pages'=16,'row'=8,'col'=4] {'col'}, dimensions={1}, use_global_device_ids=true | all-gather | bytes 40960 | tf_op jit(solution)/shard_map/all_gather | solution.py:313
  581.9 38.9 %reduce-scatter.17.cloned.1.call-done = bf16[192,64]{1,0:T(8,128)(2,1)} async-done(((bf16[1536,64]{1,0:T(8,128)(2,1)}), bf16[192,64]{1,0:T(8,128)(2,1)}) %reduce-scatter.17.cloned.1.call-update) | async-done | bytes 24592
  (213 shorter events, 32.9 us)
Async XLA Ops:
  7.2 328.9 %copy-start = (bf16[256,2048]{1,0:T(8,128)(2,1)S(1)}, bf16[256,2048]{1,0:T(8,128)(2,1)}, u32[]{:S(2)}) copy-start(bf16[256,2048]{1,0:T(8,128)(2,1)} %param.35) | copy-start | bytes 3145732
  7.2 7.4 %copy-start.25 = (s32[256]{0:T(256)S(1)}, s32[256]{0:T(256)}, u32[]{:S(2)}) copy-start(s32[256]{0:T(256)} %param.27) | copy-start | bytes 3076
  7.2 8.1 %copy-start.1 = (s32[32]{0:T(128)S(1)}, s32[32]{0:T(128)}, u32[]{:S(2)}) copy-start(s32[32]{0:T(128)} %param.29) | copy-start | bytes 388
  7.2 48.5 %all-gather.9.cloned.1.call-start = ((), (), s32[]{:S(2)}) async-start(), calls=%async_computation.8 | async-start | bytes 1114112 | tf_op jit(solution)/shard_map/all_gather | solution.py:198
  9.6 0.5 copy-start.21
  10.2 0.8 copy-start.24
  10.9 5.5 copy-start.6
  14.8 55.5 %copy-start.19 = (s32[16]{0:T(128)}, s32[16]{0:T(128)S(1)}, u32[]{:S(2)}) copy-start(s32[16]{0:T(128)S(1)} %compare_select_fusion.1) | copy-start | bytes 196
  18.9 50.4 %copy-start.16 = (pred[16,16]{1,0:T(8,128)(4,1)}, pred[16,16]{1,0:T(8,128)(4,1)S(1)}, u32[]{:S(2)}) copy-start(pred[16,16]{1,0:T(8,128)(4,1)S(1)} %broadcast_compare_fusion.1) | copy-start | bytes 772
  19.0 49.6 %copy-start.17 = (pred[32,16]{1,0:T(8,128)(4,1)}, pred[32,16]{1,0:T(8,128)(4,1)S(1)}, u32[]{:S(2)}) copy-start(pred[32,16]{1,0:T(8,128)(4,1)S(1)} %broadcast_compare_fusion) | copy-start | bytes 1540
  57.7 4.9 copy-start.2
  66.1 6.4 %copy-start.22 = (s32[32]{0:T(128)S(1)}, s32[32]{0:T(128)}, u32[]{:S(2)}) copy-start(s32[32]{0:T(128)} %copy-done.21) | copy-start | bytes 388
  67.7 0.9 copy-start.13
  70.2 4.0 copy-start.12
  75.7 9.1 %copy-start.11 = (f32[8,32,8]{1,2,0:T(8,128)S(1)}, f32[8,32,8]{1,2,0:T(8,128)}, u32[]{:S(2)}) copy-start(f32[8,32,8]{1,2,0:T(8,128)} %get-tuple-element.270) | copy-start | bytes 24580
  78.2 9.5 %copy-start.7 = (bf16[32,16,4,128]{3,2,1,0:T(4,128)(2,1)S(1)}, bf16[32,16,4,128]{3,2,1,0:T(4,128)(2,1)}, u32[]{:S(2)}) copy-start(bf16[32,16,4,128]{3,2,1,0:T(4,128)(2,1)} %reshape_squeeze.15) | copy-start | bytes 1572868
  78.2 9.5 %copy-start.14 = (f32[32,2,4,16]{3,1,2,0:T(2,128)S(1)}, f32[32,2,4,16]{3,1,2,0:T(2,128)}, u32[]{:S(2)}) copy-start(f32[32,2,4,16]{3,1,2,0:T(2,128)} %copy-done.13) | copy-start | bytes 49156
  78.2 9.5 %copy-start.18 = (pred[32,16]{1,0:T(8,128)(4,1)S(1)}, pred[32,16]{1,0:T(8,128)(4,1)}, u32[]{:S(2)}) copy-start(pred[32,16]{1,0:T(8,128)(4,1)} %copy-done.17) | copy-start | bytes 1540
  79.5 8.9 %copy-start.3 = (f32[128,8,4]{2,1,0:T(8,128)S(1)}, f32[128,8,4]{2,1,0:T(8,128)}, u32[]{:S(2)}) copy-start(f32[128,8,4]{2,1,0:T(8,128)} %get-tuple-element.271) | copy-start | bytes 49156
  80.2 15.7 %all-to-all-start = ((f32[16,1,256]{2,1,0:T(1,128)}), f32[16,1,256]{2,1,0:T(1,128)S(1)}, u32[]{:S(2)}, u32[]{:S(2)}) async-start(f32[16,1,256]{2,1,0:T(1,128)} %reshape.383), calls=%async_computation | async-start | bytes 32768 | tf_op jit(solution)/shard_map/all_to_all | solution.py:213
  87.7 1.9 copy-start.20
  93.8 0.7 copy-start.23
  96.0 14.9 %all-to-all-start.1 = ((f32[16,1,256]{2,1,0:T(1,128)}), f32[16,1,256]{2,1,0:T(1,128)S(1)}, u32[]{:S(2)}, u32[]{:S(2)}) async-start(f32[16,1,256]{2,1,0:T(1,128)} %reshape.385), calls=%async_computation.1 | async-start | bytes 32768 | tf_op jit(solution)/shard_map/all_to_all | solution.py:220
  110.8 54.9 %all-to-all-start.2 = ((f32[16,64,4,128]{3,2,1,0:T(4,128)}), f32[16,64,4,128]{3,2,1,0:T(4,128)S(1)}, u32[]{:S(2)}, u32[]{:S(2)}) async-start(f32[16,64,4,128]{3,2,1,0:T(4,128)} %bitcast.145), calls=%async_computation.2 | async-start | bytes 4194304 | tf_op jit(solution)/shard_map/all_to_all | solution.py:227
  116.5 52.1 %copy-start.8 = (bf16[32,2,3,512]{3,1,2,0:T(2,128)(2,1)S(1)}, bf16[32,2,3,512]{3,1,2,0:T(2,128)(2,1)}, u32[]{:S(2)}) copy-start(bf16[32,2,3,512]{3,1,2,0:T(2,128)(2,1)} %param.24) | copy-start | bytes 589828
  116.5 99.8 %all-gather.11.cloned.1.call-start = ((), (), s32[]{:S(2)}) async-start(), calls=%async_computation.9 | async-start | bytes 1179648 | tf_op jit(solution)/shard_map/all_gather | solution.py:21
  118.7 50.2 %copy-start.35 = (f32[4]{0:T(128)S(1)}, f32[4]{0:T(128)}, u32[]{:S(2)}) copy-start(f32[4]{0:T(128)} %multiply_exponential_fusion) | copy-start | bytes 52
  168.6 82.1 %reduce-scatter.13.cloned.1.call-start = ((), (), s32[]{:S(2)}) async-start(), calls=%async_computation.10 | async-start | bytes 163840
  170.5 58.4 %copy-start.9 = (bf16[512,256]{1,0:T(8,128)(2,1)S(1)}, bf16[512,256]{1,0:T(8,128)(2,1)}, u32[]{:S(2)}) copy-start(bf16[512,256]{1,0:T(8,128)(2,1)} %param.31) | copy-start | bytes 786436
  217.3 12.7 %copy-start.30 = (bf16[64]{0:T(256)(128)(2,1)S(1)}, bf16[64]{0:T(256)(128)(2,1)}, u32[]{:S(2)}) copy-start(bf16[64]{0:T(256)(128)(2,1)} %param.32) | copy-start | bytes 388
  217.3 12.7 %copy-start.26 = (bf16[256]{0:T(256)(128)(2,1)S(1)}, bf16[256]{0:T(256)(128)(2,1)}, u32[]{:S(2)}) copy-start(bf16[256]{0:T(256)(128)(2,1)} %param.34) | copy-start | bytes 1540
  217.3 12.7 %copy-start.27 = (bf16[256]{0:T(256)(128)(2,1)S(1)}, bf16[256]{0:T(256)(128)(2,1)}, u32[]{:S(2)}) copy-start(bf16[256]{0:T(256)(128)(2,1)} %param.33) | copy-start | bytes 1540
  217.3 34.3 %copy-start.10 = (bf16[32,2,64]{2,1,0:T(2,128)(2,1)S(1)}, bf16[32,2,64]{2,1,0:T(2,128)(2,1)}, u32[]{:S(2)}) copy-start(bf16[32,2,64]{2,1,0:T(2,128)(2,1)} %param.23) | copy-start | bytes 24580
  228.3 109.0 %copy-start.31 = (bf16[64]{0:T(256)(128)(2,1)S(1)}, bf16[64]{0:T(256)(128)(2,1)}, u32[]{:S(2)}) copy-start(bf16[64]{0:T(256)(128)(2,1)} %param.38) | copy-start | bytes 388
  228.3 109.0 %copy-start.32 = (bf16[256]{0:T(256)(128)(2,1)S(1)}, bf16[256]{0:T(256)(128)(2,1)}, u32[]{:S(2)}) copy-start(bf16[256]{0:T(256)(128)(2,1)} %param.36) | copy-start | bytes 1540
  228.3 109.0 %copy-start.28 = (bf16[256]{0:T(256)(128)(2,1)S(1)}, bf16[256]{0:T(256)(128)(2,1)}, u32[]{:S(2)}) copy-start(bf16[256]{0:T(256)(128)(2,1)} %param.40) | copy-start | bytes 1540
  228.3 109.0 %copy-start.29 = (bf16[256]{0:T(256)(128)(2,1)S(1)}, bf16[256]{0:T(256)(128)(2,1)}, u32[]{:S(2)}) copy-start(bf16[256]{0:T(256)(128)(2,1)} %param.39) | copy-start | bytes 1540
  228.3 174.4 %copy-start.4 = (bf16[2048,256]{1,0:T(8,128)(2,1)S(1)}, bf16[2048,256]{1,0:T(8,128)(2,1)}, u32[]{:S(2)}) copy-start(bf16[2048,256]{1,0:T(8,128)(2,1)} %param.37) | copy-start | bytes 3145732
  229.9 147.1 %reduce-scatter.11.cloned.1.call-start = ((), (), s32[]{:S(2)}) async-start(), calls=%async_computation.7 | async-start | bytes 589824 | tf_op jit(solution)/shard_map/reduce_scatter | solution.py:281
  323.1 80.7 %copy-start.33 = (bf16[256]{0:T(256)(128)(2,1)S(1)}, bf16[256]{0:T(256)(128)(2,1)}, u32[]{:S(2)}) copy-start(bf16[256]{0:T(256)(128)(2,1)} %param.41) | copy-start | bytes 1540
  336.0 244.0 %copy-start.5 = (bf16[256,1536]{1,0:T(8,128)(2,1)S(1)}, bf16[256,1536]{1,0:T(8,128)(2,1)}, u32[]{:S(2)}) copy-start(bf16[256,1536]{1,0:T(8,128)(2,1)} %param.42) | copy-start | bytes 2359300
  337.2 89.4 %reduce-scatter.15.cloned.1.call-start = ((), (), s32[]{:S(2)}) async-start(), calls=%async_computation.11 | async-start | bytes 81920
  377.9 203.4 %copy-start.34 = (bf16[192]{0:T(256)(128)(2,1)S(1)}, bf16[192]{0:T(256)(128)(2,1)}, u32[]{:S(2)}) copy-start(bf16[192]{0:T(256)(128)(2,1)} %param.43) | copy-start | bytes 1156
  403.7 217.1 %reduce-scatter.17.cloned.1.call-start = ((), (), s32[]{:S(2)}) async-start(), calls=%async_computation.12 | async-start | bytes 442368
  427.5 194.8 %copy-start.15 = (bf16[64,64]{1,0:T(8,128)(2,1)}, bf16[64,64]{1,0:T(8,128)(2,1)S(1)}, u32[]{:S(2)}) copy-start(bf16[64,64]{1,0:T(8,128)(2,1)S(1)} %get-tuple-element.227) | copy-start | bytes 24580
Sparse Core Ops, SparseCore 0:
  10.2 45.5 all-gather.8
  168.7 41.4 all-gather.10
  230.0 20.6 reduce-scatter.12
  337.3 39.6 reduce-scatter.10
  403.9 22.6 reduce-scatter.14
  581.4 39.3 reduce-scatter.16
where the time goes:
time: 630 us; the launch traced here: 629 us
  blocking collectives  307 us (49%)
  waiting for transfers between devices  205 us (33%)
  local copies, waits for them, and re-layouts  40.9 us (6%)
  other arithmetic  33.2 us (5%)
  starting transfers between devices  17.7 us (3%)
  between operations  14.9 us (2%)
  matrix products  10.4 us (2%)
    psum x1, blocking collectives, shards(): lax.psum((jnp.sum(out_wide, axis=1), jnp.sum(out_wide * out_wide, axis=1)...  138 us
    unnamed x9, waiting for transfers between devices  82.4 us
    psum x1, blocking collectives, shards(): lax.psum((jnp.sum(hidden_one, axis=1), jnp.sum(hidden_one * hidden_one, a...  71.3 us
    all_to_all x1, waiting for transfers between devices, shards(): lax.all_to_all(outputs.reshape(group_count, row_total, head_count, HD), '...  45.9 us
    all_gather x2, blocking collectives, combined_all(): everything = jax.tree.map(lambda part: lax.all_gather(part, axis), shard)  45.5 us
    reduce_scatter x1, waiting for transfers between devices, shards(): lax.psum_scatter(jnp.dot(normed_a, up_weight, preferred_element_type=jnp....  39.6 us
    all_gather x1, waiting for transfers between devices, shards(): everyone = lax.all_gather(fresh_qkv[:, :, 0], 'pages', axis=0, tiled=True)  35.8 us
    all_gather x1, blocking collectives, shards(): lax.all_gather(hidden_two, 'row', axis=1, tiled=True)  24.8 us
  transfers between devices with their start and end apart: 9, of which 7 were waited for; matrix products, arithmetic and copies ran while one was open for 5% of the time, Pallas kernels for 0%

commit v1 on v0

v1 whole, which is shorter than its diff:
```python
import math

import jax
import jax.numpy as jnp
from jax import lax
from jax.experimental import pallas as pl
from jax.experimental.pallas import tpu as pltpu
from jax.sharding import PartitionSpec as P

D = 2048
H = 16
HD = 128
PAGE = 128
MAXPAGES = 8
CONT = 16

GROUPS = 16
NROW = 8
NCOL = 4
ROWS = 64
HEADS = 4
WIDE = HEADS * HD
PACK = WIDE + 128
BLOCK = D // NROW
TOK = 16
TAILS = 32

masked_score = -1e30
norm_eps = 1e-05
f32 = jnp.float32
bf16 = jnp.bfloat16


def dot(a, b):
    return jnp.dot(a, b, preferred_element_type=f32)


def dot_t(a, b):
    return lax.dot_general(a, b, (((1,), (1,)), ((), ())), preferred_element_type=f32)


def iota(shape, dim):
    return lax.broadcasted_iota(jnp.int32, shape, dim)


def one_hot(mask):
    return jnp.where(mask, 1.0, 0.0).astype(bf16)


def rounded(x):
    return x.astype(bf16).astype(f32)


def slope_of(head):
    return jnp.exp2(jnp.full((ROWS, 1), -8.0 / H, f32) * (head + 1).astype(f32))


def put_stats(stats, head, m, l):
    lane = iota((ROWS, 128), 1)
    hi = rounded(l)
    stats = jnp.where(lane == head * 4, m, stats)
    stats = jnp.where(lane == head * 4 + 1, hi, stats)
    return jnp.where(lane == head * 4 + 2, l - hi, stats)


def get_stats(stats, head):
    at = head * 4
    return stats[:, at : at + 1], stats[:, at + 1 : at + 2] + stats[:, at + 2 : at + 3]


def send_kernel(tail_item, query, pages, out):
    group = lax.axis_index("pages")
    row = iota((ROWS, ROWS), 0)
    source = jnp.zeros((ROWS, ROWS), jnp.int32)
    for j in range(TAILS):
        item = tail_item[(j // 2) * TAILS + group * 2 + j % 2] - group * TAILS
        source = jnp.where((row >> 1) == j, item * 2, source)
    pick = one_hot(iota((ROWS, ROWS), 1) == source + (row & 1))
    picked = dot(pick, query[...])
    for h in range(GROUPS):
        out[h, 0:TOK] = pages[h, 0]
        out[h, TOK : 2 * TOK] = pages[h, 1]
        out[h, 2 * TOK : 2 * TOK + 4] = picked[4 * h : 4 * h + 4].astype(bf16)


def tail_kernel(tail_item, tail_length, recv, tails, out, wide):
    holder = lax.axis_index("pages")
    token_at = lax.axis_index("row") * TOK
    first_head = lax.axis_index("col") * HEADS
    for g in range(GROUPS):
        wide[4 * g : 4 * g + 4, 0:WIDE] = recv[g, 2 * TOK : 2 * TOK + 4].astype(f32)
    row = iota((ROWS, 1), 0)
    lens = jnp.zeros((ROWS, 1), jnp.int32)
    for s in range(TAILS):
        lens = jnp.where((row >> 1) == s, tail_length[tail_item[holder * TAILS + s]], lens)
    keys = TAILS * TOK
    key = iota((ROWS, keys), 1)
    token = (key & (TOK - 1)) + token_at
    usable = ((key >> 4) == (row >> 1)) & (token < lens)
    offset = (token - lens - (row & 1)).astype(f32)
    stats = jnp.zeros((ROWS, 128), f32)
    for head in range(HEADS):
        at = slice(head * HD, (head + 1) * HD)
        k = tails[:, 0, :, at].reshape(keys, HD)
        v = tails[:, 1, :, at].reshape(keys, HD)
        scores = dot_t(wide[:, at].astype(bf16), k) * (1.0 / math.sqrt(HD))
        scores = scores + slope_of(first_head + head) * offset
        scores = jnp.where(usable, scores, masked_score)
        m = rounded(jnp.max(scores, axis=1, keepdims=True))
        weights = jnp.where(usable, jnp.exp(scores - m), 0.0)
        stats = put_stats(stats, head, m, jnp.sum(weights, axis=1, keepdims=True))
        wide[:, at] = dot(weights.astype(bf16), v)
    wide[:, WIDE:PACK] = stats
    for g in range(GROUPS):
        out[g] = wide[4 * g : 4 * g + 4].astype(bf16)


def prefix_kernel(prefix_item, prefix_length, tail_length, fresh, recv, out):
    group = lax.axis_index("pages")
    row_index = lax.axis_index("row")
    first_head = lax.axis_index("col") * HEADS
    row = iota((ROWS, 1), 0)
    tail_lens = jnp.zeros((ROWS, 1), jnp.int32)
    for j in range(TAILS):
        tail_lens = jnp.where((row >> 1) == j, tail_length[group * TAILS + j], tail_lens)
    row_prompt = row >> 5
    prompt_lens = jnp.where(
        row_prompt == 0, prefix_length[group * 2], prefix_length[group * 2 + 1]
    )
    query_pos = prompt_lens + tail_lens + (row & 1)
    keys = GROUPS * TOK
    lane = iota((1, keys), 1)
    key_pos = (lane & (TOK - 1)) + row_index * TOK
    key_prompt = jnp.zeros((1, keys), jnp.int32)
    for h in range(GROUPS):
        item = prefix_item[h * GROUPS + group]
        here = (lane >> 4) == h
        key_pos = key_pos + jnp.where(here, (item & (MAXPAGES - 1)) * PAGE, 0)
        key_prompt = jnp.where(here, (item >> 3) - group * 2, key_prompt)
    usable = (key_prompt == row_prompt) & (key_pos < prompt_lens)
    offset = (key_pos - query_pos).astype(f32)
    col = iota((ROWS, ROWS), 1)
    new_usable = ((col >> 1) == (row >> 1)) & ((col & 1) <= (row & 1)) & (row_index == 0)
    new_offset = ((col & 1) - (row & 1)).astype(f32)
    stats = jnp.zeros((ROWS, 128), f32)
    for head in range(HEADS):
        at = slice(head * HD, (head + 1) * HD)
        q = fresh[:, head * HD : (head + 1) * HD]
        new_k = fresh[:, WIDE + head * HD : WIDE + (head + 1) * HD]
        new_v = fresh[:, 2 * WIDE + head * HD : 2 * WIDE + (head + 1) * HD]
        k = recv[:, 0:TOK, at].reshape(keys, HD)
        v = recv[:, TOK : 2 * TOK, at].reshape(keys, HD)
        slope = slope_of(first_head + head)
        scores = dot_t(q, k) * (1.0 / math.sqrt(HD)) + slope * offset
        scores = jnp.where(usable, scores, masked_score)
        new_scores = dot_t(q, new_k) * (1.0 / math.sqrt(HD)) + slope * new_offset
        new_scores = jnp.where(new_usable, new_scores, masked_score)
        m = rounded(
            jnp.maximum(
                jnp.max(scores, axis=1, keepdims=True),
                jnp.max(new_scores, axis=1, keepdims=True),
            )
        )
        weights = jnp.where(usable, jnp.exp(scores - m), 0.0)
        new_weights = jnp.where(new_usable, jnp.exp(new_scores - m), 0.0)
        total = jnp.sum(weights, axis=1, keepdims=True) + jnp.sum(
            new_weights, axis=1, keepdims=True
        )
        stats = put_stats(stats, head, m, total)
        out[:, at] = dot(weights.astype(bf16), v) + dot(new_weights.astype(bf16), new_v)
    out[:, WIDE:PACK] = stats


def join_kernel(tail_item, prefix, recv, out, wide):
    group = lax.axis_index("pages")
    for h in range(GROUPS):
        wide[4 * h : 4 * h + 4] = recv[h].astype(f32)
    lane = iota((1, ROWS), 1)
    target = lane & 1
    for j in range(TAILS):
        item = tail_item[(j // 2) * TAILS + group * 2 + j % 2] - group * TAILS
        target = target + jnp.where((lane >> 1) == j, item * 2, 0)
    order = one_hot(iota((ROWS, ROWS), 0) == target)
    tails = dot(order, wide[...].astype(bf16))
    tail_stats = tails[:, WIDE:PACK]
    prefix_stats = prefix[:, WIDE:PACK]
    stats = jnp.zeros((ROWS, 128), f32)
    for head in range(HEADS):
        at = slice(head * HD, (head + 1) * HD)
        left_m, left_l = get_stats(prefix_stats, head)
        right_m, right_l = get_stats(tail_stats, head)
        m = jnp.maximum(left_m, right_m)
        left = jnp.exp(left_m - m)
        right = jnp.exp(right_m - m)
        stats = put_stats(stats, head, m, left * left_l + right * right_l)
        joined = (left * prefix[:, at] + right * tails[:, at]).astype(bf16)
        for n in range(NROW):
            out[n, :, at] = joined
    stats = stats.astype(bf16)
    for n in range(NROW):
        out[n, :, WIDE:PACK] = stats


def own_columns():
    share = BLOCK // NCOL
    first = lax.axis_index("col") * share
    return one_hot(iota((share, BLOCK), 1) == iota((share, BLOCK), 0) + first)


def out_kernel(recv, weight, residual, bias, out, wide):
    stats = [recv[n, :, WIDE:PACK].astype(f32) for n in range(NROW)]
    for head in range(HEADS):
        at = slice(head * HD, (head + 1) * HD)
        parts = [get_stats(s, head) for s in stats]
        m = parts[0][0]
        for part in parts[1:]:
            m = jnp.maximum(m, part[0])
        total = jnp.zeros((ROWS, 1), f32)
        attended = jnp.zeros((ROWS, HD), f32)
        for n in range(NROW):
            scale = jnp.exp(parts[n][0] - m)
            total = total + scale * parts[n][1]
            attended = attended + scale * recv[n, :, at].astype(f32)
        wide[:, at] = (attended / total).astype(bf16)
    place = own_columns()
    share = BLOCK // NCOL
    partial = (
        dot(wide[...], weight[...])
        + dot(residual[...], place)
        + dot(jnp.broadcast_to(bias[...], (8, share)), place)[0:1]
    ).astype(bf16)
    for n in range(NCOL):
        out[n] = partial


def split(x):
    hi = rounded(x)
    return hi, x - hi


def centred(values, gain):
    mean = jnp.mean(values, axis=1, keepdims=True)
    away = values - mean
    return mean, jnp.sum(away * away, axis=1, keepdims=True), (away * gain).astype(bf16)


def as_rows(columns):
    lane = iota((ROWS, 8), 1)
    table = jnp.zeros((ROWS, 8), f32)
    for at, column in columns:
        table = jnp.where(lane == at, column, table)
    eye = one_hot(iota((ROWS, ROWS), 0) == iota((ROWS, ROWS), 1))
    return lax.dot_general(
        table.astype(bf16), eye, (((0,), (0,)), ((), ())), preferred_element_type=f32
    )


def gain_rows(gain, shift):
    row = iota((16, BLOCK), 0)
    gain = jnp.broadcast_to(gain.astype(f32), (16, BLOCK))
    shift = jnp.broadcast_to(shift.astype(f32), (16, BLOCK))
    return jnp.where(row == 0, gain, jnp.where(row == 1, shift, 0.0)).astype(bf16)


def up_kernel(recv, gain, shift, weight, hidden, out):
    values = recv[0].astype(f32)
    for n in range(1, NCOL):
        values = values + recv[n].astype(f32)
    hidden[...] = values
    mean, spread, scaled = centred(values, gain[...].astype(f32))
    columns = list(zip((4, 5, 6, 7), split(mean) + split(spread)))
    rows = as_rows(columns)
    extra = gain_rows(gain[...], shift[...])
    edge = iota((8, BLOCK), 0)
    for n in range(NROW):
        w = weight[:, n * BLOCK : (n + 1) * BLOCK]
        out[n, 0:ROWS] = dot(scaled, w).astype(bf16)
        both = dot(extra, w)
        tail = jnp.zeros((8, BLOCK), f32)
        for at, row in enumerate(split(both[0:1]) + split(both[1:2])):
            tail = jnp.where(edge == at, row, tail)
        wide = jnp.concatenate([rows, jnp.zeros((8, BLOCK - ROWS), f32)], axis=1)
        out[n, ROWS : ROWS + 8] = jnp.where(edge < 4, tail, wide).astype(bf16)


def as_columns(recv):
    rows = jnp.concatenate([recv[n, ROWS : ROWS + 8, 0:ROWS].astype(f32) for n in range(NROW)], 0)
    eye = one_hot(iota((ROWS, ROWS), 0) == iota((ROWS, ROWS), 1))
    return dot_t(eye, rows.astype(bf16))


def scale_of(means, spreads):
    mean = sum(means) / NROW
    spread = sum(spreads)
    for part in means:
        spread = spread + BLOCK * (part - mean) * (part - mean)
    return mean, lax.rsqrt(spread / D + norm_eps)


def projected(recv, width, bias, gain_at, shift_at, mean_at, spread_at):
    columns = as_columns(recv)

    def column(n, at):
        return columns[:, 8 * n + at : 8 * n + at + 1] + columns[:, 8 * n + at + 1 : 8 * n + at + 2]

    means = [column(n, mean_at) for n in range(NROW)]
    mean, scale = scale_of(means, [column(n, spread_at) for n in range(NROW)])
    total = jnp.zeros((ROWS, width), f32)
    shifted = bias.astype(f32)
    for n in range(NROW):
        edge = recv[n, ROWS : ROWS + 8].astype(f32)
        gained = sum(edge[at : at + 1] for at in gain_at)
        shifted = shifted + sum(edge[at : at + 1] for at in shift_at)
        total = total + recv[n, 0:ROWS].astype(f32) + (means[n] - mean) * gained
    return total * scale + shifted


def hidden_kernel(recv, bias, out):
    v = projected(recv, BLOCK, bias[...], (0, 1), (2, 3), 4, 6)
    v = 0.5 * v * (1.0 + jnp.tanh(math.sqrt(2.0 / math.pi) * (v + 0.044715 * (v * v * v))))
    v = v.astype(bf16)
    for n in range(NROW):
        out[n] = v


def down_kernel(recv, weight, bias, out):
    share = BLOCK // NCOL
    total = dot(jnp.broadcast_to(bias[...], (8, share)), own_columns())[0:1]
    for n in range(NROW):
        total = total + dot(recv[n], weight[n * BLOCK : (n + 1) * BLOCK])
    total = total.astype(bf16)
    for n in range(NCOL):
        out[n] = total


def next_kernel(recv, hidden, gain, shift, score, weight, layer_out, out):
    values = hidden[...]
    for n in range(NCOL):
        values = values + recv[n].astype(f32)
    low = values.astype(bf16)
    values = low.astype(f32)
    layer_out[...] = dot_t(low, own_columns()).astype(bf16)
    mean, spread, scaled = centred(values, gain[...].astype(f32))
    scores = jnp.sum(values * score[...].astype(f32), axis=1, keepdims=True)
    columns = list(zip((2, 3, 4, 5, 6, 7), split(mean) + split(spread) + split(scores)))
    rows = as_rows(columns)
    extra = gain_rows(gain[...], shift[...])
    width = out.shape[2]
    edge = iota((8, width), 0)
    for n in range(NROW):
        w = weight[:, n * width : (n + 1) * width]
        out[n, 0:ROWS] = dot(scaled, w).astype(bf16)
        both = dot(extra, w)
        wide = jnp.concatenate([rows, jnp.zeros((8, width - ROWS), f32)], axis=1)
        tail = jnp.where(edge == 0, both[0:1], jnp.where(edge == 1, both[1:2], wide))
        out[n, ROWS : ROWS + 8] = tail.astype(bf16)


def final_kernel(recv, bias, projected_next, score_out):
    width = projected_next.shape[1]
    projected_next[...] = projected(recv, width, bias[...], (0,), (1,), 2, 4).astype(bf16)
    total = jnp.zeros((1, ROWS), f32)
    for n in range(NROW):
        edge = recv[n, ROWS : ROWS + 8, 0:ROWS].astype(f32)
        total = total + edge[6:7] + edge[7:8]
    score_out[...] = total


def call(kernel, out, scalars, arrays, scratch=(), flops=0):
    many = isinstance(out, list)
    outs = out if many else [out]
    moved = sum(a.size * a.dtype.itemsize for a in arrays)
    moved += sum(math.prod(s) * jnp.dtype(t).itemsize for s, t in outs)
    shapes = [jax.ShapeDtypeStruct(s, t) for s, t in outs]
    vmem = pl.BlockSpec(memory_space=pltpu.VMEM)
    return pl.pallas_call(
        kernel,
        out_shape=shapes if many else shapes[0],
        in_specs=[pl.BlockSpec(memory_space=pltpu.SMEM)] * len(scalars) + [vmem] * len(arrays),
        out_specs=[vmem] * len(outs) if many else vmem,
        scratch_shapes=[pltpu.VMEM(s, t) for s, t in scratch],
        cost_estimate=pl.CostEstimate(flops=flops, bytes_accessed=moved, transcendentals=0),
        compiler_params=pltpu.CompilerParams(vmem_limit_bytes=24 * 1024 * 1024),
        name=kernel.__name__,
    )(*scalars, *arrays)


def exchange(x, axis):
    return lax.all_to_all(x, axis, split_axis=0, concat_axis=0, tiled=True)


def shards(
    residual,
    fresh_qkv,
    prefix_pages,
    tail_pages,
    prefix_item,
    tail_item,
    prefix_length,
    tail_length,
    out_weight,
    out_bias,
    mlp_gain,
    mlp_shift,
    up_weight,
    up_bias,
    down_weight,
    down_bias,
    next_gain,
    next_shift,
    score_weight,
    qkv_weight,
    qkv_bias,
):
    cont_local = residual.shape[0]
    share = residual.shape[2]
    width = qkv_bias.shape[0]

    def line(x):
        return x.reshape(1, x.shape[0])

    fresh = fresh_qkv.reshape(ROWS, 3 * WIDE)
    query = fresh_qkv[:, :, 0].reshape(ROWS, WIDE)
    sent = call(send_kernel, ((GROUPS, 2 * TOK + 4, WIDE), bf16), [tail_item], [query, prefix_pages])
    arrived = exchange(sent, "pages")
    tails = call(
        tail_kernel,
        ((GROUPS, 4, PACK), bf16),
        [tail_item, tail_length],
        [arrived, tail_pages],
        [((ROWS, PACK), f32)],
    )
    tails = exchange(tails, "pages")
    prefix = call(
        prefix_kernel,
        ((ROWS, PACK), f32),
        [prefix_item, prefix_length, tail_length],
        [fresh, arrived],
    )
    joined = call(
        join_kernel,
        ((NROW, ROWS, PACK), bf16),
        [tail_item],
        [prefix, tails],
        [((ROWS, PACK), f32)],
    )
    joined = exchange(joined, "row")
    partial = call(
        out_kernel,
        ((NCOL, ROWS, BLOCK), bf16),
        [],
        [joined, out_weight, residual.reshape(ROWS, share), line(out_bias)],
        [((ROWS, WIDE), bf16)],
    )
    partial = exchange(partial, "col")
    hidden_one, partial = call(
        up_kernel,
        [((ROWS, BLOCK), f32), ((NROW, ROWS + 8, BLOCK), bf16)],
        [],
        [partial, line(mlp_gain), line(mlp_shift), up_weight],
    )
    partial = exchange(partial, "row")
    hidden_two = call(hidden_kernel, ((NROW, ROWS, BLOCK), bf16), [], [partial, line(up_bias)])
    hidden_two = exchange(hidden_two, "row")
    partial = call(
        down_kernel, ((NCOL, ROWS, BLOCK), bf16), [], [hidden_two, down_weight, line(down_bias)]
    )
    partial = exchange(partial, "col")
    layer_out, partial = call(
        next_kernel,
        [((ROWS, share), bf16), ((NROW, ROWS + 8, width), bf16)],
        [],
        [partial, hidden_one, line(next_gain), line(next_shift), line(score_weight), qkv_weight],
    )
    partial = exchange(partial, "row")
    projected_next, score_sum = call(
        final_kernel, [((ROWS, width), bf16), ((1, ROWS), f32)], [], [partial, line(qkv_bias)]
    )
    return (
        layer_out.reshape(cont_local, 2, share),
        score_sum.reshape(cont_local, 2),
        projected_next.reshape(cont_local, 2, width),
    )


def solution(mesh):
    in_specs = (
        P("pages", None, ("row", "col")),
        P("pages", None, None, "col"),
        P("pages", None, "row", "col"),
        P("pages", None, "row", "col"),
        P(),
        P(),
        P(),
        P(),
        P("col", "row"),
        P(("row", "col")),
        P("row"),
        P("row"),
        P("row", "col"),
        P(("col", "row")),
        P("col", "row"),
        P(("row", "col")),
        P("row"),
        P("row"),
        P("row"),
        P("row", "col"),
        P(("col", "row")),
    )
    out_specs = (
        P("pages", None, ("row", "col")),
        P("pages", None),
        P("pages", None, ("col", "row")),
    )
    return jax.shard_map(shards, mesh=mesh, in_specs=in_specs, out_specs=out_specs, check_vma=False)
```

time: 630 us -> 150 us (0.24)
  blocking collectives: 307 us -> 71.1 us
  waiting for transfers between devices: 205 us -> 34.7 us
  other arithmetic: 33.2 us -> 0.66 us
  local copies, waits for them, and re-layouts: 40.9 us -> 8.59 us
  between operations: 14.9 us -> 0.81 us
  Pallas kernels: 0 us -> 12.4 us
  matrix products: 10.4 us -> 0 us
    psum x2 -> x0, blocking collectives: 209 us -> none  [the longest x1 138 us: shards(): lax.psum((jnp.sum(out_wide, axis=1), jnp.sum(out_wide * out_wide, axis=1)...]
    all_gather x5 -> x0, blocking collectives: 97.3 us -> none  [the longest x2 45.5 us: combined_all(): everything = jax.tree.map(lambda part: lax.all_gather(part, axis), shard)]
    unnamed x9 -> x0, waiting for transfers between devices: 82.4 us -> none
    all_to_all x0 -> x3, blocking collectives: none -> 71.1 us  [exchange(): return lax.all_to_all(x, axis, split_axis=0, concat_axis=0, tiled=True)]
    reduce_scatter x1 -> x0, waiting for transfers between devices: 39.6 us -> none  [shards(): lax.psum_scatter(jnp.dot(normed_a, up_weight, preferred_element_type=jnp....]
    all_gather x2 -> x0, waiting for transfers between devices: 35.8 us -> none  [the longest x1 35.8 us: shards(): everyone = lax.all_gather(fresh_qkv[:, :, 0], 'pages', axis=0, tiled=True)]
    add x21 -> x0, other arithmetic: 18.3 us -> none  [the longest x8 15.3 us: merge_pair(): left_scale[..., None] * left_out + right_scale[..., None] * right_out]
    all_to_all x3 -> x5, waiting for transfers between devices: 47.5 us -> 34.7 us  [exchange(): return lax.all_to_all(x, axis, split_axis=0, concat_axis=0, tiled=True)]
  transfers between devices with their start and end apart: 9 -> 5, of which waited for: 7 -> 5; matrix products, arithmetic and copies ran while one was open for 5% -> 0% of each run, Pallas kernels for 0% -> 1%
where the time goes in v1:
time: 150 us; the launch traced here: 149 us
  blocking collectives  71.1 us (47%)
  waiting for transfers between devices  34.7 us (23%)
  starting transfers between devices  20.4 us (14%)
  Pallas kernels  12.4 us (8%)
  local copies, waits for them, and re-layouts  8.59 us (6%)
    all_to_all x3, blocking collectives, exchange(): return lax.all_to_all(x, axis, split_axis=0, concat_axis=0, tiled=True)  71.1 us
    all_to_all x5, waiting for transfers between devices, exchange(): return lax.all_to_all(x, axis, split_axis=0, concat_axis=0, tiled=True)  34.7 us
    all_to_all x5, starting transfers between devices, exchange(): return lax.all_to_all(x, axis, split_axis=0, concat_axis=0, tiled=True)  20.4 us
    pallas_call x10, Pallas kernels, call(): pl.pallas_call(kernel, out_shape=shapes if many else shapes[0], in_specs=...  12.4 us
    unnamed x45, local copies, waits for them, and re-layouts  6.45 us
  transfers between devices with their start and end apart: 5, of which 5 were waited for; matrix products, arithmetic and copies ran while one was open for 0% of the time, Pallas kernels for 1%

profile of v1, /device:TPU:2, one launch (start us, length us, event | category | flops | bytes accessed | tf_op | source)
XLA Modules:
  0.0 148.7 jit_solution(7907779267641143775)
XLA Ops:
  0.6 0.0 slice-start
  0.6 0.8 slice-done
  1.5 0.6 copy-done.6
  2.2 1.0 copy-done.4
  3.2 0.8 send_kernel.1
  4.0 27.1 %all_to_all.40.recv = bf16[16,36,512]{2,1,0:T(8,128)(2,1)S(1)} all-to-all(bf16[16,36,512]{2,1,0:T(8,128)(2,1)S(1)} %send_kernel.1), channel_id=1, replica_groups=mesh['pages'=16,'row'=8,'col'=4] {'pages'}, dimensions={0} | all-to-all | bytes 1179648 | tf_op jit(solution)/shard_map/all_to_all | solution.py:389
  31.1 0.0 copy-done
  31.1 2.4 %tail_kernel.1 = bf16[16,4,640]{2,1,0:T(4,128)(2,1)} custom-call(s32[512]{0:T(512)S(1)} %copy-done.6, s32[512]{0:T(512)S(1)} %copy-done.8, bf16[16,36,512]{2,1,0:T(8,128)(2,1)S(1)} %all_to_all.40.recv, bf16[32,2,16,512]{3,2,1,0:T(8,128)(2,1)S(1)} %copy-done), custom_call_target="tpu_custom_call" | custom-call | bytes 1720320 | tf_op jit(solution)/shard_map/tail_kernel/pallas_call | solution.py:376
  33.5 3.5 %all-to-all-start.1 = ((bf16[16,4,640]{2,1,0:T(4,128)(2,1)}), bf16[16,4,640]{2,1,0:T(4,128)(2,1)S(1)}, u32[]{:S(2)}, u32[]{:S(2)}) async-start(bf16[16,4,640]{2,1,0:T(4,128)(2,1)} %tail_kernel.1), calls=%async_computation.1 | async-start | bytes 163840 | tf_op jit(solution)/shard_map/all_to_all | solution.py:389
  37.0 0.1 copy.26
  37.2 0.0 copy-start.9
  37.2 0.0 copy-start.10
  37.2 0.7 copy-done.9
  37.8 1.8 %prefix_kernel.1.prefix = f32[64,640]{1,0:T(8,128)S(1)} custom-call(s32[256]{0:T(256)S(1)} %copy-done.9, s32[32]{0:T(128)S(1)} %copy-done.10, s32[512]{0:T(512)S(1)} %copy-done.8, bf16[64,1536]{1,0:T(8,128)(2,1)S(1)} %bitcast.9, bf16[16,36,512]{2,1,0:T(8,128)(2,1)S(1)} %all_to_all.40.recv), custom_call_target="tpu_custom_call" | custom-call | bytes 950272 | tf_op jit(solution)/shard_map/prefix_kernel/pallas_call | solution.py:376
  39.6 5.4 %all-to-all-done.1.recv = bf16[16,4,640]{2,1,0:T(4,128)(2,1)S(1)} async-done(((bf16[16,4,640]{2,1,0:T(4,128)(2,1)}), bf16[16,4,640]{2,1,0:T(4,128)(2,1)S(1)}, u32[]{:S(2)}, u32[]{:S(2)}) %all-to-all-start.1) | async-done | bytes 81952 | tf_op jit(solution)/shard_map/all_to_all | solution.py:389
  45.0 1.1 join_kernel.1
  46.1 0.0 copy-start.5
  46.1 0.0 copy-start.1
  46.1 31.2 %all_to_all.41.recv = bf16[8,64,640]{2,1,0:T(8,128)(2,1)S(1)} all-to-all(bf16[8,64,640]{2,1,0:T(8,128)(2,1)S(1)} %join_kernel.1), channel_id=1, replica_groups=mesh['pages'=16,'row'=8,'col'=4] {'row'}, dimensions={0} | all-to-all | bytes 1310720 | tf_op jit(solution)/shard_map/all_to_all | solution.py:389
  77.3 0.0 copy-done.7
  77.3 0.6 copy-done.11
  77.9 1.4 out_kernel.1
  79.3 5.0 %all-to-all-start.3 = ((bf16[4,64,256]{2,1,0:T(8,128)(2,1)}), bf16[4,64,256]{2,1,0:T(8,128)(2,1)S(1)}, u32[]{:S(2)}, u32[]{:S(2)}) async-start(bf16[4,64,256]{2,1,0:T(8,128)(2,1)} %out_kernel.1), calls=%async_computation.3 | async-start | bytes 262144 | tf_op jit(solution)/shard_map/all_to_all | solution.py:389
  84.3 0.6 copy-done.15
  84.9 3.9 %all-to-all-done.3.recv = bf16[4,64,256]{2,1,0:T(8,128)(2,1)S(1)} async-done(((bf16[4,64,256]{2,1,0:T(8,128)(2,1)}), bf16[4,64,256]{2,1,0:T(8,128)(2,1)S(1)}, u32[]{:S(2)}, u32[]{:S(2)}) %all-to-all-start.3) | async-done | bytes 131104 | tf_op jit(solution)/shard_map/all_to_all | solution.py:389
  88.8 0.0 copy-done.1
  88.8 1.4 up_kernel.1
  90.2 3.6 %all-to-all-start.4 = ((bf16[8,72,256]{2,1,0:T(8,128)(2,1)}), bf16[8,72,256]{2,1,0:T(8,128)(2,1)S(1)}, u32[]{:S(2)}, u32[]{:S(2)}) async-start(bf16[8,72,256]{2,1,0:T(8,128)(2,1)} %get-tuple-element.9), calls=%async_computation.4 | async-start | bytes 589824 | tf_op jit(solution)/shard_map/all_to_all | solution.py:389
  93.7 0.0 copy-done.16
  93.7 11.5 %all-to-all-done.4.recv = bf16[8,72,256]{2,1,0:T(8,128)(2,1)S(1)} async-done(((bf16[8,72,256]{2,1,0:T(8,128)(2,1)}), bf16[8,72,256]{2,1,0:T(8,128)(2,1)S(1)}, u32[]{:S(2)}, u32[]{:S(2)}) %all-to-all-start.4) | async-done | bytes 294944 | tf_op jit(solution)/shard_map/all_to_all | solution.py:389
  105.3 0.7 hidden_kernel.1
  105.9 12.9 %all_to_all.42.recv = bf16[8,64,256]{2,1,0:T(8,128)(2,1)S(1)} all-to-all(bf16[8,64,256]{2,1,0:T(8,128)(2,1)S(1)} %hidden_kernel.1), channel_id=1, replica_groups=mesh['pages'=16,'row'=8,'col'=4] {'row'}, dimensions={0} | all-to-all | bytes 524288 | tf_op jit(solution)/shard_map/all_to_all | solution.py:389
  118.8 0.7 copy-done.12
  119.5 0.9 down_kernel.1
  120.4 4.9 %all-to-all-start.6 = ((bf16[4,64,256]{2,1,0:T(8,128)(2,1)}), bf16[4,64,256]{2,1,0:T(8,128)(2,1)S(1)}, u32[]{:S(2)}, u32[]{:S(2)}) async-start(bf16[4,64,256]{2,1,0:T(8,128)(2,1)} %down_kernel.1), calls=%async_computation.6 | async-start | bytes 262144 | tf_op jit(solution)/shard_map/all_to_all | solution.py:389
  125.3 0.0 copy-done.17
  125.3 0.6 copy-done.18
  126.0 0.6 copy-done.19
  126.6 3.2 %all-to-all-done.6.recv = bf16[4,64,256]{2,1,0:T(8,128)(2,1)S(1)} async-done(((bf16[4,64,256]{2,1,0:T(8,128)(2,1)}), bf16[4,64,256]{2,1,0:T(8,128)(2,1)S(1)}, u32[]{:S(2)}, u32[]{:S(2)}) %all-to-all-start.6) | async-done | bytes 131104 | tf_op jit(solution)/shard_map/all_to_all | solution.py:389
  129.8 1.4 next_kernel.1
  131.2 3.6 %all-to-all-start.7 = ((bf16[8,72,192]{2,1,0:T(8,128)(2,1)}), bf16[8,72,192]{2,1,0:T(8,128)(2,1)S(1)}, u32[]{:S(2)}, u32[]{:S(2)}) async-start(bf16[8,72,192]{2,1,0:T(8,128)(2,1)} %get-tuple-element.12), calls=%async_computation.7 | async-start | bytes 589824 | tf_op jit(solution)/shard_map/all_to_all | solution.py:389
  134.8 10.7 %all-to-all-done.7.recv = bf16[8,72,192]{2,1,0:T(8,128)(2,1)S(1)} async-done(((bf16[8,72,192]{2,1,0:T(8,128)(2,1)}), bf16[8,72,192]{2,1,0:T(8,128)(2,1)S(1)}, u32[]{:S(2)}, u32[]{:S(2)}) %all-to-all-start.7) | async-done | bytes 221216 | tf_op jit(solution)/shard_map/all_to_all | solution.py:389
  145.5 0.6 final_kernel.1
  146.1 0.6 reshape.61
  146.8 0.5 broadcast.3
  147.3 0.7 reduce.3
  147.9 0.1 reshape.60
  148.1 0.6 copy.27
  (34 shorter events, 0.2 us)
Async XLA Ops:
  0.6 0.8 slice-start
  1.5 0.7 copy-start.6
  2.2 1.0 copy-start.4
  3.2 27.9 %copy-start = (bf16[32,2,16,512]{3,2,1,0:T(8,128)(2,1)S(1)}, bf16[32,2,16,512]{3,2,1,0:T(8,128)(2,1)}, u32[]{:S(2)}) copy-start(bf16[32,2,16,512]{3,2,1,0:T(8,128)(2,1)} %tails.1) | copy-start | bytes 3145732
  4.0 27.1 %copy-start.8 = (s32[512]{0:T(512)S(1)}, s32[512]{0:T(512)}, u32[]{:S(2)}) copy-start(s32[512]{0:T(512)} %tail_length.3) | copy-start | bytes 6148
  31.1 5.9 %copy-start.13 = (bf16[32,2,3,512]{3,1,2,0:T(2,128)(2,1)S(1)}, bf16[32,2,3,512]{3,1,2,0:T(2,128)(2,1)}, u32[]{:S(2)}) copy-start(bf16[32,2,3,512]{3,1,2,0:T(2,128)(2,1)} %param.22) | copy-start | bytes 589828
  33.5 11.5 %all-to-all-start.1 = ((bf16[16,4,640]{2,1,0:T(4,128)(2,1)}), bf16[16,4,640]{2,1,0:T(4,128)(2,1)S(1)}, u32[]{:S(2)}, u32[]{:S(2)}) async-start(bf16[16,4,640]{2,1,0:T(4,128)(2,1)} %tail_kernel.1), calls=%async_computation.1 | async-start | bytes 163840 | tf_op jit(solution)/shard_map/all_to_all | solution.py:389
  37.2 0.7 copy-start.9
  37.2 0.7 copy-start.10
  45.0 32.3 %copy-start.7 = (bf16[32,2,64]{2,1,0:T(2,128)(2,1)S(1)}, bf16[32,2,64]{2,1,0:T(2,128)(2,1)}, u32[]{:S(2)}) copy-start(bf16[32,2,64]{2,1,0:T(2,128)(2,1)} %param.21) | copy-start | bytes 24580
  46.1 31.2 %copy-start.5 = (bf16[512,256]{1,0:T(8,128)(2,1)S(1)}, bf16[512,256]{1,0:T(8,128)(2,1)}, u32[]{:S(2)}) copy-start(bf16[512,256]{1,0:T(8,128)(2,1)} %weight.4) | copy-start | bytes 786436
  46.1 42.7 %copy-start.1 = (bf16[256,2048]{1,0:T(8,128)(2,1)S(1)}, bf16[256,2048]{1,0:T(8,128)(2,1)}, u32[]{:S(2)}) copy-start(bf16[256,2048]{1,0:T(8,128)(2,1)} %weight.5) | copy-start | bytes 3145732
  77.3 0.7 copy-start.11
  79.3 5.0 %copy-start.14 = (bf16[256]{0:T(256)(128)(2,1)S(1)}, bf16[256]{0:T(256)(128)(2,1)}, u32[]{:S(2)}) copy-start(bf16[256]{0:T(256)(128)(2,1)} %param.31) | copy-start | bytes 1540
  79.3 9.5 %all-to-all-start.3 = ((bf16[4,64,256]{2,1,0:T(8,128)(2,1)}), bf16[4,64,256]{2,1,0:T(8,128)(2,1)S(1)}, u32[]{:S(2)}, u32[]{:S(2)}) async-start(bf16[4,64,256]{2,1,0:T(8,128)(2,1)} %out_kernel.1), calls=%async_computation.3 | async-start | bytes 262144 | tf_op jit(solution)/shard_map/all_to_all | solution.py:389
  84.3 0.7 copy-start.15
  88.8 4.9 %copy-start.16 = (bf16[256]{0:T(256)(128)(2,1)S(1)}, bf16[256]{0:T(256)(128)(2,1)}, u32[]{:S(2)}) copy-start(bf16[256]{0:T(256)(128)(2,1)} %param.34) | copy-start | bytes 1540
  90.2 28.7 %copy-start.2 = (bf16[2048,256]{1,0:T(8,128)(2,1)S(1)}, bf16[2048,256]{1,0:T(8,128)(2,1)}, u32[]{:S(2)}) copy-start(bf16[2048,256]{1,0:T(8,128)(2,1)} %weight.6) | copy-start | bytes 3145732
  90.2 15.1 %all-to-all-start.4 = ((bf16[8,72,256]{2,1,0:T(8,128)(2,1)}), bf16[8,72,256]{2,1,0:T(8,128)(2,1)S(1)}, u32[]{:S(2)}, u32[]{:S(2)}) async-start(bf16[8,72,256]{2,1,0:T(8,128)(2,1)} %get-tuple-element.9), calls=%async_computation.4 | async-start | bytes 589824 | tf_op jit(solution)/shard_map/all_to_all | solution.py:389
  118.8 0.7 copy-start.12
  119.5 10.3 %copy-start.3 = (bf16[256,1536]{1,0:T(8,128)(2,1)S(1)}, bf16[256,1536]{1,0:T(8,128)(2,1)}, u32[]{:S(2)}) copy-start(bf16[256,1536]{1,0:T(8,128)(2,1)} %weight.7) | copy-start | bytes 2359300
  120.4 4.9 %copy-start.17 = (bf16[256]{0:T(256)(128)(2,1)S(1)}, bf16[256]{0:T(256)(128)(2,1)}, u32[]{:S(2)}) copy-start(bf16[256]{0:T(256)(128)(2,1)} %param.37) | copy-start | bytes 1540
  120.4 9.4 %all-to-all-start.6 = ((bf16[4,64,256]{2,1,0:T(8,128)(2,1)}), bf16[4,64,256]{2,1,0:T(8,128)(2,1)S(1)}, u32[]{:S(2)}, u32[]{:S(2)}) async-start(bf16[4,64,256]{2,1,0:T(8,128)(2,1)} %down_kernel.1), calls=%async_computation.6 | async-start | bytes 262144 | tf_op jit(solution)/shard_map/all_to_all | solution.py:389
  125.3 0.7 copy-start.18
  126.0 0.7 copy-start.19
  131.2 3.6 %copy-start.20 = (bf16[192]{0:T(256)(128)(2,1)S(1)}, bf16[192]{0:T(256)(128)(2,1)}, u32[]{:S(2)}) copy-start(bf16[192]{0:T(256)(128)(2,1)} %param.41) | copy-start | bytes 1156
  131.2 14.3 %all-to-all-start.7 = ((bf16[8,72,192]{2,1,0:T(8,128)(2,1)}), bf16[8,72,192]{2,1,0:T(8,128)(2,1)S(1)}, u32[]{:S(2)}, u32[]{:S(2)}) async-start(bf16[8,72,192]{2,1,0:T(8,128)(2,1)} %get-tuple-element.12), calls=%async_computation.7 | async-start | bytes 589824 | tf_op jit(solution)/shard_map/all_to_all | solution.py:389

commit v2 on v1

--- a/solution.py
+++ b/solution.py
@@ -68,19 +68,29 @@
     return stats[:, at : at + 1], stats[:, at + 1 : at + 2] + stats[:, at + 2 : at + 3]
 
 
-def send_kernel(tail_item, query, pages, out):
+def send_kernel(tail_item, fresh, pages, out, items, query, wide, sems):
+    copies = [
+        pltpu.make_async_copy(tail_item, items, sems.at[0]),
+        pltpu.make_async_copy(fresh.at[:, 0], query, sems.at[1]),
+        pltpu.make_async_copy(pages, out.at[:, 0 : 2 * TOK], sems.at[2]),
+    ]
+    for copy in copies:
+        copy.start()
     group = lax.axis_index("pages")
     row = iota((ROWS, ROWS), 0)
+    copies[0].wait()
     source = jnp.zeros((ROWS, ROWS), jnp.int32)
     for j in range(TAILS):
-        item = tail_item[(j // 2) * TAILS + group * 2 + j % 2] - group * TAILS
+        item = items[(j // 2) * TAILS + group * 2 + j % 2] - group * TAILS
         source = jnp.where((row >> 1) == j, item * 2, source)
     pick = one_hot(iota((ROWS, ROWS), 1) == source + (row & 1))
-    picked = dot(pick, query[...])
+    copies[1].wait()
+    for j in range(TAILS):
+        wide[2 * j : 2 * j + 2] = query[j].astype(f32)
+    picked = dot(pick, wide[...].astype(bf16))
     for h in range(GROUPS):
-        out[h, 0:TOK] = pages[h, 0]
-        out[h, TOK : 2 * TOK] = pages[h, 1]
         out[h, 2 * TOK : 2 * TOK + 4] = picked[4 * h : 4 * h + 4].astype(bf16)
+    copies[2].wait()
 
 
 def tail_kernel(tail_item, tail_length, recv, tails, out, wide):
@@ -93,29 +103,97 @@
     lens = jnp.zeros((ROWS, 1), jnp.int32)
     for s in range(TAILS):
         lens = jnp.where((row >> 1) == s, tail_length[tail_item[holder * TAILS + s]], lens)
-    keys = TAILS * TOK
+    some, keys = 16, 128
     key = iota((ROWS, keys), 1)
     token = (key & (TOK - 1)) + token_at
-    usable = ((key >> 4) == (row >> 1)) & (token < lens)
+    usable = ((key >> 4) == ((row >> 1) & 7)) & (token < lens)
     offset = (token - lens - (row & 1)).astype(f32)
     stats = jnp.zeros((ROWS, 128), f32)
     for head in range(HEADS):
         at = slice(head * HD, (head + 1) * HD)
-        k = tails[:, 0, :, at].reshape(keys, HD)
-        v = tails[:, 1, :, at].reshape(keys, HD)
-        scores = dot_t(wide[:, at].astype(bf16), k) * (1.0 / math.sqrt(HD))
+        q = wide[:, at].astype(bf16)
+        scores = jnp.concatenate(
+            [
+                dot_t(q[n * some : (n + 1) * some], tails[8 * n : 8 * n + 8, 0, :, at].reshape(keys, HD))
+                for n in range(ROWS // some)
+            ],
+            axis=0,
+        ) * (1.0 / math.sqrt(HD))
         scores = scores + slope_of(first_head + head) * offset
         scores = jnp.where(usable, scores, masked_score)
         m = rounded(jnp.max(scores, axis=1, keepdims=True))
         weights = jnp.where(usable, jnp.exp(scores - m), 0.0)
         stats = put_stats(stats, head, m, jnp.sum(weights, axis=1, keepdims=True))
-        wide[:, at] = dot(weights.astype(bf16), v)
+        weights = weights.astype(bf16)
+        for n in range(ROWS // some):
+            v = tails[8 * n : 8 * n + 8, 1, :, at].reshape(keys, HD)
+            wide[n * some : (n + 1) * some, at] = dot(weights[n * some : (n + 1) * some], v)
     wide[:, WIDE:PACK] = stats
     for g in range(GROUPS):
         out[g] = wide[4 * g : 4 * g + 4].astype(bf16)
 
 
-def prefix_kernel(prefix_item, prefix_length, tail_length, fresh, recv, out):
+def own_columns():
+    share = BLOCK // NCOL
+    first = lax.axis_index("col") * share
+    return one_hot(iota((share, BLOCK), 1) == iota((share, BLOCK), 0) + first)
+
+
+def gain_rows(gain, shift):
+    row = iota((16, BLOCK), 0)
+    return jnp.where(row == 0, gain, jnp.where(row == 1, shift, 0.0)).astype(bf16)
+
+
+def split(x):
+    hi = rounded(x)
+    return hi, x - hi
+
+
+def prefix_kernel(
+    prefix_item,
+    prefix_length,
+    tail_length,
+    fresh,
+    recv,
+    residual,
+    small,
+    up_weight,
+    qkv_weight,
+    out,
+    base,
+    vectors,
+    up_rows,
+    qkv_rows,
+):
+    table = small[...].astype(f32)
+
+    def line(at):
+        return jnp.concatenate([table[at : at + 1], table[at + 1 : at + 2]], axis=1)
+
+    share = BLOCK // NCOL
+    place = own_columns()
+
+    def placed(row):
+        return dot(jnp.broadcast_to(row, (8, share)).astype(bf16), place)[0:1]
+
+    base[...] = dot(residual[...], place) + placed(table[13:14, 64:128])
+    rows = [line(0), line(4), line(8), placed(table[14:15, 0:64]), line(10), line(12)]
+    edge = iota((8, BLOCK), 0)
+    filled = jnp.zeros((8, BLOCK), f32)
+    for at, values in enumerate(rows):
+        filled = jnp.where(edge == at, values, filled)
+    vectors[...] = filled
+    both = gain_rows(line(0), line(2))
+    for n in range(NROW):
+        parts = dot(both, up_weight[:, n * BLOCK : (n + 1) * BLOCK])
+        rows = jnp.zeros((8, BLOCK), f32)
+        for at, values in enumerate(split(parts[0:1]) + split(parts[1:2])):
+            rows = jnp.where(edge == at, values, rows)
+        up_rows[n] = rows
+    both = gain_rows(line(4), line(6))
+    width = qkv_rows.shape[2]
+    for n in range(NROW):
+        qkv_rows[n] = dot(both, qkv_weight[:, n * width : (n + 1) * width])[0:8]
     group = lax.axis_index("pages")
     row_index = lax.axis_index("row")
     first_head = lax.axis_index("col") * HEADS
@@ -201,13 +279,7 @@
         out[n, :, WIDE:PACK] = stats
 
 
-def own_columns():
-    share = BLOCK // NCOL
-    first = lax.axis_index("col") * share
-    return one_hot(iota((share, BLOCK), 1) == iota((share, BLOCK), 0) + first)
-
-
-def out_kernel(recv, weight, residual, bias, out, wide):
+def out_kernel(recv, weight, base, out, wide):
     stats = [recv[n, :, WIDE:PACK].astype(f32) for n in range(NROW)]
     for head in range(HEADS):
         at = slice(head * HD, (head + 1) * HD)
@@ -222,20 +294,9 @@
             total = total + scale * parts[n][1]
             attended = attended + scale * recv[n, :, at].astype(f32)
         wide[:, at] = (attended / total).astype(bf16)
-    place = own_columns()
-    share = BLOCK // NCOL
-    partial = (
-        dot(wide[...], weight[...])
-        + dot(residual[...], place)
-        + dot(jnp.broadcast_to(bias[...], (8, share)), place)[0:1]
-    ).astype(bf16)
+    partial = (dot(wide[...], weight[...]) + base[...]).astype(bf16)
     for n in range(NCOL):
         out[n] = partial
-
-
-def split(x):
-    hi = rounded(x)
-    return hi, x - hi
 
 
 def centred(values, gain):
@@ -255,32 +316,18 @@
     )
 
 
-def gain_rows(gain, shift):
-    row = iota((16, BLOCK), 0)
-    gain = jnp.broadcast_to(gain.astype(f32), (16, BLOCK))
-    shift = jnp.broadcast_to(shift.astype(f32), (16, BLOCK))
-    return jnp.where(row == 0, gain, jnp.where(row == 1, shift, 0.0)).astype(bf16)
-
-
-def up_kernel(recv, gain, shift, weight, hidden, out):
+def up_kernel(recv, vectors, extra, weight, hidden, out):
     values = recv[0].astype(f32)
     for n in range(1, NCOL):
         values = values + recv[n].astype(f32)
     hidden[...] = values
-    mean, spread, scaled = centred(values, gain[...].astype(f32))
-    columns = list(zip((4, 5, 6, 7), split(mean) + split(spread)))
-    rows = as_rows(columns)
-    extra = gain_rows(gain[...], shift[...])
+    mean, spread, scaled = centred(values, vectors[0:1])
+    rows = as_rows(list(zip((4, 5, 6, 7), split(mean) + split(spread))))
+    rows = jnp.concatenate([rows, jnp.zeros((8, BLOCK - ROWS), f32)], axis=1)
     edge = iota((8, BLOCK), 0)
     for n in range(NROW):
-        w = weight[:, n * BLOCK : (n + 1) * BLOCK]
-        out[n, 0:ROWS] = dot(scaled, w).astype(bf16)
-        both = dot(extra, w)
-        tail = jnp.zeros((8, BLOCK), f32)
-        for at, row in enumerate(split(both[0:1]) + split(both[1:2])):
-            tail = jnp.where(edge == at, row, tail)
-        wide = jnp.concatenate([rows, jnp.zeros((8, BLOCK - ROWS), f32)], axis=1)
-        out[n, ROWS : ROWS + 8] = jnp.where(edge < 4, tail, wide).astype(bf16)
+        out[n, 0:ROWS] = dot(scaled, weight[:, n * BLOCK : (n + 1) * BLOCK]).astype(bf16)
+        out[n, ROWS : ROWS + 8] = jnp.where(edge < 4, extra[n], rows).astype(bf16)
 
 
 def as_columns(recv):
@@ -306,7 +353,7 @@
     means = [column(n, mean_at) for n in range(NROW)]
     mean, scale = scale_of(means, [column(n, spread_at) for n in range(NROW)])
     total = jnp.zeros((ROWS, width), f32)
-    shifted = bias.astype(f32)
+    shifted = bias
     for n in range(NROW):
         edge = recv[n, ROWS : ROWS + 8].astype(f32)
         gained = sum(edge[at : at + 1] for at in gain_at)
@@ -315,17 +362,16 @@
     return total * scale + shifted
 
 
-def hidden_kernel(recv, bias, out):
-    v = projected(recv, BLOCK, bias[...], (0, 1), (2, 3), 4, 6)
+def hidden_kernel(recv, vectors, out):
+    v = projected(recv, BLOCK, vectors[4:5], (0, 1), (2, 3), 4, 6)
     v = 0.5 * v * (1.0 + jnp.tanh(math.sqrt(2.0 / math.pi) * (v + 0.044715 * (v * v * v))))
     v = v.astype(bf16)
     for n in range(NROW):
         out[n] = v
 
 
-def down_kernel(recv, weight, bias, out):
-    share = BLOCK // NCOL
-    total = dot(jnp.broadcast_to(bias[...], (8, share)), own_columns())[0:1]
+def down_kernel(recv, weight, vectors, out):
+    total = vectors[3:4]
     for n in range(NROW):
         total = total + dot(recv[n], weight[n * BLOCK : (n + 1) * BLOCK])
     total = total.astype(bf16)
@@ -333,56 +379,63 @@
         out[n] = total
 
 
-def next_kernel(recv, hidden, gain, shift, score, weight, layer_out, out):
+def next_kernel(recv, hidden, vectors, extra, weight, layer_out, out):
     values = hidden[...]
     for n in range(NCOL):
         values = values + recv[n].astype(f32)
     low = values.astype(bf16)
     values = low.astype(f32)
     layer_out[...] = dot_t(low, own_columns()).astype(bf16)
-    mean, spread, scaled = centred(values, gain[...].astype(f32))
-    scores = jnp.sum(values * score[...].astype(f32), axis=1, keepdims=True)
-    columns = list(zip((2, 3, 4, 5, 6, 7), split(mean) + split(spread) + split(scores)))
-    rows = as_rows(columns)
-    extra = gain_rows(gain[...], shift[...])
+    mean, spread, scaled = centred(values, vectors[1:2])
+    scores = jnp.sum(values * vectors[2:3], axis=1, keepdims=True)
+    rows = as_rows(list(zip((2, 3, 4, 5, 6, 7), split(mean) + split(spread) + split(scores))))
     width = out.shape[2]
+    rows = jnp.concatenate([rows, jnp.zeros((8, width - ROWS), f32)], axis=1)
     edge = iota((8, width), 0)
     for n in range(NROW):
-        w = weight[:, n * width : (n + 1) * width]
-        out[n, 0:ROWS] = dot(scaled, w).astype(bf16)
-        both = dot(extra, w)
-        wide = jnp.concatenate([rows, jnp.zeros((8, width - ROWS), f32)], axis=1)
-        tail = jnp.where(edge == 0, both[0:1], jnp.where(edge == 1, both[1:2], wide))
-        out[n, ROWS : ROWS + 8] = tail.astype(bf16)
-
-
-def final_kernel(recv, bias, projected_next, score_out):
-    width = projected_next.shape[1]
-    projected_next[...] = projected(recv, width, bias[...], (0,), (1,), 2, 4).astype(bf16)
+        out[n, 0:ROWS] = dot(scaled, weight[:, n * width : (n + 1) * width]).astype(bf16)
+        out[n, ROWS : ROWS + 8] = jnp.where(edge < 2, extra[n], rows).astype(bf16)
+
+
+def final_kernel(recv, vectors, projected_next, score_out, wide):
+    width = projected_next.shape[2]
+    wide[...] = projected(recv, width, vectors[5:6, 0:width], (0,), (1,), 2, 4)
+    for i in range(ROWS // 2):
+        projected_next[i] = wide[2 * i : 2 * i + 2].astype(bf16)
     total = jnp.zeros((1, ROWS), f32)
     for n in range(NROW):
         edge = recv[n, ROWS : ROWS + 8, 0:ROWS].astype(f32)
         total = total + edge[6:7] + edge[7:8]
-    score_out[...] = total
-
-
-def call(kernel, out, scalars, arrays, scratch=(), flops=0):
+    hi, rest = split(total)
+    mid, low = split(rest)
+    row = iota((8, ROWS), 0)
+    parts = jnp.where(row == 0, hi, jnp.where(row == 1, mid, jnp.where(row == 2, low, 0.0)))
+    source = iota((ROWS, ROWS // 2), 0)
+    target = iota((ROWS, ROWS // 2), 1) * 2
+    for u in range(2):
+        taken = dot(parts.astype(bf16), one_hot(source == target + u))
+        score_out[u : u + 1] = taken[0:1] + taken[1:2] + taken[2:3]
+
+
+def call(kernel, out, scalars, arrays, scratch=(), remote=()):
     many = isinstance(out, list)
     outs = out if many else [out]
     moved = sum(a.size * a.dtype.itemsize for a in arrays)
     moved += sum(math.prod(s) * jnp.dtype(t).itemsize for s, t in outs)
     shapes = [jax.ShapeDtypeStruct(s, t) for s, t in outs]
     vmem = pl.BlockSpec(memory_space=pltpu.VMEM)
+    specs = [pl.BlockSpec(memory_space=pltpu.HBM)] * len(remote)
+    specs += [pl.BlockSpec(memory_space=pltpu.SMEM)] * len(scalars) + [vmem] * len(arrays)
     return pl.pallas_call(
         kernel,
         out_shape=shapes if many else shapes[0],
-        in_specs=[pl.BlockSpec(memory_space=pltpu.SMEM)] * len(scalars) + [vmem] * len(arrays),
+        in_specs=specs,
         out_specs=[vmem] * len(outs) if many else vmem,
-        scratch_shapes=[pltpu.VMEM(s, t) for s, t in scratch],
-        cost_estimate=pl.CostEstimate(flops=flops, bytes_accessed=moved, transcendentals=0),
+        scratch_shapes=scratch,
+        cost_estimate=pl.CostEstimate(flops=0, bytes_accessed=moved, transcendentals=0),
         compiler_params=pltpu.CompilerParams(vmem_limit_bytes=24 * 1024 * 1024),
         name=kernel.__name__,
-    )(*scalars, *arrays)
+    )(*remote, *scalars, *arrays)
 
 
 def exchange(x, axis):
@@ -416,71 +469,106 @@
     share = residual.shape[2]
     width = qkv_bias.shape[0]
 
-    def line(x):
-        return x.reshape(1, x.shape[0])
-
-    fresh = fresh_qkv.reshape(ROWS, 3 * WIDE)
-    query = fresh_qkv[:, :, 0].reshape(ROWS, WIDE)
-    sent = call(send_kernel, ((GROUPS, 2 * TOK + 4, WIDE), bf16), [tail_item], [query, prefix_pages])
+    small = jnp.concatenate(
+        [
+            mlp_gain,
+            mlp_shift,
+            next_gain,
+            next_shift,
+            score_weight,
+            up_bias,
+            qkv_bias,
+            out_bias,
+            down_bias,
+            jnp.zeros((192,), bf16),
+        ]
+    ).reshape(16, 128)
+    stored = jnp.swapaxes(fresh_qkv, 1, 2).reshape(cont_local, 3, 2, WIDE)
+    sent = call(
+        send_kernel,
+        ((GROUPS, 2 * TOK + 4, WIDE), bf16),
+        [],
+        [],
+        [
+            pltpu.SMEM(tail_item.shape, jnp.int32),
+            pltpu.VMEM((cont_local, 2, WIDE), bf16),
+            pltpu.VMEM((ROWS, WIDE), f32),
+            pltpu.SemaphoreType.DMA((3,)),
+        ],
+        [tail_item, stored, prefix_pages.reshape(GROUPS, 2 * TOK, WIDE)],
+    )
     arrived = exchange(sent, "pages")
     tails = call(
         tail_kernel,
         ((GROUPS, 4, PACK), bf16),
         [tail_item, tail_length],
         [arrived, tail_pages],
-        [((ROWS, PACK), f32)],
+        [pltpu.VMEM((ROWS, PACK), f32)],
     )
     tails = exchange(tails, "pages")
-    prefix = call(
+    prefix, base, vectors, up_rows, qkv_rows = call(
         prefix_kernel,
-        ((ROWS, PACK), f32),
+        [
+            ((ROWS, PACK), f32),
+            ((ROWS, BLOCK), f32),
+            ((8, BLOCK), f32),
+            ((NROW, 8, BLOCK), f32),
+            ((NROW, 8, width), f32),
+        ],
         [prefix_item, prefix_length, tail_length],
-        [fresh, arrived],
+        [
+            fresh_qkv.reshape(ROWS, 3 * WIDE),
+            arrived,
+            residual.reshape(ROWS, share),
+            small,
+            up_weight,
+            qkv_weight,
+        ],
     )
     joined = call(
         join_kernel,
         ((NROW, ROWS, PACK), bf16),
         [tail_item],
         [prefix, tails],
-        [((ROWS, PACK), f32)],
+        [pltpu.VMEM((ROWS, PACK), f32)],
     )
     joined = exchange(joined, "row")
     partial = call(
         out_kernel,
         ((NCOL, ROWS, BLOCK), bf16),
         [],
-        [joined, out_weight, residual.reshape(ROWS, share), line(out_bias)],
-        [((ROWS, WIDE), bf16)],
+        [joined, out_weight, base],
+        [pltpu.VMEM((ROWS, WIDE), bf16)],
     )
     partial = exchange(partial, "col")
     hidden_one, partial = call(
         up_kernel,
         [((ROWS, BLOCK), f32), ((NROW, ROWS + 8, BLOCK), bf16)],
         [],
-        [partial, line(mlp_gain), line(mlp_shift), up_weight],
+        [partial, vectors, up_rows, up_weight],
     )
     partial = exchange(partial, "row")
-    hidden_two = call(hidden_kernel, ((NROW, ROWS, BLOCK), bf16), [], [partial, line(up_bias)])
+    hidden_two = call(hidden_kernel, ((NROW, ROWS, BLOCK), bf16), [], [partial, vectors])
     hidden_two = exchange(hidden_two, "row")
     partial = call(
-        down_kernel, ((NCOL, ROWS, BLOCK), bf16), [], [hidden_two, down_weight, line(down_bias)]
+        down_kernel, ((NCOL, ROWS, BLOCK), bf16), [], [hidden_two, down_weight, vectors]
     )
     partial = exchange(partial, "col")
     layer_out, partial = call(
         next_kernel,
         [((ROWS, share), bf16), ((NROW, ROWS + 8, width), bf16)],
         [],
-        [partial, hidden_one, line(next_gain), line(next_shift), line(score_weight), qkv_weight],
+        [partial, hidden_one, vectors, qkv_rows, qkv_weight],
     )
     partial = exchange(partial, "row")
     projected_next, score_sum = call(
-        final_kernel, [((ROWS, width), bf16), ((1, ROWS), f32)], [], [partial, line(qkv_bias)]
-    )
-    return (
-        layer_out.reshape(cont_local, 2, share),
-        score_sum.reshape(cont_local, 2),
-        projected_next.reshape(cont_local, 2, width),
-    )
+        final_kernel,
+        [((cont_local, 2, width), bf16), ((2, cont_local), f32)],
+        [],
+        [partial, vectors],
+        [pltpu.VMEM((ROWS, width), f32)],
+    )
+    return (layer_out.reshape(cont_local, 2, share), score_sum.T, projected_next)
 
 
 def solution(mesh):

time: 150 us -> 140 us (0.933)
  blocking collectives: 71.1 us -> 116 us
  waiting for transfers between devices: 34.7 us -> 4.27 us
  starting transfers between devices: 20.4 us -> 3.64 us
  local copies, waits for them, and re-layouts: 8.59 us -> 4.19 us
  Pallas kernels: 12.4 us -> 10.8 us
    all_to_all x3 -> x7, blocking collectives: 71.1 us -> 116 us  [exchange(): return lax.all_to_all(x, axis, split_axis=0, concat_axis=0, tiled=True)]
    all_to_all x5 -> x1, waiting for transfers between devices: 34.7 us -> 4.27 us  [exchange(): return lax.all_to_all(x, axis, split_axis=0, concat_axis=0, tiled=True)]
    all_to_all x5 -> x1, starting transfers between devices: 20.4 us -> 3.64 us  [exchange(): return lax.all_to_all(x, axis, split_axis=0, concat_axis=0, tiled=True)]
    unnamed x45 -> x46, local copies, waits for them, and re-layouts: 6.45 us -> 4.1 us
    pallas_call x10, Pallas kernels: 12.4 us -> 10.8 us  [call(): pl.pallas_call(kernel, out_shape=shapes if many else shapes[0], in_specs=...]
  transfers between devices with their start and end apart: 5 -> 1, of which waited for: 5 -> 1; matrix products, arithmetic and copies ran while one was open for 0% -> 0% of each run, Pallas kernels for 1% -> 1%
where the time goes in v2:
time: 140 us
  blocking collectives  116 us (83%)
  Pallas kernels  10.8 us (8%)
  waiting for transfers between devices  4.27 us (3%)
  local copies, waits for them, and re-layouts  4.19 us (3%)
  starting transfers between devices  3.64 us (3%)
    all_to_all x7, blocking collectives, exchange(): return lax.all_to_all(x, axis, split_axis=0, concat_axis=0, tiled=True)  116 us
    pallas_call x10, Pallas kernels, call(): pl.pallas_call(kernel, out_shape=shapes if many else shapes[0], in_specs=...  10.8 us
    all_to_all x1, waiting for transfers between devices, exchange(): return lax.all_to_all(x, axis, split_axis=0, concat_axis=0, tiled=True)  4.27 us
    unnamed x46, local copies, waits for them, and re-layouts  4.1 us
    all_to_all x1, starting transfers between devices, exchange(): return lax.all_to_all(x, axis, split_axis=0, concat_axis=0, tiled=True)  3.64 us
  transfers between devices with their start and end apart: 1, of which 1 were waited for; matrix products, arithmetic and copies ran while one was open for 0% of the time, Pallas kernels for 1%

profile of v2, /device:TPU:2, one launch (start us, length us, event | category | flops | bytes accessed | tf_op | source)
XLA Modules:
  0.0 139.6 jit_solution(642407403344599495)
XLA Ops:
  0.6 0.7 copy-done.8
  1.3 0.9 copy-done.4
  2.2 1.0 copy-done.6
  3.3 0.9 send_kernel.1
  4.2 0.0 copy-start.10
  4.2 26.9 %all_to_all.40.recv = bf16[16,36,512]{2,1,0:T(8,128)(2,1)S(1)} all-to-all(bf16[16,36,512]{2,1,0:T(8,128)(2,1)S(1)} %send_kernel.1), channel_id=1, replica_groups=mesh['pages'=16,'row'=8,'col'=4] {'pages'}, dimensions={0} | all-to-all | bytes 1179648 | tf_op jit(solution)/shard_map/all_to_all | solution.py:442
  31.1 2.4 %tail_kernel.1 = bf16[16,4,640]{2,1,0:T(4,128)(2,1)} custom-call(s32[512]{0:T(512)S(1)} %copy-done.8, s32[512]{0:T(512)S(1)} %copy-done.10, bf16[16,36,512]{2,1,0:T(8,128)(2,1)S(1)} %all_to_all.40.recv, bf16[32,2,16,512]{3,2,1,0:T(8,128)(2,1)S(1)} %copy-done.2), custom_call_target="tpu_custom_call" | custom-call | bytes 1720320 | tf_op jit(solution)/shard_map/tail_kernel/pallas_call | solution.py:429
  33.6 3.6 %all-to-all-start.1 = ((bf16[16,4,640]{2,1,0:T(4,128)(2,1)}), bf16[16,4,640]{2,1,0:T(4,128)(2,1)S(1)}, u32[]{:S(2)}, u32[]{:S(2)}) async-start(bf16[16,4,640]{2,1,0:T(4,128)(2,1)} %tail_kernel.1), calls=%async_computation.1 | async-start | bytes 163840 | tf_op jit(solution)/shard_map/all_to_all | solution.py:442
  37.2 0.1 copy.25
  37.3 0.0 copy-start.13
  37.3 0.0 copy-start.14
  37.4 0.0 copy-start.15
  37.4 0.0 copy-start.16
  37.4 0.0 copy-start.17
  37.4 0.0 copy-start.18
  37.4 0.0 copy-start.19
  37.4 0.0 copy-start.20
  37.4 0.0 copy-start.21
  37.4 0.0 copy-start.11
  37.5 0.5 copy-done.13
  38.0 0.0 copy-done.14
  38.0 0.0 copy-done.15
  38.0 0.0 copy-done.16
  38.0 0.0 copy-done.17
  38.0 0.0 copy-done.18
  38.1 0.0 copy-done.19
  38.1 0.0 copy-done.20
  38.1 0.0 copy-done.21
  38.1 0.1 concatenate.3
  38.2 0.0 copy-done.9
  38.2 0.6 copy-done.12
  38.9 2.1 %prefix_kernel.1 = (f32[64,640]{1,0:T(8,128)S(1)}, f32[64,256]{1,0:T(8,128)S(1)}, f32[8,256]{1,0:T(8,128)S(1)}, f32[8,8,256]{2,1,0:T(8,128)S(1)}, f32[8,8,192]{2,1,0:T(8,128)S(1)}) custom-call(s32[256]{0:T(256)S(1)} %copy-done.11, s32[32]{0:T(128)S(1)} %copy-done.12, s32[512]{0:T(512)S(1)} %copy-done.10, bf16[64,1536]{1,0:T(8,128)(2,1)S(1)} %bitcast.9, ...), custom_call_target="tpu_custom_call" | custom-call | bytes 2985984 | tf_op jit(solution)/shard_map/prefix_kernel/pallas_call | solution.py:429
  40.9 4.3 %all-to-all-done.1.recv = bf16[16,4,640]{2,1,0:T(4,128)(2,1)S(1)} async-done(((bf16[16,4,640]{2,1,0:T(4,128)(2,1)}), bf16[16,4,640]{2,1,0:T(4,128)(2,1)S(1)}, u32[]{:S(2)}, u32[]{:S(2)}) %all-to-all-start.1) | async-done | bytes 81952 | tf_op jit(solution)/shard_map/all_to_all | solution.py:442
  45.2 1.1 join_kernel.1
  46.3 0.0 copy-start.7
  46.3 31.2 %all_to_all.41.recv = bf16[8,64,640]{2,1,0:T(8,128)(2,1)S(1)} all-to-all(bf16[8,64,640]{2,1,0:T(8,128)(2,1)S(1)} %join_kernel.1), channel_id=1, replica_groups=mesh['pages'=16,'row'=8,'col'=4] {'row'}, dimensions={0} | all-to-all | bytes 1310720 | tf_op jit(solution)/shard_map/all_to_all | solution.py:442
  77.5 0.7 out_kernel.1
  78.2 9.1 %all_to_all.42.recv = bf16[4,64,256]{2,1,0:T(8,128)(2,1)S(1)} all-to-all(bf16[4,64,256]{2,1,0:T(8,128)(2,1)S(1)} %out_kernel.1), channel_id=1, replica_groups=mesh['pages'=16,'row'=8,'col'=4] {'col'}, dimensions={0} | all-to-all | bytes 262144 | tf_op jit(solution)/shard_map/all_to_all | solution.py:442
  87.3 0.5 up_kernel.1
  87.8 0.0 copy-start.3
  87.9 14.1 %all_to_all.43.recv = bf16[8,72,256]{2,1,0:T(8,128)(2,1)S(1)} all-to-all(bf16[8,72,256]{2,1,0:T(8,128)(2,1)S(1)} %get-tuple-element.18), channel_id=1, replica_groups=mesh['pages'=16,'row'=8,'col'=4] {'row'}, dimensions={0} | all-to-all | bytes 589824 | tf_op jit(solution)/shard_map/all_to_all | solution.py:442
  102.0 0.7 hidden_kernel.1
  102.7 12.9 %all_to_all.44.recv = bf16[8,64,256]{2,1,0:T(8,128)(2,1)S(1)} all-to-all(bf16[8,64,256]{2,1,0:T(8,128)(2,1)S(1)} %hidden_kernel.1), channel_id=1, replica_groups=mesh['pages'=16,'row'=8,'col'=4] {'row'}, dimensions={0} | all-to-all | bytes 524288 | tf_op jit(solution)/shard_map/all_to_all | solution.py:442
  115.6 0.3 down_kernel.1
  115.9 8.4 %all_to_all.45.recv = bf16[4,64,256]{2,1,0:T(8,128)(2,1)S(1)} all-to-all(bf16[4,64,256]{2,1,0:T(8,128)(2,1)S(1)} %down_kernel.1), channel_id=1, replica_groups=mesh['pages'=16,'row'=8,'col'=4] {'col'}, dimensions={0} | all-to-all | bytes 262144 | tf_op jit(solution)/shard_map/all_to_all | solution.py:442
  124.2 0.9 next_kernel.1
  125.1 13.2 %all_to_all.46.recv = bf16[8,72,192]{2,1,0:T(8,128)(2,1)S(1)} all-to-all(bf16[8,72,192]{2,1,0:T(8,128)(2,1)S(1)} %get-tuple-element.22), channel_id=1, replica_groups=mesh['pages'=16,'row'=8,'col'=4] {'row'}, dimensions={0} | all-to-all | bytes 442368 | tf_op jit(solution)/shard_map/all_to_all | solution.py:442
  138.3 1.2 final_kernel.1
  (19 shorter events, 0.1 us)
Async XLA Ops:
  0.6 0.7 copy-start.8
  1.3 0.9 copy-start.4
  2.2 1.0 copy-start.6
  3.3 27.8 %copy-start.2 = (bf16[32,2,16,512]{3,2,1,0:T(8,128)(2,1)S(1)}, bf16[32,2,16,512]{3,2,1,0:T(8,128)(2,1)}, u32[]{:S(2)}) copy-start(bf16[32,2,16,512]{3,2,1,0:T(8,128)(2,1)} %tails.1) | copy-start | bytes 3145732
  4.2 27.0 %copy-start.10 = (s32[512]{0:T(512)S(1)}, s32[512]{0:T(512)}, u32[]{:S(2)}) copy-start(s32[512]{0:T(512)} %tail_length.3) | copy-start | bytes 6148
  31.1 6.1 %copy-start.5 = (bf16[32,2,3,512]{3,1,2,0:T(2,128)(2,1)S(1)}, bf16[32,2,3,512]{3,1,2,0:T(2,128)(2,1)}, u32[]{:S(2)}) copy-start(bf16[32,2,3,512]{3,1,2,0:T(2,128)(2,1)} %param.22) | copy-start | bytes 589828
  31.1 7.1 %copy-start = (bf16[256,2048]{1,0:T(8,128)(2,1)S(1)}, bf16[256,2048]{1,0:T(8,128)(2,1)}, u32[]{:S(2)}) copy-start(bf16[256,2048]{1,0:T(8,128)(2,1)} %weight.5) | copy-start | bytes 3145732
  33.6 4.6 %copy-start.1 = (bf16[256,1536]{1,0:T(8,128)(2,1)S(1)}, bf16[256,1536]{1,0:T(8,128)(2,1)}, u32[]{:S(2)}) copy-start(bf16[256,1536]{1,0:T(8,128)(2,1)} %weight.7) | copy-start | bytes 2359300
  33.6 11.7 %all-to-all-start.1 = ((bf16[16,4,640]{2,1,0:T(4,128)(2,1)}), bf16[16,4,640]{2,1,0:T(4,128)(2,1)S(1)}, u32[]{:S(2)}, u32[]{:S(2)}) async-start(bf16[16,4,640]{2,1,0:T(4,128)(2,1)} %tail_kernel.1), calls=%async_computation.1 | async-start | bytes 163840 | tf_op jit(solution)/shard_map/all_to_all | solution.py:442
  37.3 0.7 copy-start.13
  37.3 0.7 copy-start.14
  37.4 0.7 copy-start.15
  37.4 0.7 copy-start.16
  37.4 0.7 copy-start.17
  37.4 0.7 copy-start.18
  37.4 0.7 copy-start.19
  37.4 0.7 copy-start.20
  37.4 0.7 copy-start.21
  37.4 0.8 copy-start.11
  37.5 0.7 copy-start.9
  38.2 0.7 copy-start.12
  46.3 31.2 %copy-start.7 = (bf16[512,256]{1,0:T(8,128)(2,1)S(1)}, bf16[512,256]{1,0:T(8,128)(2,1)}, u32[]{:S(2)}) copy-start(bf16[512,256]{1,0:T(8,128)(2,1)} %weight.4) | copy-start | bytes 786436
  87.8 27.7 %copy-start.3 = (bf16[2048,256]{1,0:T(8,128)(2,1)S(1)}, bf16[2048,256]{1,0:T(8,128)(2,1)}, u32[]{:S(2)}) copy-start(bf16[2048,256]{1,0:T(8,128)(2,1)} %weight.6) | copy-start | bytes 3145732

commit v3 on v2

--- a/solution.py
+++ b/solution.py
@@ -24,6 +24,7 @@
 BLOCK = D // NROW
 TOK = 16
 TAILS = 32
+KEYROWS = 2 * HEADS * TOK
 
 masked_score = -1e30
 norm_eps = 1e-05
@@ -68,69 +69,60 @@
     return stats[:, at : at + 1], stats[:, at + 1 : at + 2] + stats[:, at + 2 : at + 3]
 
 
-def send_kernel(tail_item, fresh, pages, out, items, query, wide, sems):
+def send_kernel(tail_item, fresh, pages, out, items, query, wide, rows, stage, sems, out_sems):
     copies = [
         pltpu.make_async_copy(tail_item, items, sems.at[0]),
         pltpu.make_async_copy(fresh.at[:, 0], query, sems.at[1]),
-        pltpu.make_async_copy(pages, out.at[:, 0 : 2 * TOK], sems.at[2]),
     ]
+    for n in range(2 * HEADS):
+        head = slice((n % HEADS) * HD, (n % HEADS + 1) * HD)
+        copies.append(
+            pltpu.make_async_copy(
+                pages.at[:, n // HEADS, :, head],
+                stage.at[:, n * TOK : (n + 1) * TOK],
+                sems.at[2 + n],
+            )
+        )
     for copy in copies:
         copy.start()
     group = lax.axis_index("pages")
-    row = iota((ROWS, ROWS), 0)
+    source, lane = iota((128, ROWS), 0), iota((128, ROWS), 1)
+    place = (((lane >> 2) & 3) == (source >> 5)) & (
+        (source & (TAILS - 1)) == group * 2 + ((lane >> 1) & 1)
+    )
+    place = one_hot(place)
     copies[0].wait()
-    source = jnp.zeros((ROWS, ROWS), jnp.int32)
-    for j in range(TAILS):
-        item = items[(j // 2) * TAILS + group * 2 + j % 2] - group * TAILS
-        source = jnp.where((row >> 1) == j, item * 2, source)
-    pick = one_hot(iota((ROWS, ROWS), 1) == source + (row & 1))
+    local = (items[...] & (TAILS - 1)).astype(f32).astype(bf16)
+    found = dot(local, place)
+    here = iota(found.shape, 0) == (iota(found.shape, 1) >> 4)
+    target = jnp.sum(jnp.where(here, found, 0.0), axis=0, keepdims=True).astype(jnp.int32) * 2
+    target = target + (iota((1, ROWS), 1) & 1)
+    pick = one_hot(iota((ROWS, ROWS), 0) == target)
     copies[1].wait()
     for j in range(TAILS):
         wide[2 * j : 2 * j + 2] = query[j].astype(f32)
-    picked = dot(pick, wide[...].astype(bf16))
+    leaving = []
+    for n in range(2 * HEADS):
+        part = slice(n * TOK, (n + 1) * TOK)
+        copies[2 + n].wait()
+        leaving.append(pltpu.make_async_copy(stage.at[:, part], out.at[:, part], out_sems.at[n]))
+        leaving[n].start()
+    picked = lax.dot_general(
+        pick, wide[...].astype(bf16), (((0,), (0,)), ((), ())), preferred_element_type=f32
+    )
     for h in range(GROUPS):
-        out[h, 2 * TOK : 2 * TOK + 4] = picked[4 * h : 4 * h + 4].astype(bf16)
-    copies[2].wait()
-
-
-def tail_kernel(tail_item, tail_length, recv, tails, out, wide):
-    holder = lax.axis_index("pages")
-    token_at = lax.axis_index("row") * TOK
-    first_head = lax.axis_index("col") * HEADS
-    for g in range(GROUPS):
-        wide[4 * g : 4 * g + 4, 0:WIDE] = recv[g, 2 * TOK : 2 * TOK + 4].astype(f32)
-    row = iota((ROWS, 1), 0)
-    lens = jnp.zeros((ROWS, 1), jnp.int32)
-    for s in range(TAILS):
-        lens = jnp.where((row >> 1) == s, tail_length[tail_item[holder * TAILS + s]], lens)
-    some, keys = 16, 128
-    key = iota((ROWS, keys), 1)
-    token = (key & (TOK - 1)) + token_at
-    usable = ((key >> 4) == ((row >> 1) & 7)) & (token < lens)
-    offset = (token - lens - (row & 1)).astype(f32)
-    stats = jnp.zeros((ROWS, 128), f32)
-    for head in range(HEADS):
-        at = slice(head * HD, (head + 1) * HD)
-        q = wide[:, at].astype(bf16)
-        scores = jnp.concatenate(
-            [
-                dot_t(q[n * some : (n + 1) * some], tails[8 * n : 8 * n + 8, 0, :, at].reshape(keys, HD))
-                for n in range(ROWS // some)
-            ],
-            axis=0,
-        ) * (1.0 / math.sqrt(HD))
-        scores = scores + slope_of(first_head + head) * offset
-        scores = jnp.where(usable, scores, masked_score)
-        m = rounded(jnp.max(scores, axis=1, keepdims=True))
-        weights = jnp.where(usable, jnp.exp(scores - m), 0.0)
-        stats = put_stats(stats, head, m, jnp.sum(weights, axis=1, keepdims=True))
-        weights = weights.astype(bf16)
-        for n in range(ROWS // some):
-            v = tails[8 * n : 8 * n + 8, 1, :, at].reshape(keys, HD)
-            wide[n * some : (n + 1) * some, at] = dot(weights[n * some : (n + 1) * some], v)
-    wide[:, WIDE:PACK] = stats
-    for g in range(GROUPS):
-        out[g] = wide[4 * g : 4 * g + 4].astype(bf16)
+        for head in range(HEADS):
+            at = h * TOK + head * 4
+            rows[at : at + 4] = picked[4 * h : 4 * h + 4, head * HD : (head + 1) * HD]
+    stage[:, KEYROWS:] = rows[...].reshape(GROUPS, TOK, HD).astype(bf16)
+    last = pltpu.make_async_copy(
+        stage.at[:, KEYROWS : KEYROWS + TOK],
+        out.at[:, KEYROWS : KEYROWS + TOK],
+        out_sems.at[2 * HEADS],
+    )
+    last.start()
+    for copy in leaving + [last]:
+        copy.wait()
 
 
 def own_columns():
@@ -149,67 +141,49 @@
     return hi, x - hi
 
 
-def prefix_kernel(
+def ready_kernel(
+    tail_item,
+    tail_length,
     prefix_item,
     prefix_length,
-    tail_length,
-    fresh,
-    recv,
     residual,
     small,
-    up_weight,
-    qkv_weight,
-    out,
+    tail_offset,
+    prefix_offset,
+    order,
     base,
     vectors,
-    up_rows,
-    qkv_rows,
 ):
-    table = small[...].astype(f32)
-
-    def line(at):
-        return jnp.concatenate([table[at : at + 1], table[at + 1 : at + 2]], axis=1)
-
-    share = BLOCK // NCOL
-    place = own_columns()
-
-    def placed(row):
-        return dot(jnp.broadcast_to(row, (8, share)).astype(bf16), place)[0:1]
-
-    base[...] = dot(residual[...], place) + placed(table[13:14, 64:128])
-    rows = [line(0), line(4), line(8), placed(table[14:15, 0:64]), line(10), line(12)]
-    edge = iota((8, BLOCK), 0)
-    filled = jnp.zeros((8, BLOCK), f32)
-    for at, values in enumerate(rows):
-        filled = jnp.where(edge == at, values, filled)
-    vectors[...] = filled
-    both = gain_rows(line(0), line(2))
-    for n in range(NROW):
-        parts = dot(both, up_weight[:, n * BLOCK : (n + 1) * BLOCK])
-        rows = jnp.zeros((8, BLOCK), f32)
-        for at, values in enumerate(split(parts[0:1]) + split(parts[1:2])):
-            rows = jnp.where(edge == at, values, rows)
-        up_rows[n] = rows
-    both = gain_rows(line(4), line(6))
-    width = qkv_rows.shape[2]
-    for n in range(NROW):
-        qkv_rows[n] = dot(both, qkv_weight[:, n * width : (n + 1) * width])[0:8]
     group = lax.axis_index("pages")
     row_index = lax.axis_index("row")
-    first_head = lax.axis_index("col") * HEADS
     row = iota((ROWS, 1), 0)
-    tail_lens = jnp.zeros((ROWS, 1), jnp.int32)
+    step = row & 1
+    lens = jnp.zeros((ROWS, 1), jnp.int32)
+    own_lens = jnp.zeros((ROWS, 1), jnp.int32)
+    lane = iota((1, ROWS), 1)
+    target = lane & 1
     for j in range(TAILS):
-        tail_lens = jnp.where((row >> 1) == j, tail_length[group * TAILS + j], tail_lens)
+        here = (row >> 1) == j
+        lens = jnp.where(here, tail_length[tail_item[group * TAILS + j]], lens)
+        own_lens = jnp.where(here, tail_length[group * TAILS + j], own_lens)
+        item = tail_item[(j // 2) * TAILS + group * 2 + j % 2] - group * TAILS
+        target = target + jnp.where((lane >> 1) == j, item * 2, 0)
+    order[...] = one_hot(iota((ROWS, ROWS), 0) == target)
+
+    key = iota((ROWS, 8 * TOK), 1)
+    token = (key & (TOK - 1)) + row_index * TOK
+    usable = ((key >> 4) == ((row >> 1) & 7)) & (token < lens)
+    offset = (token - lens - step).astype(f32)
+    tail_offset[...] = jnp.where(usable, offset, masked_score)
+
     row_prompt = row >> 5
     prompt_lens = jnp.where(
         row_prompt == 0, prefix_length[group * 2], prefix_length[group * 2 + 1]
     )
-    query_pos = prompt_lens + tail_lens + (row & 1)
-    keys = GROUPS * TOK
-    lane = iota((1, keys), 1)
+    query_pos = prompt_lens + own_lens + step
+    lane = iota((1, GROUPS * TOK), 1)
     key_pos = (lane & (TOK - 1)) + row_index * TOK
-    key_prompt = jnp.zeros((1, keys), jnp.int32)
+    key_prompt = jnp.zeros((1, GROUPS * TOK), jnp.int32)
     for h in range(GROUPS):
         item = prefix_item[h * GROUPS + group]
         here = (lane >> 4) == h
@@ -217,6 +191,83 @@
         key_prompt = jnp.where(here, (item >> 3) - group * 2, key_prompt)
     usable = (key_prompt == row_prompt) & (key_pos < prompt_lens)
     offset = (key_pos - query_pos).astype(f32)
+    prefix_offset[...] = jnp.where(usable, offset, masked_score)
+
+    table = small[...].astype(f32)
+
+    def line(at):
+        return jnp.concatenate([table[at : at + 1], table[at + 1 : at + 2]], axis=1)
+
+    share = BLOCK // NCOL
+    place = own_columns()
+
+    def placed(values):
+        return dot(jnp.broadcast_to(values, (8, share)).astype(bf16), place)[0:1]
+
+    base[...] = dot(residual[...], place) + placed(table[13:14, 64:128])
+    rows = [line(0), line(4), line(8), placed(table[14:15, 0:64]), line(10), line(12), line(2), line(6)]
+    edge = iota((8, BLOCK), 0)
+    filled = jnp.zeros((8, BLOCK), f32)
+    for at, values in enumerate(rows):
+        filled = jnp.where(edge == at, values, filled)
+    vectors[...] = filled
+
+
+def tail_kernel(recv, tails, distance, out, query, wide):
+    first_head = lax.axis_index("col") * HEADS
+    distance = distance[...]
+    usable = distance > 0.5 * masked_score
+    for g in range(GROUPS):
+        rows = recv[g, KEYROWS:].astype(f32)
+        for head in range(HEADS):
+            query[head, 4 * g : 4 * g + 4] = rows[4 * head : 4 * head + 4]
+    some = ROWS * 8 // TAILS
+    blocks = ROWS // some
+    stats = jnp.zeros((ROWS, 128), f32)
+    for head in range(HEADS):
+        at = slice(head * HD, (head + 1) * HD)
+        q = query[head].astype(bf16)
+        parts = []
+        for n in range(blocks):
+            k = tails[8 * n : 8 * n + 8, 0, :, at].reshape(8 * TOK, HD)
+            parts.append(dot_t(q[n * some : (n + 1) * some], k))
+        scores = jnp.concatenate(parts, axis=0) * (1.0 / math.sqrt(HD))
+        scores = scores + slope_of(first_head + head) * distance
+        scores = jnp.where(usable, scores, masked_score)
+        m = rounded(jnp.max(scores, axis=1, keepdims=True))
+        weights = jnp.where(usable, jnp.exp(scores - m), 0.0)
+        stats = put_stats(stats, head, m, jnp.sum(weights, axis=1, keepdims=True))
+        weights = weights.astype(bf16)
+        for n in range(blocks):
+            v = tails[8 * n : 8 * n + 8, 1, :, at].reshape(8 * TOK, HD)
+            wide[n * some : (n + 1) * some, at] = dot(weights[n * some : (n + 1) * some], v)
+    wide[:, WIDE:PACK] = stats
+    for g in range(GROUPS):
+        out[g] = wide[4 * g : 4 * g + 4].astype(bf16)
+
+
+def prefix_kernel(
+    fresh, recv, distance, vectors, up_weight, qkv_weight, out, up_rows, qkv_rows
+):
+    both = gain_rows(vectors[0:1], vectors[6:7])
+    edge = iota((8, BLOCK), 0)
+    for n in range(NROW):
+        parts = dot(both, up_weight[:, n * BLOCK : (n + 1) * BLOCK])
+        rows = jnp.zeros((8, BLOCK), f32)
+        for at, values in enumerate(split(parts[0:1]) + split(parts[1:2])):
+            rows = jnp.where(edge == at, values, rows)
+        up_rows[n] = rows
+    both = gain_rows(vectors[1:2], vectors[7:8])
+    width = qkv_rows.shape[2]
+    for n in range(NROW):
+        qkv_rows[n] = dot(both, qkv_weight[:, n * width : (n + 1) * width])[0:8]
+
+    distance = distance[...]
+    usable = distance > 0.5 * masked_score
+    row_index = lax.axis_index("row")
+    first_head = lax.axis_index("col") * HEADS
+    row = iota((ROWS, 1), 0)
+    keys = GROUPS * TOK
     col = iota((ROWS, ROWS), 1)
     new_usable = ((col >> 1) == (row >> 1)) & ((col & 1) <= (row & 1)) & (row_index == 0)
     new_offset = ((col & 1) - (row & 1)).astype(f32)
@@ -226,10 +277,10 @@
         q = fresh[:, head * HD : (head + 1) * HD]
         new_k = fresh[:, WIDE + head * HD : WIDE + (head + 1) * HD]
         new_v = fresh[:, 2 * WIDE + head * HD : 2 * WIDE + (head + 1) * HD]
-        k = recv[:, 0:TOK, at].reshape(keys, HD)
-        v = recv[:, TOK : 2 * TOK, at].reshape(keys, HD)
+        k = recv[:, head * TOK : (head + 1) * TOK].reshape(keys, HD)
+        v = recv[:, (HEADS + head) * TOK : (HEADS + head + 1) * TOK].reshape(keys, HD)
         slope = slope_of(first_head + head)
-        scores = dot_t(q, k) * (1.0 / math.sqrt(HD)) + slope * offset
+        scores = dot_t(q, k) * (1.0 / math.sqrt(HD)) + slope * distance
         scores = jnp.where(usable, scores, masked_score)
         new_scores = dot_t(q, new_k) * (1.0 / math.sqrt(HD)) + slope * new_offset
         new_scores = jnp.where(new_usable, new_scores, masked_score)
@@ -249,17 +300,10 @@
     out[:, WIDE:PACK] = stats
 
 
-def join_kernel(tail_item, prefix, recv, out, wide):
-    group = lax.axis_index("pages")
+def join_kernel(order, prefix, recv, out, wide):
     for h in range(GROUPS):
         wide[4 * h : 4 * h + 4] = recv[h].astype(f32)
-    lane = iota((1, ROWS), 1)
-    target = lane & 1
-    for j in range(TAILS):
-        item = tail_item[(j // 2) * TAILS + group * 2 + j % 2] - group * TAILS
-        target = target + jnp.where((lane >> 1) == j, item * 2, 0)
-    order = one_hot(iota((ROWS, ROWS), 0) == target)
-    tails = dot(order, wide[...].astype(bf16))
+    tails = dot(order[...], wide[...].astype(bf16))
     tail_stats = tails[:, WIDE:PACK]
     prefix_stats = prefix[:, WIDE:PACK]
     stats = jnp.zeros((ROWS, 128), f32)
@@ -305,14 +349,16 @@
     return mean, jnp.sum(away * away, axis=1, keepdims=True), (away * gain).astype(bf16)
 
 
-def as_rows(columns):
+def as_rows(columns, order=None):
     lane = iota((ROWS, 8), 1)
     table = jnp.zeros((ROWS, 8), f32)
     for at, column in columns:
         table = jnp.where(lane == at, column, table)
-    eye = one_hot(iota((ROWS, ROWS), 0) == iota((ROWS, ROWS), 1))
+    if order is None:
+        order = iota((ROWS, ROWS), 1)
+    order = one_hot(iota((ROWS, ROWS), 0) == order)
     return lax.dot_general(
-        table.astype(bf16), eye, (((0,), (0,)), ((), ())), preferred_element_type=f32
+        table.astype(bf16), order, (((0,), (0,)), ((), ())), preferred_element_type=f32
     )
 
 
@@ -388,7 +434,10 @@
     layer_out[...] = dot_t(low, own_columns()).astype(bf16)
     mean, spread, scaled = centred(values, vectors[1:2])
     scores = jnp.sum(values * vectors[2:3], axis=1, keepdims=True)
-    rows = as_rows(list(zip((2, 3, 4, 5, 6, 7), split(mean) + split(spread) + split(scores))))
+    lane = iota((ROWS, ROWS), 1)
+    by_step = ((lane & 31) << 1) + (lane >> 5)
+    rows = as_rows(list(zip((2, 3, 4, 5), split(mean) + split(spread))))
+    rows = rows + as_rows(list(zip((6, 7), split(scores))), by_step)
     width = out.shape[2]
     rows = jnp.concatenate([rows, jnp.zeros((8, width - ROWS), f32)], axis=1)
     edge = iota((8, width), 0)
@@ -406,18 +455,12 @@
     for n in range(NROW):
         edge = recv[n, ROWS : ROWS + 8, 0:ROWS].astype(f32)
         total = total + edge[6:7] + edge[7:8]
-    hi, rest = split(total)
-    mid, low = split(rest)
-    row = iota((8, ROWS), 0)
-    parts = jnp.where(row == 0, hi, jnp.where(row == 1, mid, jnp.where(row == 2, low, 0.0)))
-    source = iota((ROWS, ROWS // 2), 0)
-    target = iota((ROWS, ROWS // 2), 1) * 2
-    for u in range(2):
-        taken = dot(parts.astype(bf16), one_hot(source == target + u))
-        score_out[u : u + 1] = taken[0:1] + taken[1:2] + taken[2:3]
-
-
-def call(kernel, out, scalars, arrays, scratch=(), remote=()):
+    half = ROWS // 2
+    score_out[0:1] = total[:, 0:half]
+    score_out[1:2] = total[:, half:]
+
+
+def call(kernel, out, scalars, arrays, scratch=(), remote=(), limit=16, home=pltpu.VMEM):
     many = isinstance(out, list)
     outs = out if many else [out]
     moved = sum(a.size * a.dtype.itemsize for a in arrays)
@@ -430,10 +473,10 @@
         kernel,
         out_shape=shapes if many else shapes[0],
         in_specs=specs,
-        out_specs=[vmem] * len(outs) if many else vmem,
+        out_specs=[vmem] * len(outs) if many else pl.BlockSpec(memory_space=home),
         scratch_shapes=scratch,
         cost_estimate=pl.CostEstimate(flops=0, bytes_accessed=moved, transcendentals=0),
-        compiler_params=pltpu.CompilerParams(vmem_limit_bytes=24 * 1024 * 1024),
+        compiler_params=pltpu.CompilerParams(vmem_limit_bytes=limit * 1024 * 1024),
         name=kernel.__name__,
     )(*remote, *scalars, *arrays)
 
@@ -486,41 +529,52 @@
     stored = jnp.swapaxes(fresh_qkv, 1, 2).reshape(cont_local, 3, 2, WIDE)
     sent = call(
         send_kernel,
-        ((GROUPS, 2 * TOK + 4, WIDE), bf16),
+        ((GROUPS, KEYROWS + TOK, HD), bf16),
         [],
         [],
         [
-            pltpu.SMEM(tail_item.shape, jnp.int32),
+            pltpu.VMEM((4, 128), jnp.int32),
             pltpu.VMEM((cont_local, 2, WIDE), bf16),
             pltpu.VMEM((ROWS, WIDE), f32),
-            pltpu.SemaphoreType.DMA((3,)),
+            pltpu.VMEM((GROUPS * TOK, HD), f32),
+            pltpu.VMEM((GROUPS, KEYROWS + TOK, HD), bf16),
+            pltpu.SemaphoreType.DMA((2 + 2 * HEADS,)),
+            pltpu.SemaphoreType.DMA((1 + 2 * HEADS,)),
         ],
-        [tail_item, stored, prefix_pages.reshape(GROUPS, 2 * TOK, WIDE)],
+        [tail_item.reshape(4, 128), stored, prefix_pages],
+        60,
+        pltpu.HBM,
     )
     arrived = exchange(sent, "pages")
+    tail_offset, prefix_offset, order, base, vectors = call(
+        ready_kernel,
+        [
+            ((ROWS, 8 * TOK), f32),
+            ((ROWS, GROUPS * TOK), f32),
+            ((ROWS, ROWS), bf16),
+            ((ROWS, BLOCK), f32),
+            ((8, BLOCK), f32),
+        ],
+        [tail_item, tail_length, prefix_item, prefix_length],
+        [residual.reshape(ROWS, share), small],
+    )
     tails = call(
         tail_kernel,
         ((GROUPS, 4, PACK), bf16),
-        [tail_item, tail_length],
-        [arrived, tail_pages],
-        [pltpu.VMEM((ROWS, PACK), f32)],
+        [],
+        [arrived, tail_pages, tail_offset],
+        [pltpu.VMEM((HEADS, ROWS, HD), f32), pltpu.VMEM((ROWS, PACK), f32)],
     )
     tails = exchange(tails, "pages")
-    prefix, base, vectors, up_rows, qkv_rows = call(
+    prefix, up_rows, qkv_rows = call(
         prefix_kernel,
-        [
-            ((ROWS, PACK), f32),
-            ((ROWS, BLOCK), f32),
-            ((8, BLOCK), f32),
-            ((NROW, 8, BLOCK), f32),
-            ((NROW, 8, width), f32),
-        ],
-        [prefix_item, prefix_length, tail_length],
+        [((ROWS, PACK), f32), ((NROW, 8, BLOCK), f32), ((NROW, 8, width), f32)],
+        [],
         [
             fresh_qkv.reshape(ROWS, 3 * WIDE),
             arrived,
-            residual.reshape(ROWS, share),
-            small,
+            prefix_offset,
+            vectors,
             up_weight,
             qkv_weight,
         ],
@@ -528,8 +582,8 @@
     joined = call(
         join_kernel,
         ((NROW, ROWS, PACK), bf16),
-        [tail_item],
-        [prefix, tails],
+        [],
+        [order, prefix, tails],
         [pltpu.VMEM((ROWS, PACK), f32)],
     )
     joined = exchange(joined, "row")

time: 140 us -> 135 us (0.964)
  blocking collectives: 116 us -> 87.9 us
  waiting for transfers between devices: 4.27 us -> 21.2 us
  starting transfers between devices: 3.64 us -> 11.9 us
  local copies, waits for them, and re-layouts: 4.19 us -> 1.6 us
    all_to_all x7 -> x6, blocking collectives: 116 us -> 87.9 us  [exchange(): return lax.all_to_all(x, axis, split_axis=0, concat_axis=0, tiled=True)]
    all_to_all x1 -> x2, waiting for transfers between devices: 4.27 us -> 21.2 us  [exchange(): return lax.all_to_all(x, axis, split_axis=0, concat_axis=0, tiled=True)]
    all_to_all x1 -> x2, starting transfers between devices: 3.64 us -> 11.9 us  [exchange(): return lax.all_to_all(x, axis, split_axis=0, concat_axis=0, tiled=True)]
    unnamed x46 -> x42, local copies, waits for them, and re-layouts: 4.1 us -> 1.51 us
    pallas_call x10 -> x11, Pallas kernels: 10.8 us -> 11.1 us  [call(): pl.pallas_call(kernel, out_shape=shapes if many else shapes[0], in_specs=...]
  transfers between devices with their start and end apart: 1 -> 2, of which waited for: 1 -> 2; matrix products, arithmetic and copies ran while one was open for 0% -> 0% of each run, Pallas kernels for 1% -> 2%
where the time goes in v3:
time: 135 us
  blocking collectives  87.9 us (65%)
  waiting for transfers between devices  21.2 us (16%)
  starting transfers between devices  11.9 us (9%)
  Pallas kernels  11.1 us (8%)
  local copies, waits for them, and re-layouts  1.6 us (1%)
    all_to_all x6, blocking collectives, exchange(): return lax.all_to_all(x, axis, split_axis=0, concat_axis=0, tiled=True)  87.9 us
    all_to_all x2, waiting for transfers between devices, exchange(): return lax.all_to_all(x, axis, split_axis=0, concat_axis=0, tiled=True)  21.2 us
    all_to_all x2, starting transfers between devices, exchange(): return lax.all_to_all(x, axis, split_axis=0, concat_axis=0, tiled=True)  11.9 us
    pallas_call x11, Pallas kernels, call(): pl.pallas_call(kernel, out_shape=shapes if many else shapes[0], in_specs=...  11.1 us
  transfers between devices with their start and end apart: 2, of which 2 were waited for; matrix products, arithmetic and copies ran while one was open for 0% of the time, Pallas kernels for 2%

profile of v3, /device:TPU:2, one launch (start us, length us, event | category | flops | bytes accessed | tf_op | source)
XLA Modules:
  0.0 134.7 jit_solution(17735690539573467360)
XLA Ops:
  0.6 2.2 %send_kernel.1 = bf16[16,144,128]{2,1,0:T(8,128)(2,1)} custom-call(s32[4,128]{1,0:T(4,128)} %bitcast.12, bf16[32,3,2,512]{3,2,1,0:T(2,128)(2,1)} %bitcast.14, bf16[16,2,16,512]{3,2,1,0:T(8,128)(2,1)} %pages.1), custom_call_target="tpu_custom_call" | custom-call | bytes 589824 | tf_op jit(solution)/shard_map/send_kernel/pallas_call | solution.py:472
  2.9 0.0 copy-start.14
  2.9 0.0 copy-start.15
  2.9 0.0 copy-start.16
  2.9 0.0 copy-start.17
  2.9 0.0 copy-start.18
  2.9 0.0 copy-start.19
  2.9 0.0 copy-start.5
  3.0 7.3 %all-to-all-start = ((bf16[16,144,128]{2,1,0:T(8,128)(2,1)}), bf16[16,144,128]{2,1,0:T(8,128)(2,1)S(1)}, u32[]{:S(2)}, u32[]{:S(2)}) async-start(bf16[16,144,128]{2,1,0:T(8,128)(2,1)} %send_kernel.1), calls=%async_computation | async-start | bytes 1179648 | tf_op jit(solution)/shard_map/all_to_all | solution.py:485
  10.3 0.0 copy-start.11
  10.3 0.0 copy-start.12
  10.3 0.0 copy-start.13
  10.4 0.0 copy-done.14
  10.4 0.0 copy-done.15
  10.4 0.0 copy-done.16
  10.4 0.0 copy-done.17
  10.4 0.0 copy-done.18
  10.4 0.0 copy-done.19
  10.4 0.6 copy-done.11
  11.0 0.0 copy-done.12
  11.0 0.0 copy-done.13
  11.0 0.1 concatenate.3
  11.1 0.6 copy-done.7
  11.7 0.1 copy-done.6
  11.8 0.0 copy-done.8
  11.8 1.0 ready_kernel.1
  12.8 14.8 %all-to-all-done.recv = bf16[16,144,128]{2,1,0:T(8,128)(2,1)S(1)} async-done(((bf16[16,144,128]{2,1,0:T(8,128)(2,1)}), bf16[16,144,128]{2,1,0:T(8,128)(2,1)S(1)}, u32[]{:S(2)}, u32[]{:S(2)}) %all-to-all-start) | async-done | bytes 589856 | tf_op jit(solution)/shard_map/all_to_all | solution.py:485
  27.5 0.0 copy-done.2
  27.5 1.8 %tail_kernel.1 = bf16[16,4,640]{2,1,0:T(4,128)(2,1)} custom-call(bf16[16,144,128]{2,1,0:T(8,128)(2,1)S(1)} %all-to-all-done.recv, bf16[32,2,16,512]{3,2,1,0:T(8,128)(2,1)S(1)} %copy-done.2, f32[64,128]{1,0:T(8,128)S(1)} %get-tuple-element.21.distance), custom_call_target="tpu_custom_call" | custom-call | bytes 1753088 | tf_op jit(solution)/shard_map/tail_kernel/pallas_call | solution.py:472
  29.4 4.5 %all-to-all-start.1 = ((bf16[16,4,640]{2,1,0:T(4,128)(2,1)}), bf16[16,4,640]{2,1,0:T(4,128)(2,1)S(1)}, u32[]{:S(2)}, u32[]{:S(2)}) async-start(bf16[16,4,640]{2,1,0:T(4,128)(2,1)} %tail_kernel.1), calls=%async_computation.1 | async-start | bytes 163840 | tf_op jit(solution)/shard_map/all_to_all | solution.py:485
  33.9 0.1 copy.25
  34.1 1.4 %prefix_kernel.1 = (f32[64,640]{1,0:T(8,128)S(1)}, f32[8,8,256]{2,1,0:T(8,128)S(1)}, f32[8,8,192]{2,1,0:T(8,128)S(1)}) custom-call(bf16[64,1536]{1,0:T(8,128)(2,1)S(1)} %bitcast.9, bf16[16,144,128]{2,1,0:T(8,128)(2,1)S(1)} %all-to-all-done.recv, f32[64,256]{1,0:T(8,128)S(1)} %get-tuple-element.18.distance, f32[8,256]{1,0:T(8,128)S(1)} %get-tuple-element.19.vectors, ...), custom_call_target="tpu_custom_call" | custom-call | bytes 2973696 | tf_op jit(solution)/shard_map/prefix_kernel/pallas_call | solution.py:472
  35.6 6.5 %all-to-all-done.1.recv = bf16[16,4,640]{2,1,0:T(4,128)(2,1)S(1)} async-done(((bf16[16,4,640]{2,1,0:T(4,128)(2,1)}), bf16[16,4,640]{2,1,0:T(4,128)(2,1)S(1)}, u32[]{:S(2)}, u32[]{:S(2)}) %all-to-all-start.1) | async-done | bytes 81952 | tf_op jit(solution)/shard_map/all_to_all | solution.py:485
  42.0 0.5 join_kernel.1
  42.5 0.0 copy-start.4
  42.5 31.0 %all_to_all.40.recv = bf16[8,64,640]{2,1,0:T(8,128)(2,1)S(1)} all-to-all(bf16[8,64,640]{2,1,0:T(8,128)(2,1)S(1)} %join_kernel.1), channel_id=1, replica_groups=mesh['pages'=16,'row'=8,'col'=4] {'row'}, dimensions={0} | all-to-all | bytes 1310720 | tf_op jit(solution)/shard_map/all_to_all | solution.py:485
  73.6 0.7 out_kernel.1
  74.3 9.1 %all_to_all.41.recv = bf16[4,64,256]{2,1,0:T(8,128)(2,1)S(1)} all-to-all(bf16[4,64,256]{2,1,0:T(8,128)(2,1)S(1)} %out_kernel.1), channel_id=1, replica_groups=mesh['pages'=16,'row'=8,'col'=4] {'col'}, dimensions={0} | all-to-all | bytes 262144 | tf_op jit(solution)/shard_map/all_to_all | solution.py:485
  83.4 0.5 up_kernel.1
  83.9 0.0 copy-start.3
  83.9 13.3 %all_to_all.42.recv = bf16[8,72,256]{2,1,0:T(8,128)(2,1)S(1)} all-to-all(bf16[8,72,256]{2,1,0:T(8,128)(2,1)S(1)} %get-tuple-element.24), channel_id=1, replica_groups=mesh['pages'=16,'row'=8,'col'=4] {'row'}, dimensions={0} | all-to-all | bytes 589824 | tf_op jit(solution)/shard_map/all_to_all | solution.py:485
  97.3 0.7 hidden_kernel.1
  97.9 12.9 %all_to_all.43.recv = bf16[8,64,256]{2,1,0:T(8,128)(2,1)S(1)} all-to-all(bf16[8,64,256]{2,1,0:T(8,128)(2,1)S(1)} %hidden_kernel.1), channel_id=1, replica_groups=mesh['pages'=16,'row'=8,'col'=4] {'row'}, dimensions={0} | all-to-all | bytes 524288 | tf_op jit(solution)/shard_map/all_to_all | solution.py:485
  110.8 0.3 down_kernel.1
  111.1 8.4 %all_to_all.44.recv = bf16[4,64,256]{2,1,0:T(8,128)(2,1)S(1)} all-to-all(bf16[4,64,256]{2,1,0:T(8,128)(2,1)S(1)} %down_kernel.1), channel_id=1, replica_groups=mesh['pages'=16,'row'=8,'col'=4] {'col'}, dimensions={0} | all-to-all | bytes 262144 | tf_op jit(solution)/shard_map/all_to_all | solution.py:485
  119.5 0.8 next_kernel.1
  120.3 13.2 %all_to_all.45.recv = bf16[8,72,192]{2,1,0:T(8,128)(2,1)S(1)} all-to-all(bf16[8,72,192]{2,1,0:T(8,128)(2,1)S(1)} %get-tuple-element.28), channel_id=1, replica_groups=mesh['pages'=16,'row'=8,'col'=4] {'row'}, dimensions={0} | all-to-all | bytes 442368 | tf_op jit(solution)/shard_map/all_to_all | solution.py:485
  133.4 1.3 final_kernel.1
  (17 shorter events, 0.1 us)
Async XLA Ops:
  0.6 26.9 %copy-start.2 = (bf16[32,2,16,512]{3,2,1,0:T(8,128)(2,1)S(1)}, bf16[32,2,16,512]{3,2,1,0:T(8,128)(2,1)}, u32[]{:S(2)}) copy-start(bf16[32,2,16,512]{3,2,1,0:T(8,128)(2,1)} %tails.1) | copy-start | bytes 3145732
  2.9 7.5 %copy-start.14 = (bf16[256]{0:T(256)(128)(2,1)S(1)}, bf16[256]{0:T(256)(128)(2,1)}, u32[]{:S(2)}) copy-start(bf16[256]{0:T(256)(128)(2,1)} %param.38) | copy-start | bytes 1540
  2.9 7.5 %copy-start.15 = (bf16[256]{0:T(256)(128)(2,1)S(1)}, bf16[256]{0:T(256)(128)(2,1)}, u32[]{:S(2)}) copy-start(bf16[256]{0:T(256)(128)(2,1)} %param.39) | copy-start | bytes 1540
  2.9 7.5 %copy-start.16 = (bf16[256]{0:T(256)(128)(2,1)S(1)}, bf16[256]{0:T(256)(128)(2,1)}, u32[]{:S(2)}) copy-start(bf16[256]{0:T(256)(128)(2,1)} %param.34) | copy-start | bytes 1540
  2.9 7.5 %copy-start.17 = (bf16[192]{0:T(256)(128)(2,1)S(1)}, bf16[192]{0:T(256)(128)(2,1)}, u32[]{:S(2)}) copy-start(bf16[192]{0:T(256)(128)(2,1)} %param.41) | copy-start | bytes 1156
  2.9 7.5 %copy-start.18 = (bf16[64]{0:T(256)(128)(2,1)S(1)}, bf16[64]{0:T(256)(128)(2,1)}, u32[]{:S(2)}) copy-start(bf16[64]{0:T(256)(128)(2,1)} %param.30) | copy-start | bytes 388
  2.9 7.5 %copy-start.19 = (bf16[64]{0:T(256)(128)(2,1)S(1)}, bf16[64]{0:T(256)(128)(2,1)}, u32[]{:S(2)}) copy-start(bf16[64]{0:T(256)(128)(2,1)} %param.36) | copy-start | bytes 388
  2.9 8.2 %copy-start.5 = (bf16[32,2,64]{2,1,0:T(2,128)(2,1)S(1)}, bf16[32,2,64]{2,1,0:T(2,128)(2,1)}, u32[]{:S(2)}) copy-start(bf16[32,2,64]{2,1,0:T(2,128)(2,1)} %param.21) | copy-start | bytes 24580
  3.0 24.6 %all-to-all-start = ((bf16[16,144,128]{2,1,0:T(8,128)(2,1)}), bf16[16,144,128]{2,1,0:T(8,128)(2,1)S(1)}, u32[]{:S(2)}, u32[]{:S(2)}) async-start(bf16[16,144,128]{2,1,0:T(8,128)(2,1)} %send_kernel.1), calls=%async_computation | async-start | bytes 1179648 | tf_op jit(solution)/shard_map/all_to_all | solution.py:485
  10.3 0.7 copy-start.11
  10.3 0.7 copy-start.12
  10.3 0.7 copy-start.13
  11.0 0.7 copy-start.7
  11.1 0.7 copy-start.6
  11.1 0.7 copy-start.8
  11.1 0.7 copy-start.9
  27.5 6.4 %copy-start.10 = (bf16[32,2,3,512]{3,1,2,0:T(2,128)(2,1)S(1)}, bf16[32,2,3,512]{3,1,2,0:T(2,128)(2,1)}, u32[]{:S(2)}) copy-start(bf16[32,2,3,512]{3,1,2,0:T(2,128)(2,1)} %param.22) | copy-start | bytes 589828
  27.5 6.6 %copy-start = (bf16[256,2048]{1,0:T(8,128)(2,1)S(1)}, bf16[256,2048]{1,0:T(8,128)(2,1)}, u32[]{:S(2)}) copy-start(bf16[256,2048]{1,0:T(8,128)(2,1)} %weight.5) | copy-start | bytes 3145732
  29.4 4.7 %copy-start.1 = (bf16[256,1536]{1,0:T(8,128)(2,1)S(1)}, bf16[256,1536]{1,0:T(8,128)(2,1)}, u32[]{:S(2)}) copy-start(bf16[256,1536]{1,0:T(8,128)(2,1)} %weight.7) | copy-start | bytes 2359300
  29.4 12.7 %all-to-all-start.1 = ((bf16[16,4,640]{2,1,0:T(4,128)(2,1)}), bf16[16,4,640]{2,1,0:T(4,128)(2,1)S(1)}, u32[]{:S(2)}, u32[]{:S(2)}) async-start(bf16[16,4,640]{2,1,0:T(4,128)(2,1)} %tail_kernel.1), calls=%async_computation.1 | async-start | bytes 163840 | tf_op jit(solution)/shard_map/all_to_all | solution.py:485
  42.5 31.1 %copy-start.4 = (bf16[512,256]{1,0:T(8,128)(2,1)S(1)}, bf16[512,256]{1,0:T(8,128)(2,1)}, u32[]{:S(2)}) copy-start(bf16[512,256]{1,0:T(8,128)(2,1)} %weight.4) | copy-start | bytes 786436
  83.9 26.9 %copy-start.3 = (bf16[2048,256]{1,0:T(8,128)(2,1)S(1)}, bf16[2048,256]{1,0:T(8,128)(2,1)}, u32[]{:S(2)}) copy-start(bf16[2048,256]{1,0:T(8,128)(2,1)} %weight.6) | copy-start | bytes 3145732

commit v4 on v3

--- a/solution.py
+++ b/solution.py
@@ -224,6 +224,7 @@
     some = ROWS * 8 // TAILS
     blocks = ROWS // some
     stats = jnp.zeros((ROWS, 128), f32)
+    scores, weights = [], []
     for head in range(HEADS):
         at = slice(head * HD, (head + 1) * HD)
         q = query[head].astype(bf16)
@@ -231,16 +232,20 @@
         for n in range(blocks):
             k = tails[8 * n : 8 * n + 8, 0, :, at].reshape(8 * TOK, HD)
             parts.append(dot_t(q[n * some : (n + 1) * some], k))
-        scores = jnp.concatenate(parts, axis=0) * (1.0 / math.sqrt(HD))
-        scores = scores + slope_of(first_head + head) * distance
-        scores = jnp.where(usable, scores, masked_score)
-        m = rounded(jnp.max(scores, axis=1, keepdims=True))
-        weights = jnp.where(usable, jnp.exp(scores - m), 0.0)
-        stats = put_stats(stats, head, m, jnp.sum(weights, axis=1, keepdims=True))
-        weights = weights.astype(bf16)
+        scores.append(jnp.concatenate(parts, axis=0))
+    for head in range(HEADS):
+        biased = scores[head] * (1.0 / math.sqrt(HD)) + slope_of(first_head + head) * distance
+        biased = jnp.where(usable, biased, masked_score)
+        m = rounded(jnp.max(biased, axis=1, keepdims=True))
+        shares = jnp.where(usable, jnp.exp(biased - m), 0.0)
+        stats = put_stats(stats, head, m, jnp.sum(shares, axis=1, keepdims=True))
+        weights.append(shares.astype(bf16))
+    for head in range(HEADS):
+        at = slice(head * HD, (head + 1) * HD)
         for n in range(blocks):
             v = tails[8 * n : 8 * n + 8, 1, :, at].reshape(8 * TOK, HD)
-            wide[n * some : (n + 1) * some, at] = dot(weights[n * some : (n + 1) * some], v)
+            rows = slice(n * some, (n + 1) * some)
+            wide[rows, at] = dot(weights[head][rows], v)
     wide[:, WIDE:PACK] = stats
     for g in range(GROUPS):
         out[g] = wide[4 * g : 4 * g + 4].astype(bf16)
@@ -323,22 +328,34 @@
         out[n, :, WIDE:PACK] = stats
 
 
-def out_kernel(recv, weight, base, out, wide):
-    stats = [recv[n, :, WIDE:PACK].astype(f32) for n in range(NROW)]
-    for head in range(HEADS):
-        at = slice(head * HD, (head + 1) * HD)
-        parts = [get_stats(s, head) for s in stats]
-        m = parts[0][0]
-        for part in parts[1:]:
-            m = jnp.maximum(m, part[0])
-        total = jnp.zeros((ROWS, 1), f32)
-        attended = jnp.zeros((ROWS, HD), f32)
-        for n in range(NROW):
-            scale = jnp.exp(parts[n][0] - m)
-            total = total + scale * parts[n][1]
-            attended = attended + scale * recv[n, :, at].astype(f32)
-        wide[:, at] = (attended / total).astype(bf16)
-    partial = (dot(wide[...], weight[...]) + base[...]).astype(bf16)
+def columns_of(rows, other):
+    return lax.dot_general(
+        rows.astype(bf16), other.astype(bf16), (((0,), (0,)), ((), ())), preferred_element_type=f32
+    )
+
+
+def out_kernel(recv, weight, base, out):
+    row, lane = iota((16, 128), 0), iota((16, 128), 1)
+    head = (row & 7) * 4
+    first = jnp.where(row < 8, head, head + 1)
+    last = jnp.where(row < 8, head, head + 2)
+    chosen = one_hot((lane >= first) & (lane <= last) & ((row & 7) < HEADS))
+    tables = [dot_t(chosen, recv[n, :, WIDE:PACK]) for n in range(NROW)]
+    m = tables[0][0:8]
+    for table in tables[1:]:
+        m = jnp.maximum(m, table[0:8])
+    scales = [jnp.exp(table[0:8] - m) for table in tables]
+    total = scales[0] * tables[0][8:16]
+    for n in range(1, NROW):
+        total = total + scales[n] * tables[n][8:16]
+    spread = iota((16, WIDE), 0) & 7
+    spread = one_hot(spread == (iota((16, WIDE), 1) >> 7))
+    inverse = jnp.where(iota((8, ROWS), 0) < HEADS, 1.0 / total, 0.0)
+    attended = jnp.zeros((ROWS, WIDE), f32)
+    for n in range(NROW):
+        factor = jnp.concatenate(split(scales[n] * inverse), axis=0)
+        attended = attended + columns_of(factor, spread) * recv[n, :, 0:WIDE].astype(f32)
+    partial = (dot(attended.astype(bf16), weight[...]) + base[...]).astype(bf16)
     for n in range(NCOL):
         out[n] = partial
 
@@ -376,40 +393,41 @@
         out[n, ROWS : ROWS + 8] = jnp.where(edge < 4, extra[n], rows).astype(bf16)
 
 
-def as_columns(recv):
-    rows = jnp.concatenate([recv[n, ROWS : ROWS + 8, 0:ROWS].astype(f32) for n in range(NROW)], 0)
-    eye = one_hot(iota((ROWS, ROWS), 0) == iota((ROWS, ROWS), 1))
-    return dot_t(eye, rows.astype(bf16))
-
-
-def scale_of(means, spreads):
-    mean = sum(means) / NROW
-    spread = sum(spreads)
-    for part in means:
-        spread = spread + BLOCK * (part - mean) * (part - mean)
-    return mean, lax.rsqrt(spread / D + norm_eps)
-
-
-def projected(recv, width, bias, gain_at, shift_at, mean_at, spread_at):
-    columns = as_columns(recv)
-
-    def column(n, at):
-        return columns[:, 8 * n + at : 8 * n + at + 1] + columns[:, 8 * n + at + 1 : 8 * n + at + 2]
-
-    means = [column(n, mean_at) for n in range(NROW)]
-    mean, scale = scale_of(means, [column(n, spread_at) for n in range(NROW)])
-    total = jnp.zeros((ROWS, width), f32)
-    shifted = bias
+def projected(recv, bias, edges, gain_at, shift_at, mean_at, spread_at):
+    width = recv.shape[2]
     for n in range(NROW):
         edge = recv[n, ROWS : ROWS + 8].astype(f32)
-        gained = sum(edge[at : at + 1] for at in gain_at)
-        shifted = shifted + sum(edge[at : at + 1] for at in shift_at)
-        total = total + recv[n, 0:ROWS].astype(f32) + (means[n] - mean) * gained
-    return total * scale + shifted
-
-
-def hidden_kernel(recv, vectors, out):
-    v = projected(recv, BLOCK, vectors[4:5], (0, 1), (2, 3), 4, 6)
+        edges[0, 8 * n : 8 * n + 8] = edge[:, 0:128]
+        edges[1, 8 * n : 8 * n + 8, 0 : width - 128] = edge[:, 128:width]
+
+    def row(at):
+        halves = [edges[half, pl.ds(at, NROW, stride=8), :] for half in range(2)]
+        return jnp.concatenate(halves, axis=1)[:, 0:width]
+
+    means = (row(mean_at) + row(mean_at + 1))[:, 0:ROWS]
+    spreads = (row(spread_at) + row(spread_at + 1))[:, 0:ROWS]
+    away = means - jnp.mean(means, axis=0, keepdims=True)
+    spread = jnp.sum(spreads + BLOCK * away * away, axis=0, keepdims=True)
+    scale = lax.rsqrt(spread / D + norm_eps)
+    high, low = split(away)
+    gains = [row(at) for at in gain_at]
+    lefts = [high, low] if len(gains) == 1 else [high, low, high, low]
+    rights = [part for part in gains for _ in range(2)]
+    fixed = columns_of(jnp.concatenate(lefts, axis=0), jnp.concatenate(rights, axis=0))
+    shifted = bias + sum(jnp.sum(row(at), axis=0, keepdims=True) for at in shift_at)
+    high, rest = split(scale)
+    middle, low = split(rest)
+    at = iota((8, ROWS), 0)
+    parts = jnp.where(at == 0, high, jnp.where(at == 1, middle, jnp.where(at == 2, low, 0.0)))
+    scales = columns_of(parts, jnp.ones((8, width), f32))
+    total = recv[0, 0:ROWS].astype(f32)
+    for n in range(1, NROW):
+        total = total + recv[n, 0:ROWS].astype(f32)
+    return (total + fixed) * scales + shifted
+
+
+def hidden_kernel(recv, vectors, out, edges):
+    v = projected(recv, vectors[4:5], edges, (0, 1), (2, 3), 4, 6)
     v = 0.5 * v * (1.0 + jnp.tanh(math.sqrt(2.0 / math.pi) * (v + 0.044715 * (v * v * v))))
     v = v.astype(bf16)
     for n in range(NROW):
@@ -446,18 +464,16 @@
         out[n, ROWS : ROWS + 8] = jnp.where(edge < 2, extra[n], rows).astype(bf16)
 
 
-def final_kernel(recv, vectors, projected_next, score_out, wide):
+def final_kernel(recv, vectors, projected_next, score_out, wide, edges):
     width = projected_next.shape[2]
-    wide[...] = projected(recv, width, vectors[5:6, 0:width], (0,), (1,), 2, 4)
+    wide[...] = projected(recv, vectors[5:6, 0:width], edges, (0,), (1,), 2, 4)
     for i in range(ROWS // 2):
         projected_next[i] = wide[2 * i : 2 * i + 2].astype(bf16)
-    total = jnp.zeros((1, ROWS), f32)
-    for n in range(NROW):
-        edge = recv[n, ROWS : ROWS + 8, 0:ROWS].astype(f32)
-        total = total + edge[6:7] + edge[7:8]
+    scores = edges[0, pl.ds(6, NROW, stride=8), :] + edges[0, pl.ds(7, NROW, stride=8), :]
+    total = jnp.sum(scores, axis=0, keepdims=True)
     half = ROWS // 2
     score_out[0:1] = total[:, 0:half]
-    score_out[1:2] = total[:, half:]
+    score_out[1:2] = total[:, half:ROWS]
 
 
 def call(kernel, out, scalars, arrays, scratch=(), remote=(), limit=16, home=pltpu.VMEM):
@@ -592,7 +608,6 @@
         ((NCOL, ROWS, BLOCK), bf16),
         [],
         [joined, out_weight, base],
-        [pltpu.VMEM((ROWS, WIDE), bf16)],
     )
     partial = exchange(partial, "col")
     hidden_one, partial = call(
@@ -602,7 +617,13 @@
         [partial, vectors, up_rows, up_weight],
     )
     partial = exchange(partial, "row")
-    hidden_two = call(hidden_kernel, ((NROW, ROWS, BLOCK), bf16), [], [partial, vectors])
+    hidden_two = call(
+        hidden_kernel,
+        ((NROW, ROWS, BLOCK), bf16),
+        [],
+        [partial, vectors],
+        [pltpu.VMEM((2, ROWS, 128), f32)],
+    )
     hidden_two = exchange(hidden_two, "row")
     partial = call(
         down_kernel, ((NCOL, ROWS, BLOCK), bf16), [], [hidden_two, down_weight, vectors]
@@ -620,7 +641,7 @@
         [((cont_local, 2, width), bf16), ((2, cont_local), f32)],
         [],
         [partial, vectors],
-        [pltpu.VMEM((ROWS, width), f32)],
+        [pltpu.VMEM((ROWS, width), f32), pltpu.VMEM((2, ROWS, 128), f32)],
     )
     return (layer_out.reshape(cont_local, 2, share), score_sum.T, projected_next)
 

time: 135 us -> 134 us (level)
  Pallas kernels: 11.1 us -> 9.66 us
    pallas_call x11, Pallas kernels: 11.1 us -> 9.66 us  [call(): pl.pallas_call(kernel, out_shape=shapes if many else shapes[0], in_specs=...]
where the time goes in v4:
time: 134 us; the launch traced here: 133 us
  blocking collectives  87.9 us (66%)
  waiting for transfers between devices  21.2 us (16%)
  starting transfers between devices  11.9 us (9%)
  Pallas kernels  9.66 us (7%)
  local copies, waits for them, and re-layouts  1.6 us (1%)
    all_to_all x6, blocking collectives, exchange(): return lax.all_to_all(x, axis, split_axis=0, concat_axis=0, tiled=True)  87.9 us
    all_to_all x2, waiting for transfers between devices, exchange(): return lax.all_to_all(x, axis, split_axis=0, concat_axis=0, tiled=True)  21.2 us
    all_to_all x2, starting transfers between devices, exchange(): return lax.all_to_all(x, axis, split_axis=0, concat_axis=0, tiled=True)  11.9 us
    pallas_call x11, Pallas kernels, call(): pl.pallas_call(kernel, out_shape=shapes if many else shapes[0], in_specs=...  9.66 us
  transfers between devices with their start and end apart: 2, of which 2 were waited for; matrix products, arithmetic and copies ran while one was open for 0% of the time, Pallas kernels for 2%

profile of v4, /device:TPU:2, one launch (start us, length us, event | category | flops | bytes accessed | tf_op | source)
XLA Modules:
  0.0 133.3 jit_solution(2905142807945997030)
XLA Ops:
  0.6 2.2 %send_kernel.1 = bf16[16,144,128]{2,1,0:T(8,128)(2,1)} custom-call(s32[4,128]{1,0:T(4,128)} %bitcast.12, bf16[32,3,2,512]{3,2,1,0:T(2,128)(2,1)} %bitcast.14, bf16[16,2,16,512]{3,2,1,0:T(8,128)(2,1)} %pages.1), custom_call_target="tpu_custom_call" | custom-call | bytes 589824 | tf_op jit(solution)/shard_map/send_kernel/pallas_call | solution.py:488
  2.9 0.0 copy-start.14
  2.9 0.0 copy-start.15
  2.9 0.0 copy-start.16
  2.9 0.0 copy-start.17
  2.9 0.0 copy-start.18
  2.9 0.0 copy-start.19
  2.9 0.0 copy-start.5
  3.0 7.3 %all-to-all-start = ((bf16[16,144,128]{2,1,0:T(8,128)(2,1)}), bf16[16,144,128]{2,1,0:T(8,128)(2,1)S(1)}, u32[]{:S(2)}, u32[]{:S(2)}) async-start(bf16[16,144,128]{2,1,0:T(8,128)(2,1)} %send_kernel.1), calls=%async_computation | async-start | bytes 1179648 | tf_op jit(solution)/shard_map/all_to_all | solution.py:501
  10.3 0.0 copy-start.11
  10.3 0.0 copy-start.12
  10.3 0.0 copy-start.13
  10.4 0.0 copy-done.14
  10.4 0.0 copy-done.15
  10.4 0.0 copy-done.16
  10.4 0.0 copy-done.17
  10.4 0.0 copy-done.18
  10.4 0.0 copy-done.19
  10.4 0.6 copy-done.11
  11.0 0.0 copy-done.12
  11.0 0.0 copy-done.13
  11.0 0.1 concatenate.3
  11.1 0.6 copy-done.7
  11.7 0.1 copy-done.6
  11.8 0.0 copy-done.8
  11.8 1.0 ready_kernel.1
  12.8 14.8 %all-to-all-done.recv = bf16[16,144,128]{2,1,0:T(8,128)(2,1)S(1)} async-done(((bf16[16,144,128]{2,1,0:T(8,128)(2,1)}), bf16[16,144,128]{2,1,0:T(8,128)(2,1)S(1)}, u32[]{:S(2)}, u32[]{:S(2)}) %all-to-all-start) | async-done | bytes 589856 | tf_op jit(solution)/shard_map/all_to_all | solution.py:501
  27.5 0.0 copy-done.2
  27.5 1.2 tail_kernel.1
  28.8 4.5 %all-to-all-start.1 = ((bf16[16,4,640]{2,1,0:T(4,128)(2,1)}), bf16[16,4,640]{2,1,0:T(4,128)(2,1)S(1)}, u32[]{:S(2)}, u32[]{:S(2)}) async-start(bf16[16,4,640]{2,1,0:T(4,128)(2,1)} %tail_kernel.1), calls=%async_computation.1 | async-start | bytes 163840 | tf_op jit(solution)/shard_map/all_to_all | solution.py:501
  33.3 0.1 copy.25
  33.5 1.4 %prefix_kernel.1 = (f32[64,640]{1,0:T(8,128)S(1)}, f32[8,8,256]{2,1,0:T(8,128)S(1)}, f32[8,8,192]{2,1,0:T(8,128)S(1)}) custom-call(bf16[64,1536]{1,0:T(8,128)(2,1)S(1)} %bitcast.9, bf16[16,144,128]{2,1,0:T(8,128)(2,1)S(1)} %all-to-all-done.recv, f32[64,256]{1,0:T(8,128)S(1)} %get-tuple-element.18.distance, f32[8,256]{1,0:T(8,128)S(1)} %get-tuple-element.19.vectors, ...), custom_call_target="tpu_custom_call" | custom-call | bytes 2973696 | tf_op jit(solution)/shard_map/prefix_kernel/pallas_call | solution.py:488
  34.9 6.5 %all-to-all-done.1.recv = bf16[16,4,640]{2,1,0:T(4,128)(2,1)S(1)} async-done(((bf16[16,4,640]{2,1,0:T(4,128)(2,1)}), bf16[16,4,640]{2,1,0:T(4,128)(2,1)S(1)}, u32[]{:S(2)}, u32[]{:S(2)}) %all-to-all-start.1) | async-done | bytes 81952 | tf_op jit(solution)/shard_map/all_to_all | solution.py:501
  41.4 0.5 join_kernel.1
  41.9 0.0 copy-start.4
  41.9 31.0 %all_to_all.40.recv = bf16[8,64,640]{2,1,0:T(8,128)(2,1)S(1)} all-to-all(bf16[8,64,640]{2,1,0:T(8,128)(2,1)S(1)} %join_kernel.1), channel_id=1, replica_groups=mesh['pages'=16,'row'=8,'col'=4] {'row'}, dimensions={0} | all-to-all | bytes 1310720 | tf_op jit(solution)/shard_map/all_to_all | solution.py:501
  72.9 0.7 out_kernel.1
  73.6 9.1 %all_to_all.41.recv = bf16[4,64,256]{2,1,0:T(8,128)(2,1)S(1)} all-to-all(bf16[4,64,256]{2,1,0:T(8,128)(2,1)S(1)} %out_kernel.1), channel_id=1, replica_groups=mesh['pages'=16,'row'=8,'col'=4] {'col'}, dimensions={0} | all-to-all | bytes 262144 | tf_op jit(solution)/shard_map/all_to_all | solution.py:501
  82.7 0.5 up_kernel.1
  83.2 0.0 copy-start.3
  83.3 13.3 %all_to_all.42.recv = bf16[8,72,256]{2,1,0:T(8,128)(2,1)S(1)} all-to-all(bf16[8,72,256]{2,1,0:T(8,128)(2,1)S(1)} %get-tuple-element.24), channel_id=1, replica_groups=mesh['pages'=16,'row'=8,'col'=4] {'row'}, dimensions={0} | all-to-all | bytes 589824 | tf_op jit(solution)/shard_map/all_to_all | solution.py:501
  96.6 0.2 hidden_kernel.1
  96.9 12.9 %all_to_all.43.recv = bf16[8,64,256]{2,1,0:T(8,128)(2,1)S(1)} all-to-all(bf16[8,64,256]{2,1,0:T(8,128)(2,1)S(1)} %hidden_kernel.1), channel_id=1, replica_groups=mesh['pages'=16,'row'=8,'col'=4] {'row'}, dimensions={0} | all-to-all | bytes 524288 | tf_op jit(solution)/shard_map/all_to_all | solution.py:501
  109.7 0.3 down_kernel.1
  110.0 8.4 %all_to_all.44.recv = bf16[4,64,256]{2,1,0:T(8,128)(2,1)S(1)} all-to-all(bf16[4,64,256]{2,1,0:T(8,128)(2,1)S(1)} %down_kernel.1), channel_id=1, replica_groups=mesh['pages'=16,'row'=8,'col'=4] {'col'}, dimensions={0} | all-to-all | bytes 262144 | tf_op jit(solution)/shard_map/all_to_all | solution.py:501
  118.4 0.8 next_kernel.1
  119.2 13.2 %all_to_all.45.recv = bf16[8,72,192]{2,1,0:T(8,128)(2,1)S(1)} all-to-all(bf16[8,72,192]{2,1,0:T(8,128)(2,1)S(1)} %get-tuple-element.28), channel_id=1, replica_groups=mesh['pages'=16,'row'=8,'col'=4] {'row'}, dimensions={0} | all-to-all | bytes 442368 | tf_op jit(solution)/shard_map/all_to_all | solution.py:501
  132.4 0.9 final_kernel.1
  (17 shorter events, 0.1 us)
Async XLA Ops:
  0.6 26.9 %copy-start.2 = (bf16[32,2,16,512]{3,2,1,0:T(8,128)(2,1)S(1)}, bf16[32,2,16,512]{3,2,1,0:T(8,128)(2,1)}, u32[]{:S(2)}) copy-start(bf16[32,2,16,512]{3,2,1,0:T(8,128)(2,1)} %tails.1) | copy-start | bytes 3145732
  2.9 7.5 %copy-start.14 = (bf16[256]{0:T(256)(128)(2,1)S(1)}, bf16[256]{0:T(256)(128)(2,1)}, u32[]{:S(2)}) copy-start(bf16[256]{0:T(256)(128)(2,1)} %param.38) | copy-start | bytes 1540
  2.9 7.5 %copy-start.15 = (bf16[256]{0:T(256)(128)(2,1)S(1)}, bf16[256]{0:T(256)(128)(2,1)}, u32[]{:S(2)}) copy-start(bf16[256]{0:T(256)(128)(2,1)} %param.39) | copy-start | bytes 1540
  2.9 7.5 %copy-start.16 = (bf16[256]{0:T(256)(128)(2,1)S(1)}, bf16[256]{0:T(256)(128)(2,1)}, u32[]{:S(2)}) copy-start(bf16[256]{0:T(256)(128)(2,1)} %param.34) | copy-start | bytes 1540
  2.9 7.5 %copy-start.17 = (bf16[192]{0:T(256)(128)(2,1)S(1)}, bf16[192]{0:T(256)(128)(2,1)}, u32[]{:S(2)}) copy-start(bf16[192]{0:T(256)(128)(2,1)} %param.41) | copy-start | bytes 1156
  2.9 7.5 %copy-start.18 = (bf16[64]{0:T(256)(128)(2,1)S(1)}, bf16[64]{0:T(256)(128)(2,1)}, u32[]{:S(2)}) copy-start(bf16[64]{0:T(256)(128)(2,1)} %param.30) | copy-start | bytes 388
  2.9 7.5 %copy-start.19 = (bf16[64]{0:T(256)(128)(2,1)S(1)}, bf16[64]{0:T(256)(128)(2,1)}, u32[]{:S(2)}) copy-start(bf16[64]{0:T(256)(128)(2,1)} %param.36) | copy-start | bytes 388
  2.9 8.2 %copy-start.5 = (bf16[32,2,64]{2,1,0:T(2,128)(2,1)S(1)}, bf16[32,2,64]{2,1,0:T(2,128)(2,1)}, u32[]{:S(2)}) copy-start(bf16[32,2,64]{2,1,0:T(2,128)(2,1)} %param.21) | copy-start | bytes 24580
  3.0 24.6 %all-to-all-start = ((bf16[16,144,128]{2,1,0:T(8,128)(2,1)}), bf16[16,144,128]{2,1,0:T(8,128)(2,1)S(1)}, u32[]{:S(2)}, u32[]{:S(2)}) async-start(bf16[16,144,128]{2,1,0:T(8,128)(2,1)} %send_kernel.1), calls=%async_computation | async-start | bytes 1179648 | tf_op jit(solution)/shard_map/all_to_all | solution.py:501
  10.3 0.7 copy-start.11
  10.3 0.7 copy-start.12
  10.3 0.7 copy-start.13
  11.0 0.7 copy-start.7
  11.1 0.7 copy-start.6
  11.1 0.7 copy-start.8
  11.1 0.7 copy-start.9
  27.5 5.8 %copy-start.10 = (bf16[32,2,3,512]{3,1,2,0:T(2,128)(2,1)S(1)}, bf16[32,2,3,512]{3,1,2,0:T(2,128)(2,1)}, u32[]{:S(2)}) copy-start(bf16[32,2,3,512]{3,1,2,0:T(2,128)(2,1)} %param.22) | copy-start | bytes 589828
  27.5 6.0 %copy-start = (bf16[256,2048]{1,0:T(8,128)(2,1)S(1)}, bf16[256,2048]{1,0:T(8,128)(2,1)}, u32[]{:S(2)}) copy-start(bf16[256,2048]{1,0:T(8,128)(2,1)} %weight.5) | copy-start | bytes 3145732
  28.8 4.7 %copy-start.1 = (bf16[256,1536]{1,0:T(8,128)(2,1)S(1)}, bf16[256,1536]{1,0:T(8,128)(2,1)}, u32[]{:S(2)}) copy-start(bf16[256,1536]{1,0:T(8,128)(2,1)} %weight.7) | copy-start | bytes 2359300
  28.8 12.7 %all-to-all-start.1 = ((bf16[16,4,640]{2,1,0:T(4,128)(2,1)}), bf16[16,4,640]{2,1,0:T(4,128)(2,1)S(1)}, u32[]{:S(2)}, u32[]{:S(2)}) async-start(bf16[16,4,640]{2,1,0:T(4,128)(2,1)} %tail_kernel.1), calls=%async_computation.1 | async-start | bytes 163840 | tf_op jit(solution)/shard_map/all_to_all | solution.py:501
  41.9 31.1 %copy-start.4 = (bf16[512,256]{1,0:T(8,128)(2,1)S(1)}, bf16[512,256]{1,0:T(8,128)(2,1)}, u32[]{:S(2)}) copy-start(bf16[512,256]{1,0:T(8,128)(2,1)} %weight.4) | copy-start | bytes 786436
  83.2 26.5 %copy-start.3 = (bf16[2048,256]{1,0:T(8,128)(2,1)S(1)}, bf16[2048,256]{1,0:T(8,128)(2,1)}, u32[]{:S(2)}) copy-start(bf16[2048,256]{1,0:T(8,128)(2,1)} %weight.6) | copy-start | bytes 3145732

commit v5 on v4

--- a/solution.py
+++ b/solution.py
@@ -62,11 +62,6 @@
     stats = jnp.where(lane == head * 4, m, stats)
     stats = jnp.where(lane == head * 4 + 1, hi, stats)
     return jnp.where(lane == head * 4 + 2, l - hi, stats)
-
-
-def get_stats(stats, head):
-    at = head * 4
-    return stats[:, at : at + 1], stats[:, at + 1 : at + 2] + stats[:, at + 2 : at + 3]
 
 
 def send_kernel(tail_item, fresh, pages, out, items, query, wide, rows, stage, sems, out_sems):
@@ -305,56 +300,63 @@
     out[:, WIDE:PACK] = stats
 
 
+def columns_of(rows, other):
+    return lax.dot_general(
+        rows.astype(bf16), other.astype(bf16), (((0,), (0,)), ((), ())), preferred_element_type=f32
+    )
+
+
+def head_spread():
+    return one_hot((iota((16, WIDE), 0) & 7) == (iota((16, WIDE), 1) >> 7))
+
+
 def join_kernel(order, prefix, recv, out, wide):
     for h in range(GROUPS):
         wide[4 * h : 4 * h + 4] = recv[h].astype(f32)
-    tails = dot(order[...], wide[...].astype(bf16))
-    tail_stats = tails[:, WIDE:PACK]
-    prefix_stats = prefix[:, WIDE:PACK]
-    stats = jnp.zeros((ROWS, 128), f32)
-    for head in range(HEADS):
-        at = slice(head * HD, (head + 1) * HD)
-        left_m, left_l = get_stats(prefix_stats, head)
-        right_m, right_l = get_stats(tail_stats, head)
-        m = jnp.maximum(left_m, right_m)
-        left = jnp.exp(left_m - m)
-        right = jnp.exp(right_m - m)
-        stats = put_stats(stats, head, m, left * left_l + right * right_l)
-        joined = (left * prefix[:, at] + right * tails[:, at]).astype(bf16)
-        for n in range(NROW):
-            out[n, :, at] = joined
-    stats = stats.astype(bf16)
-    for n in range(NROW):
-        out[n, :, WIDE:PACK] = stats
-
-
-def columns_of(rows, other):
-    return lax.dot_general(
-        rows.astype(bf16), other.astype(bf16), (((0,), (0,)), ((), ())), preferred_element_type=f32
-    )
-
-
-def out_kernel(recv, weight, base, out):
     row, lane = iota((16, 128), 0), iota((16, 128), 1)
     head = (row & 7) * 4
     first = jnp.where(row < 8, head, head + 1)
     last = jnp.where(row < 8, head, head + 2)
     chosen = one_hot((lane >= first) & (lane <= last) & ((row & 7) < HEADS))
-    tables = [dot_t(chosen, recv[n, :, WIDE:PACK]) for n in range(NROW)]
-    m = tables[0][0:8]
-    for table in tables[1:]:
-        m = jnp.maximum(m, table[0:8])
-    scales = [jnp.exp(table[0:8] - m) for table in tables]
-    total = scales[0] * tables[0][8:16]
+    left = dot_t(chosen, prefix[:, WIDE:PACK].astype(bf16))
+    tails = dot(order[...], wide[...].astype(bf16))
+    right = dot_t(chosen, tails[:, WIDE:PACK].astype(bf16))
+    m = jnp.maximum(left[0:8], right[0:8])
+    left_scale = jnp.exp(left[0:8] - m)
+    right_scale = jnp.exp(right[0:8] - m)
+    total = split(left_scale * left[8:16] + right_scale * right[8:16])
+    spread = head_spread()
+    left_scale = columns_of(jnp.concatenate(split(left_scale), axis=0), spread)
+    right_scale = columns_of(jnp.concatenate(split(right_scale), axis=0), spread)
+    joined = (left_scale * prefix[:, 0:WIDE] + right_scale * tails[:, 0:WIDE]).astype(bf16)
+    blank = jnp.zeros((8, 128 - ROWS), f32)
+    parts = []
+    for part in (m,) + total:
+        parts = parts + [part, blank]
+    stats = jnp.concatenate(parts, axis=1).astype(bf16)
+    for n in range(NROW):
+        out[n, 0:ROWS] = joined
+        out[n, ROWS : ROWS + 8, 0:384] = stats
+        out[n, ROWS : ROWS + 8, 384:WIDE] = jnp.zeros((8, WIDE - 384), bf16)
+
+
+def out_kernel(recv, weight, base, out):
+    tables = [recv[n, ROWS : ROWS + 8, 0:384].astype(f32) for n in range(NROW)]
+    maxima = [table[:, 0:ROWS] for table in tables]
+    m = maxima[0]
+    for part in maxima[1:]:
+        m = jnp.maximum(m, part)
+    scales = [jnp.exp(part - m) for part in maxima]
+    sums = [table[:, 128 : 128 + ROWS] + table[:, 256 : 256 + ROWS] for table in tables]
+    total = scales[0] * sums[0]
     for n in range(1, NROW):
-        total = total + scales[n] * tables[n][8:16]
-    spread = iota((16, WIDE), 0) & 7
-    spread = one_hot(spread == (iota((16, WIDE), 1) >> 7))
+        total = total + scales[n] * sums[n]
+    spread = head_spread()
     inverse = jnp.where(iota((8, ROWS), 0) < HEADS, 1.0 / total, 0.0)
     attended = jnp.zeros((ROWS, WIDE), f32)
     for n in range(NROW):
         factor = jnp.concatenate(split(scales[n] * inverse), axis=0)
-        attended = attended + columns_of(factor, spread) * recv[n, :, 0:WIDE].astype(f32)
+        attended = attended + columns_of(factor, spread) * recv[n, 0:ROWS].astype(f32)
     partial = (dot(attended.astype(bf16), weight[...]) + base[...]).astype(bf16)
     for n in range(NCOL):
         out[n] = partial
@@ -597,7 +599,7 @@
     )
     joined = call(
         join_kernel,
-        ((NROW, ROWS, PACK), bf16),
+        ((NROW, ROWS + 8, WIDE), bf16),
         [],
         [order, prefix, tails],
         [pltpu.VMEM((ROWS, PACK), f32)],

time: 134 us -> 132 us (0.985)
  no operation moved by 1% of the time
where the time goes in v5:
time: 132 us
  blocking collectives  86.7 us (66%)
  waiting for transfers between devices  21.2 us (16%)
  starting transfers between devices  11.9 us (9%)
  Pallas kernels  9.57 us (7%)
  local copies, waits for them, and re-layouts  1.6 us (1%)
    all_to_all x6, blocking collectives, exchange(): return lax.all_to_all(x, axis, split_axis=0, concat_axis=0, tiled=True)  86.7 us
    all_to_all x2, waiting for transfers between devices, exchange(): return lax.all_to_all(x, axis, split_axis=0, concat_axis=0, tiled=True)  21.2 us
    all_to_all x2, starting transfers between devices, exchange(): return lax.all_to_all(x, axis, split_axis=0, concat_axis=0, tiled=True)  11.9 us
    pallas_call x11, Pallas kernels, call(): pl.pallas_call(kernel, out_shape=shapes if many else shapes[0], in_specs=...  9.57 us
  transfers between devices with their start and end apart: 2, of which 2 were waited for; matrix products, arithmetic and copies ran while one was open for 0% of the time, Pallas kernels for 2%

profile of v5, /device:TPU:2, one launch (start us, length us, event | category | flops | bytes accessed | tf_op | source)
XLA Modules:
  0.0 131.9 jit_solution(17085367777462443936)
XLA Ops:
  0.6 2.2 %send_kernel.1 = bf16[16,144,128]{2,1,0:T(8,128)(2,1)} custom-call(s32[4,128]{1,0:T(4,128)} %bitcast.12, bf16[32,3,2,512]{3,2,1,0:T(2,128)(2,1)} %bitcast.14, bf16[16,2,16,512]{3,2,1,0:T(8,128)(2,1)} %pages.1), custom_call_target="tpu_custom_call" | custom-call | bytes 589824 | tf_op jit(solution)/shard_map/send_kernel/pallas_call | solution.py:490
  2.9 0.0 copy-start.14
  2.9 0.0 copy-start.15
  2.9 0.0 copy-start.16
  2.9 0.0 copy-start.17
  2.9 0.0 copy-start.18
  2.9 0.0 copy-start.19
  2.9 0.0 copy-start.5
  3.0 7.3 %all-to-all-start = ((bf16[16,144,128]{2,1,0:T(8,128)(2,1)}), bf16[16,144,128]{2,1,0:T(8,128)(2,1)S(1)}, u32[]{:S(2)}, u32[]{:S(2)}) async-start(bf16[16,144,128]{2,1,0:T(8,128)(2,1)} %send_kernel.1), calls=%async_computation | async-start | bytes 1179648 | tf_op jit(solution)/shard_map/all_to_all | solution.py:503
  10.3 0.0 copy-start.11
  10.3 0.0 copy-start.12
  10.3 0.0 copy-start.13
  10.4 0.0 copy-done.14
  10.4 0.0 copy-done.15
  10.4 0.0 copy-done.16
  10.4 0.0 copy-done.17
  10.4 0.0 copy-done.18
  10.4 0.0 copy-done.19
  10.4 0.6 copy-done.11
  11.0 0.0 copy-done.12
  11.0 0.0 copy-done.13
  11.0 0.1 concatenate.3
  11.1 0.6 copy-done.7
  11.7 0.1 copy-done.6
  11.8 0.0 copy-done.8
  11.8 1.0 ready_kernel.1
  12.8 14.8 %all-to-all-done.recv = bf16[16,144,128]{2,1,0:T(8,128)(2,1)S(1)} async-done(((bf16[16,144,128]{2,1,0:T(8,128)(2,1)}), bf16[16,144,128]{2,1,0:T(8,128)(2,1)S(1)}, u32[]{:S(2)}, u32[]{:S(2)}) %all-to-all-start) | async-done | bytes 589856 | tf_op jit(solution)/shard_map/all_to_all | solution.py:503
  27.5 0.0 copy-done.2
  27.5 1.2 tail_kernel.1
  28.8 4.5 %all-to-all-start.1 = ((bf16[16,4,640]{2,1,0:T(4,128)(2,1)}), bf16[16,4,640]{2,1,0:T(4,128)(2,1)S(1)}, u32[]{:S(2)}, u32[]{:S(2)}) async-start(bf16[16,4,640]{2,1,0:T(4,128)(2,1)} %tail_kernel.1), calls=%async_computation.1 | async-start | bytes 163840 | tf_op jit(solution)/shard_map/all_to_all | solution.py:503
  33.3 0.1 copy.25
  33.5 1.4 %prefix_kernel.1 = (f32[64,640]{1,0:T(8,128)S(1)}, f32[8,8,256]{2,1,0:T(8,128)S(1)}, f32[8,8,192]{2,1,0:T(8,128)S(1)}) custom-call(bf16[64,1536]{1,0:T(8,128)(2,1)S(1)} %bitcast.9, bf16[16,144,128]{2,1,0:T(8,128)(2,1)S(1)} %all-to-all-done.recv, f32[64,256]{1,0:T(8,128)S(1)} %get-tuple-element.18.distance, f32[8,256]{1,0:T(8,128)S(1)} %get-tuple-element.19.vectors, ...), custom_call_target="tpu_custom_call" | custom-call | bytes 2973696 | tf_op jit(solution)/shard_map/prefix_kernel/pallas_call | solution.py:490
  34.9 6.5 %all-to-all-done.1.recv = bf16[16,4,640]{2,1,0:T(4,128)(2,1)S(1)} async-done(((bf16[16,4,640]{2,1,0:T(4,128)(2,1)}), bf16[16,4,640]{2,1,0:T(4,128)(2,1)S(1)}, u32[]{:S(2)}, u32[]{:S(2)}) %all-to-all-start.1) | async-done | bytes 81952 | tf_op jit(solution)/shard_map/all_to_all | solution.py:503
  41.4 0.5 join_kernel.1
  42.0 0.0 copy-start.4
  42.0 29.6 %all_to_all.40.recv = bf16[8,72,512]{2,1,0:T(8,128)(2,1)S(1)} all-to-all(bf16[8,72,512]{2,1,0:T(8,128)(2,1)S(1)} %join_kernel.1), channel_id=1, replica_groups=mesh['pages'=16,'row'=8,'col'=4] {'row'}, dimensions={0} | all-to-all | bytes 1179648 | tf_op jit(solution)/shard_map/all_to_all | solution.py:503
  71.6 0.5 out_kernel.1
  72.1 9.1 %all_to_all.41.recv = bf16[4,64,256]{2,1,0:T(8,128)(2,1)S(1)} all-to-all(bf16[4,64,256]{2,1,0:T(8,128)(2,1)S(1)} %out_kernel.1), channel_id=1, replica_groups=mesh['pages'=16,'row'=8,'col'=4] {'col'}, dimensions={0} | all-to-all | bytes 262144 | tf_op jit(solution)/shard_map/all_to_all | solution.py:503
  81.2 0.5 up_kernel.1
  81.8 0.0 copy-start.3
  81.8 13.5 %all_to_all.42.recv = bf16[8,72,256]{2,1,0:T(8,128)(2,1)S(1)} all-to-all(bf16[8,72,256]{2,1,0:T(8,128)(2,1)S(1)} %get-tuple-element.24), channel_id=1, replica_groups=mesh['pages'=16,'row'=8,'col'=4] {'row'}, dimensions={0} | all-to-all | bytes 589824 | tf_op jit(solution)/shard_map/all_to_all | solution.py:503
  95.2 0.2 hidden_kernel.1
  95.5 12.9 %all_to_all.43.recv = bf16[8,64,256]{2,1,0:T(8,128)(2,1)S(1)} all-to-all(bf16[8,64,256]{2,1,0:T(8,128)(2,1)S(1)} %hidden_kernel.1), channel_id=1, replica_groups=mesh['pages'=16,'row'=8,'col'=4] {'row'}, dimensions={0} | all-to-all | bytes 524288 | tf_op jit(solution)/shard_map/all_to_all | solution.py:503
  108.4 0.3 down_kernel.1
  108.7 8.4 %all_to_all.44.recv = bf16[4,64,256]{2,1,0:T(8,128)(2,1)S(1)} all-to-all(bf16[4,64,256]{2,1,0:T(8,128)(2,1)S(1)} %down_kernel.1), channel_id=1, replica_groups=mesh['pages'=16,'row'=8,'col'=4] {'col'}, dimensions={0} | all-to-all | bytes 262144 | tf_op jit(solution)/shard_map/all_to_all | solution.py:503
  117.0 0.8 next_kernel.1
  117.8 13.2 %all_to_all.45.recv = bf16[8,72,192]{2,1,0:T(8,128)(2,1)S(1)} all-to-all(bf16[8,72,192]{2,1,0:T(8,128)(2,1)S(1)} %get-tuple-element.28), channel_id=1, replica_groups=mesh['pages'=16,'row'=8,'col'=4] {'row'}, dimensions={0} | all-to-all | bytes 442368 | tf_op jit(solution)/shard_map/all_to_all | solution.py:503
  131.0 0.9 final_kernel.1
  (17 shorter events, 0.1 us)
Async XLA Ops:
  0.6 26.9 %copy-start.2 = (bf16[32,2,16,512]{3,2,1,0:T(8,128)(2,1)S(1)}, bf16[32,2,16,512]{3,2,1,0:T(8,128)(2,1)}, u32[]{:S(2)}) copy-start(bf16[32,2,16,512]{3,2,1,0:T(8,128)(2,1)} %tails.1) | copy-start | bytes 3145732
  2.9 7.5 %copy-start.14 = (bf16[256]{0:T(256)(128)(2,1)S(1)}, bf16[256]{0:T(256)(128)(2,1)}, u32[]{:S(2)}) copy-start(bf16[256]{0:T(256)(128)(2,1)} %param.38) | copy-start | bytes 1540
  2.9 7.5 %copy-start.15 = (bf16[256]{0:T(256)(128)(2,1)S(1)}, bf16[256]{0:T(256)(128)(2,1)}, u32[]{:S(2)}) copy-start(bf16[256]{0:T(256)(128)(2,1)} %param.39) | copy-start | bytes 1540
  2.9 7.5 %copy-start.16 = (bf16[256]{0:T(256)(128)(2,1)S(1)}, bf16[256]{0:T(256)(128)(2,1)}, u32[]{:S(2)}) copy-start(bf16[256]{0:T(256)(128)(2,1)} %param.34) | copy-start | bytes 1540
  2.9 7.5 %copy-start.17 = (bf16[192]{0:T(256)(128)(2,1)S(1)}, bf16[192]{0:T(256)(128)(2,1)}, u32[]{:S(2)}) copy-start(bf16[192]{0:T(256)(128)(2,1)} %param.41) | copy-start | bytes 1156
  2.9 7.5 %copy-start.18 = (bf16[64]{0:T(256)(128)(2,1)S(1)}, bf16[64]{0:T(256)(128)(2,1)}, u32[]{:S(2)}) copy-start(bf16[64]{0:T(256)(128)(2,1)} %param.30) | copy-start | bytes 388
  2.9 7.5 %copy-start.19 = (bf16[64]{0:T(256)(128)(2,1)S(1)}, bf16[64]{0:T(256)(128)(2,1)}, u32[]{:S(2)}) copy-start(bf16[64]{0:T(256)(128)(2,1)} %param.36) | copy-start | bytes 388
  2.9 8.2 %copy-start.5 = (bf16[32,2,64]{2,1,0:T(2,128)(2,1)S(1)}, bf16[32,2,64]{2,1,0:T(2,128)(2,1)}, u32[]{:S(2)}) copy-start(bf16[32,2,64]{2,1,0:T(2,128)(2,1)} %param.21) | copy-start | bytes 24580
  3.0 24.6 %all-to-all-start = ((bf16[16,144,128]{2,1,0:T(8,128)(2,1)}), bf16[16,144,128]{2,1,0:T(8,128)(2,1)S(1)}, u32[]{:S(2)}, u32[]{:S(2)}) async-start(bf16[16,144,128]{2,1,0:T(8,128)(2,1)} %send_kernel.1), calls=%async_computation | async-start | bytes 1179648 | tf_op jit(solution)/shard_map/all_to_all | solution.py:503
  10.3 0.7 copy-start.11
  10.3 0.7 copy-start.12
  10.3 0.7 copy-start.13
  11.0 0.7 copy-start.7
  11.1 0.7 copy-start.6
  11.1 0.7 copy-start.8
  11.1 0.7 copy-start.9
  27.5 5.8 %copy-start.10 = (bf16[32,2,3,512]{3,1,2,0:T(2,128)(2,1)S(1)}, bf16[32,2,3,512]{3,1,2,0:T(2,128)(2,1)}, u32[]{:S(2)}) copy-start(bf16[32,2,3,512]{3,1,2,0:T(2,128)(2,1)} %param.22) | copy-start | bytes 589828
  27.5 6.0 %copy-start = (bf16[256,2048]{1,0:T(8,128)(2,1)S(1)}, bf16[256,2048]{1,0:T(8,128)(2,1)}, u32[]{:S(2)}) copy-start(bf16[256,2048]{1,0:T(8,128)(2,1)} %weight.5) | copy-start | bytes 3145732
  28.8 4.7 %copy-start.1 = (bf16[256,1536]{1,0:T(8,128)(2,1)S(1)}, bf16[256,1536]{1,0:T(8,128)(2,1)}, u32[]{:S(2)}) copy-start(bf16[256,1536]{1,0:T(8,128)(2,1)} %weight.7) | copy-start | bytes 2359300
  28.8 12.7 %all-to-all-start.1 = ((bf16[16,4,640]{2,1,0:T(4,128)(2,1)}), bf16[16,4,640]{2,1,0:T(4,128)(2,1)S(1)}, u32[]{:S(2)}, u32[]{:S(2)}) async-start(bf16[16,4,640]{2,1,0:T(4,128)(2,1)} %tail_kernel.1), calls=%async_computation.1 | async-start | bytes 163840 | tf_op jit(solution)/shard_map/all_to_all | solution.py:503
  42.0 29.6 %copy-start.4 = (bf16[512,256]{1,0:T(8,128)(2,1)S(1)}, bf16[512,256]{1,0:T(8,128)(2,1)}, u32[]{:S(2)}) copy-start(bf16[512,256]{1,0:T(8,128)(2,1)} %weight.4) | copy-start | bytes 786436
  81.8 26.6 %copy-start.3 = (bf16[2048,256]{1,0:T(8,128)(2,1)S(1)}, bf16[2048,256]{1,0:T(8,128)(2,1)}, u32[]{:S(2)}) copy-start(bf16[2048,256]{1,0:T(8,128)(2,1)} %weight.6) | copy-start | bytes 3145732

commit v6 on v5

--- a/solution.py
+++ b/solution.py
@@ -258,9 +258,14 @@
             rows = jnp.where(edge == at, values, rows)
         up_rows[n] = rows
     both = gain_rows(vectors[1:2], vectors[7:8])
-    width = qkv_rows.shape[2]
-    for n in range(NROW):
-        qkv_rows[n] = dot(both, qkv_weight[:, n * width : (n + 1) * width])[0:8]
+    width = qkv_weight.shape[1] // NROW
+    edge, blank = iota((8, 128), 0), jnp.zeros((8, 64), f32)
+    for n in range(NROW):
+        parts = dot(both, qkv_weight[:, n * width : (n + 1) * width])[0:8]
+        rest = jnp.concatenate([blank, parts[:, 128:width]], axis=1)
+        rows = jnp.where(edge < 2, parts[:, 0:128], 0.0)
+        rows = jnp.where(edge == 2, rest[0:1], rows)
+        qkv_rows[n] = jnp.where(edge == 3, rest[1:2], rows)
 
     distance = distance[...]
     usable = distance > 0.5 * masked_score
@@ -395,41 +400,45 @@
         out[n, ROWS : ROWS + 8] = jnp.where(edge < 4, extra[n], rows).astype(bf16)
 
 
-def projected(recv, bias, edges, gain_at, shift_at, mean_at, spread_at):
-    width = recv.shape[2]
-    for n in range(NROW):
-        edge = recv[n, ROWS : ROWS + 8].astype(f32)
-        edges[0, 8 * n : 8 * n + 8] = edge[:, 0:128]
-        edges[1, 8 * n : 8 * n + 8, 0 : width - 128] = edge[:, 128:width]
-
-    def row(at):
-        halves = [edges[half, pl.ds(at, NROW, stride=8), :] for half in range(2)]
-        return jnp.concatenate(halves, axis=1)[:, 0:width]
-
-    means = (row(mean_at) + row(mean_at + 1))[:, 0:ROWS]
-    spreads = (row(spread_at) + row(spread_at + 1))[:, 0:ROWS]
+def normed(total, bias, gains, shifts, means, spreads):
+    width = total.shape[1]
     away = means - jnp.mean(means, axis=0, keepdims=True)
     spread = jnp.sum(spreads + BLOCK * away * away, axis=0, keepdims=True)
     scale = lax.rsqrt(spread / D + norm_eps)
     high, low = split(away)
-    gains = [row(at) for at in gain_at]
-    lefts = [high, low] if len(gains) == 1 else [high, low, high, low]
+    lefts = [high, low] * len(gains)
     rights = [part for part in gains for _ in range(2)]
     fixed = columns_of(jnp.concatenate(lefts, axis=0), jnp.concatenate(rights, axis=0))
-    shifted = bias + sum(jnp.sum(row(at), axis=0, keepdims=True) for at in shift_at)
+    shifted = bias + sum(jnp.sum(part, axis=0, keepdims=True) for part in shifts)
     high, rest = split(scale)
     middle, low = split(rest)
     at = iota((8, ROWS), 0)
     parts = jnp.where(at == 0, high, jnp.where(at == 1, middle, jnp.where(at == 2, low, 0.0)))
     scales = columns_of(parts, jnp.ones((8, width), f32))
-    total = recv[0, 0:ROWS].astype(f32)
+    return (total + fixed) * scales + shifted
+
+
+def summed(recv, first, last):
+    total = recv[0, first:last].astype(f32)
     for n in range(1, NROW):
-        total = total + recv[n, 0:ROWS].astype(f32)
-    return (total + fixed) * scales + shifted
+        total = total + recv[n, first:last].astype(f32)
+    return total
 
 
 def hidden_kernel(recv, vectors, out, edges):
-    v = projected(recv, vectors[4:5], edges, (0, 1), (2, 3), 4, 6)
+    for n in range(NROW):
+        edge = recv[n, ROWS : ROWS + 8].astype(f32)
+        edges[0, 8 * n : 8 * n + 8] = edge[:, 0:128]
+        edges[1, 8 * n : 8 * n + 8] = edge[:, 128:BLOCK]
+
+    def row(at):
+        halves = [edges[half, pl.ds(at, NROW, stride=8), :] for half in range(2)]
+        return jnp.concatenate(halves, axis=1)
+
+    means = (row(4) + row(5))[:, 0:ROWS]
+    spreads = (row(6) + row(7))[:, 0:ROWS]
+    total = summed(recv, 0, ROWS)
+    v = normed(total, vectors[4:5], [row(0), row(1)], [row(2), row(3)], means, spreads)
     v = 0.5 * v * (1.0 + jnp.tanh(math.sqrt(2.0 / math.pi) * (v + 0.044715 * (v * v * v))))
     v = v.astype(bf16)
     for n in range(NROW):
@@ -458,22 +467,39 @@
     by_step = ((lane & 31) << 1) + (lane >> 5)
     rows = as_rows(list(zip((2, 3, 4, 5), split(mean) + split(spread))))
     rows = rows + as_rows(list(zip((6, 7), split(scores))), by_step)
-    width = out.shape[2]
-    rows = jnp.concatenate([rows, jnp.zeros((8, width - ROWS), f32)], axis=1)
-    edge = iota((8, width), 0)
-    for n in range(NROW):
-        out[n, 0:ROWS] = dot(scaled, weight[:, n * width : (n + 1) * width]).astype(bf16)
-        out[n, ROWS : ROWS + 8] = jnp.where(edge < 2, extra[n], rows).astype(bf16)
+    width = weight.shape[1] // NROW
+    half = ROWS // 2
+    rows = jnp.concatenate([rows, jnp.zeros((8, 128 - ROWS), f32)], axis=1)
+    for n in range(NROW):
+        part = dot(scaled, weight[:, n * width : (n + 1) * width])
+        rest = part[:, 128:width]
+        rest = jnp.concatenate([rest[0:half], rest[half:ROWS]], axis=1)
+        out[n, 0:ROWS] = part[:, 0:128].astype(bf16)
+        out[n, ROWS : ROWS + half] = rest.astype(bf16)
+        out[n, ROWS + half : ROWS + half + 8] = (extra[n] + rows).astype(bf16)
 
 
 def final_kernel(recv, vectors, projected_next, score_out, wide, edges):
     width = projected_next.shape[2]
-    wide[...] = projected(recv, vectors[5:6, 0:width], edges, (0,), (1,), 2, 4)
+    half = ROWS // 2
+    for n in range(NROW):
+        edges[8 * n : 8 * n + 8] = recv[n, ROWS + half : ROWS + half + 8].astype(f32)
+
+    def row(at):
+        return edges[pl.ds(at, NROW, stride=8), :]
+
+    second, third = row(2), row(3)
+    gain = jnp.concatenate([row(0), second[:, 64:128]], axis=1)
+    shift = jnp.concatenate([row(1), third[:, 64:128]], axis=1)
+    means = (second + third)[:, 0:ROWS]
+    spreads = (row(4) + row(5))[:, 0:ROWS]
+    rest = summed(recv, ROWS, ROWS + half)
+    rest = jnp.concatenate([rest[:, 0:64], rest[:, 64:128]], axis=0)
+    total = jnp.concatenate([summed(recv, 0, ROWS), rest], axis=1)
+    wide[...] = normed(total, vectors[5:6, 0:width], [gain], [shift], means, spreads)
     for i in range(ROWS // 2):
         projected_next[i] = wide[2 * i : 2 * i + 2].astype(bf16)
-    scores = edges[0, pl.ds(6, NROW, stride=8), :] + edges[0, pl.ds(7, NROW, stride=8), :]
-    total = jnp.sum(scores, axis=0, keepdims=True)
-    half = ROWS // 2
+    total = jnp.sum(row(6) + row(7), axis=0, keepdims=True)
     score_out[0:1] = total[:, 0:half]
     score_out[1:2] = total[:, half:ROWS]
 
@@ -586,7 +612,7 @@
     tails = exchange(tails, "pages")
     prefix, up_rows, qkv_rows = call(
         prefix_kernel,
-        [((ROWS, PACK), f32), ((NROW, 8, BLOCK), f32), ((NROW, 8, width), f32)],
+        [((ROWS, PACK), f32), ((NROW, 8, BLOCK), f32), ((NROW, 8, 128), f32)],
         [],
         [
             fresh_qkv.reshape(ROWS, 3 * WIDE),
@@ -633,7 +659,7 @@
     partial = exchange(partial, "col")
     layer_out, partial = call(
         next_kernel,
-        [((ROWS, share), bf16), ((NROW, ROWS + 8, width), bf16)],
+        [((ROWS, share), bf16), ((NROW, ROWS + ROWS // 2 + 8, 128), bf16)],
         [],
         [partial, hidden_one, vectors, qkv_rows, qkv_weight],
     )
@@ -643,7 +669,7 @@
         [((cont_local, 2, width), bf16), ((2, cont_local), f32)],
         [],
         [partial, vectors],
-        [pltpu.VMEM((ROWS, width), f32), pltpu.VMEM((2, ROWS, 128), f32)],
+        [pltpu.VMEM((ROWS, width), f32), pltpu.VMEM((ROWS, 128), f32)],
     )
     return (layer_out.reshape(cont_local, 2, share), score_sum.T, projected_next)
 

time: 132 us -> 132 us (level)
  no operation moved by 1% of the time
where the time goes in v6:
time: 132 us; the launch traced here: 131 us
  blocking collectives  85.8 us (65%)
  waiting for transfers between devices  21.2 us (16%)
  starting transfers between devices  11.9 us (9%)
  Pallas kernels  9.57 us (7%)
  local copies, waits for them, and re-layouts  1.6 us (1%)
    all_to_all x6, blocking collectives, exchange(): return lax.all_to_all(x, axis, split_axis=0, concat_axis=0, tiled=True)  85.8 us
    all_to_all x2, waiting for transfers between devices, exchange(): return lax.all_to_all(x, axis, split_axis=0, concat_axis=0, tiled=True)  21.2 us
    all_to_all x2, starting transfers between devices, exchange(): return lax.all_to_all(x, axis, split_axis=0, concat_axis=0, tiled=True)  11.9 us
    pallas_call x11, Pallas kernels, call(): pl.pallas_call(kernel, out_shape=shapes if many else shapes[0], in_specs=...  9.57 us
  transfers between devices with their start and end apart: 2, of which 2 were waited for; matrix products, arithmetic and copies ran while one was open for 0% of the time, Pallas kernels for 2%

profile of v6, /device:TPU:2, one launch (start us, length us, event | category | flops | bytes accessed | tf_op | source)
XLA Modules:
  0.0 131.0 jit_solution(7922343834255541542)
XLA Ops:
  0.6 2.2 %send_kernel.1 = bf16[16,144,128]{2,1,0:T(8,128)(2,1)} custom-call(s32[4,128]{1,0:T(4,128)} %bitcast.12, bf16[32,3,2,512]{3,2,1,0:T(2,128)(2,1)} %bitcast.14, bf16[16,2,16,512]{3,2,1,0:T(8,128)(2,1)} %pages.1), custom_call_target="tpu_custom_call" | custom-call | bytes 589824 | tf_op jit(solution)/shard_map/send_kernel/pallas_call | solution.py:516
  2.9 0.0 copy-start.14
  2.9 0.0 copy-start.15
  2.9 0.0 copy-start.16
  2.9 0.0 copy-start.17
  2.9 0.0 copy-start.18
  2.9 0.0 copy-start.19
  2.9 0.0 copy-start.5
  3.0 7.3 %all-to-all-start = ((bf16[16,144,128]{2,1,0:T(8,128)(2,1)}), bf16[16,144,128]{2,1,0:T(8,128)(2,1)S(1)}, u32[]{:S(2)}, u32[]{:S(2)}) async-start(bf16[16,144,128]{2,1,0:T(8,128)(2,1)} %send_kernel.1), calls=%async_computation | async-start | bytes 1179648 | tf_op jit(solution)/shard_map/all_to_all | solution.py:529
  10.3 0.0 copy-start.11
  10.3 0.0 copy-start.12
  10.3 0.0 copy-start.13
  10.4 0.0 copy-done.14
  10.4 0.0 copy-done.15
  10.4 0.0 copy-done.16
  10.4 0.0 copy-done.17
  10.4 0.0 copy-done.18
  10.4 0.0 copy-done.19
  10.4 0.6 copy-done.11
  11.0 0.0 copy-done.12
  11.0 0.0 copy-done.13
  11.0 0.1 concatenate.3
  11.1 0.6 copy-done.7
  11.7 0.1 copy-done.6
  11.8 0.0 copy-done.8
  11.8 1.0 ready_kernel.1
  12.8 14.8 %all-to-all-done.recv = bf16[16,144,128]{2,1,0:T(8,128)(2,1)S(1)} async-done(((bf16[16,144,128]{2,1,0:T(8,128)(2,1)}), bf16[16,144,128]{2,1,0:T(8,128)(2,1)S(1)}, u32[]{:S(2)}, u32[]{:S(2)}) %all-to-all-start) | async-done | bytes 589856 | tf_op jit(solution)/shard_map/all_to_all | solution.py:529
  27.5 0.0 copy-done.2
  27.5 1.2 tail_kernel.1
  28.8 4.5 %all-to-all-start.1 = ((bf16[16,4,640]{2,1,0:T(4,128)(2,1)}), bf16[16,4,640]{2,1,0:T(4,128)(2,1)S(1)}, u32[]{:S(2)}, u32[]{:S(2)}) async-start(bf16[16,4,640]{2,1,0:T(4,128)(2,1)} %tail_kernel.1), calls=%async_computation.1 | async-start | bytes 163840 | tf_op jit(solution)/shard_map/all_to_all | solution.py:529
  33.3 0.1 copy.25
  33.5 1.4 %prefix_kernel.1 = (f32[64,640]{1,0:T(8,128)S(1)}, f32[8,8,256]{2,1,0:T(8,128)S(1)}, f32[8,8,128]{2,1,0:T(8,128)S(1)}) custom-call(bf16[64,1536]{1,0:T(8,128)(2,1)S(1)} %bitcast.9, bf16[16,144,128]{2,1,0:T(8,128)(2,1)S(1)} %all-to-all-done.recv, f32[64,256]{1,0:T(8,128)S(1)} %get-tuple-element.18.distance, f32[8,256]{1,0:T(8,128)S(1)} %get-tuple-element.19.vectors, ...), custom_call_target="tpu_custom_call" | custom-call | bytes 2957312 | tf_op jit(solution)/shard_map/prefix_kernel/pallas_call | solution.py:516
  34.9 6.5 %all-to-all-done.1.recv = bf16[16,4,640]{2,1,0:T(4,128)(2,1)S(1)} async-done(((bf16[16,4,640]{2,1,0:T(4,128)(2,1)}), bf16[16,4,640]{2,1,0:T(4,128)(2,1)S(1)}, u32[]{:S(2)}, u32[]{:S(2)}) %all-to-all-start.1) | async-done | bytes 81952 | tf_op jit(solution)/shard_map/all_to_all | solution.py:529
  41.4 0.5 join_kernel.1
  42.0 0.0 copy-start.4
  42.0 29.6 %all_to_all.40.recv = bf16[8,72,512]{2,1,0:T(8,128)(2,1)S(1)} all-to-all(bf16[8,72,512]{2,1,0:T(8,128)(2,1)S(1)} %join_kernel.1), channel_id=1, replica_groups=mesh['pages'=16,'row'=8,'col'=4] {'row'}, dimensions={0} | all-to-all | bytes 1179648 | tf_op jit(solution)/shard_map/all_to_all | solution.py:529
  71.6 0.5 out_kernel.1
  72.1 9.1 %all_to_all.41.recv = bf16[4,64,256]{2,1,0:T(8,128)(2,1)S(1)} all-to-all(bf16[4,64,256]{2,1,0:T(8,128)(2,1)S(1)} %out_kernel.1), channel_id=1, replica_groups=mesh['pages'=16,'row'=8,'col'=4] {'col'}, dimensions={0} | all-to-all | bytes 262144 | tf_op jit(solution)/shard_map/all_to_all | solution.py:529
  81.2 0.5 up_kernel.1
  81.8 0.0 copy-start.3
  81.8 13.5 %all_to_all.42.recv = bf16[8,72,256]{2,1,0:T(8,128)(2,1)S(1)} all-to-all(bf16[8,72,256]{2,1,0:T(8,128)(2,1)S(1)} %get-tuple-element.24), channel_id=1, replica_groups=mesh['pages'=16,'row'=8,'col'=4] {'row'}, dimensions={0} | all-to-all | bytes 589824 | tf_op jit(solution)/shard_map/all_to_all | solution.py:529
  95.2 0.2 hidden_kernel.1
  95.5 12.9 %all_to_all.43.recv = bf16[8,64,256]{2,1,0:T(8,128)(2,1)S(1)} all-to-all(bf16[8,64,256]{2,1,0:T(8,128)(2,1)S(1)} %hidden_kernel.1), channel_id=1, replica_groups=mesh['pages'=16,'row'=8,'col'=4] {'row'}, dimensions={0} | all-to-all | bytes 524288 | tf_op jit(solution)/shard_map/all_to_all | solution.py:529
  108.4 0.3 down_kernel.1
  108.7 8.4 %all_to_all.44.recv = bf16[4,64,256]{2,1,0:T(8,128)(2,1)S(1)} all-to-all(bf16[4,64,256]{2,1,0:T(8,128)(2,1)S(1)} %down_kernel.1), channel_id=1, replica_groups=mesh['pages'=16,'row'=8,'col'=4] {'col'}, dimensions={0} | all-to-all | bytes 262144 | tf_op jit(solution)/shard_map/all_to_all | solution.py:529
  117.0 0.8 next_kernel.1
  117.8 12.3 %all_to_all.45.recv = bf16[8,104,128]{2,1,0:T(8,128)(2,1)S(1)} all-to-all(bf16[8,104,128]{2,1,0:T(8,128)(2,1)S(1)} %get-tuple-element.28), channel_id=1, replica_groups=mesh['pages'=16,'row'=8,'col'=4] {'row'}, dimensions={0} | all-to-all | bytes 425984 | tf_op jit(solution)/shard_map/all_to_all | solution.py:529
  130.2 0.9 final_kernel.1
  (17 shorter events, 0.1 us)
Async XLA Ops:
  0.6 26.9 %copy-start.2 = (bf16[32,2,16,512]{3,2,1,0:T(8,128)(2,1)S(1)}, bf16[32,2,16,512]{3,2,1,0:T(8,128)(2,1)}, u32[]{:S(2)}) copy-start(bf16[32,2,16,512]{3,2,1,0:T(8,128)(2,1)} %tails.1) | copy-start | bytes 3145732
  2.9 7.5 %copy-start.14 = (bf16[256]{0:T(256)(128)(2,1)S(1)}, bf16[256]{0:T(256)(128)(2,1)}, u32[]{:S(2)}) copy-start(bf16[256]{0:T(256)(128)(2,1)} %param.38) | copy-start | bytes 1540
  2.9 7.5 %copy-start.15 = (bf16[256]{0:T(256)(128)(2,1)S(1)}, bf16[256]{0:T(256)(128)(2,1)}, u32[]{:S(2)}) copy-start(bf16[256]{0:T(256)(128)(2,1)} %param.39) | copy-start | bytes 1540
  2.9 7.5 %copy-start.16 = (bf16[256]{0:T(256)(128)(2,1)S(1)}, bf16[256]{0:T(256)(128)(2,1)}, u32[]{:S(2)}) copy-start(bf16[256]{0:T(256)(128)(2,1)} %param.34) | copy-start | bytes 1540
  2.9 7.5 %copy-start.17 = (bf16[192]{0:T(256)(128)(2,1)S(1)}, bf16[192]{0:T(256)(128)(2,1)}, u32[]{:S(2)}) copy-start(bf16[192]{0:T(256)(128)(2,1)} %param.41) | copy-start | bytes 1156
  2.9 7.5 %copy-start.18 = (bf16[64]{0:T(256)(128)(2,1)S(1)}, bf16[64]{0:T(256)(128)(2,1)}, u32[]{:S(2)}) copy-start(bf16[64]{0:T(256)(128)(2,1)} %param.30) | copy-start | bytes 388
  2.9 7.5 %copy-start.19 = (bf16[64]{0:T(256)(128)(2,1)S(1)}, bf16[64]{0:T(256)(128)(2,1)}, u32[]{:S(2)}) copy-start(bf16[64]{0:T(256)(128)(2,1)} %param.36) | copy-start | bytes 388
  2.9 8.2 %copy-start.5 = (bf16[32,2,64]{2,1,0:T(2,128)(2,1)S(1)}, bf16[32,2,64]{2,1,0:T(2,128)(2,1)}, u32[]{:S(2)}) copy-start(bf16[32,2,64]{2,1,0:T(2,128)(2,1)} %param.21) | copy-start | bytes 24580
  3.0 24.6 %all-to-all-start = ((bf16[16,144,128]{2,1,0:T(8,128)(2,1)}), bf16[16,144,128]{2,1,0:T(8,128)(2,1)S(1)}, u32[]{:S(2)}, u32[]{:S(2)}) async-start(bf16[16,144,128]{2,1,0:T(8,128)(2,1)} %send_kernel.1), calls=%async_computation | async-start | bytes 1179648 | tf_op jit(solution)/shard_map/all_to_all | solution.py:529
  10.3 0.7 copy-start.11
  10.3 0.7 copy-start.12
  10.3 0.7 copy-start.13
  11.0 0.7 copy-start.7
  11.1 0.7 copy-start.6
  11.1 0.7 copy-start.8
  11.1 0.7 copy-start.9
  27.5 5.8 %copy-start.10 = (bf16[32,2,3,512]{3,1,2,0:T(2,128)(2,1)S(1)}, bf16[32,2,3,512]{3,1,2,0:T(2,128)(2,1)}, u32[]{:S(2)}) copy-start(bf16[32,2,3,512]{3,1,2,0:T(2,128)(2,1)} %param.22) | copy-start | bytes 589828
  27.5 6.0 %copy-start = (bf16[256,2048]{1,0:T(8,128)(2,1)S(1)}, bf16[256,2048]{1,0:T(8,128)(2,1)}, u32[]{:S(2)}) copy-start(bf16[256,2048]{1,0:T(8,128)(2,1)} %weight.5) | copy-start | bytes 3145732
  28.8 4.7 %copy-start.1 = (bf16[256,1536]{1,0:T(8,128)(2,1)S(1)}, bf16[256,1536]{1,0:T(8,128)(2,1)}, u32[]{:S(2)}) copy-start(bf16[256,1536]{1,0:T(8,128)(2,1)} %weight.7) | copy-start | bytes 2359300
  28.8 12.7 %all-to-all-start.1 = ((bf16[16,4,640]{2,1,0:T(4,128)(2,1)}), bf16[16,4,640]{2,1,0:T(4,128)(2,1)S(1)}, u32[]{:S(2)}, u32[]{:S(2)}) async-start(bf16[16,4,640]{2,1,0:T(4,128)(2,1)} %tail_kernel.1), calls=%async_computation.1 | async-start | bytes 163840 | tf_op jit(solution)/shard_map/all_to_all | solution.py:529
  42.0 29.6 %copy-start.4 = (bf16[512,256]{1,0:T(8,128)(2,1)S(1)}, bf16[512,256]{1,0:T(8,128)(2,1)}, u32[]{:S(2)}) copy-start(bf16[512,256]{1,0:T(8,128)(2,1)} %weight.4) | copy-start | bytes 786436
  81.8 26.6 %copy-start.3 = (bf16[2048,256]{1,0:T(8,128)(2,1)S(1)}, bf16[2048,256]{1,0:T(8,128)(2,1)}, u32[]{:S(2)}) copy-start(bf16[2048,256]{1,0:T(8,128)(2,1)} %weight.6) | copy-start | bytes 3145732

commit v7 on v6

--- a/solution.py
+++ b/solution.py
@@ -454,13 +454,13 @@
         out[n] = total
 
 
-def next_kernel(recv, hidden, vectors, extra, weight, layer_out, out):
+def next_kernel(recv, hidden, vectors, extra, weight, own, out):
     values = hidden[...]
     for n in range(NCOL):
         values = values + recv[n].astype(f32)
     low = values.astype(bf16)
     values = low.astype(f32)
-    layer_out[...] = dot_t(low, own_columns()).astype(bf16)
+    own[...] = dot_t(low, own_columns()).astype(bf16)
     mean, spread, scaled = centred(values, vectors[1:2])
     scores = jnp.sum(values * vectors[2:3], axis=1, keepdims=True)
     lane = iota((ROWS, ROWS), 1)
@@ -479,7 +479,8 @@
         out[n, ROWS + half : ROWS + half + 8] = (extra[n] + rows).astype(bf16)
 
 
-def final_kernel(recv, vectors, projected_next, score_out, wide, edges):
+def final_kernel(recv, vectors, own, layer_out, projected_next, score_out, wide, edges):
+    layer_out[...] = own[...]
     width = projected_next.shape[2]
     half = ROWS // 2
     for n in range(NROW):
@@ -657,18 +658,18 @@
         down_kernel, ((NCOL, ROWS, BLOCK), bf16), [], [hidden_two, down_weight, vectors]
     )
     partial = exchange(partial, "col")
-    layer_out, partial = call(
+    own, partial = call(
         next_kernel,
         [((ROWS, share), bf16), ((NROW, ROWS + ROWS // 2 + 8, 128), bf16)],
         [],
         [partial, hidden_one, vectors, qkv_rows, qkv_weight],
     )
     partial = exchange(partial, "row")
-    projected_next, score_sum = call(
+    layer_out, projected_next, score_sum = call(
         final_kernel,
-        [((cont_local, 2, width), bf16), ((2, cont_local), f32)],
-        [],
-        [partial, vectors],
+        [((ROWS, share), bf16), ((cont_local, 2, width), bf16), ((2, cont_local), f32)],
+        [],
+        [partial, vectors, own],
         [pltpu.VMEM((ROWS, width), f32), pltpu.VMEM((ROWS, 128), f32)],
     )
     return (layer_out.reshape(cont_local, 2, share), score_sum.T, projected_next)

time: 132 us -> 131 us (level)
  no operation moved by 1% of the time
where the time goes in v7:
time: 131 us
  blocking collectives  85.8 us (65%)
  waiting for transfers between devices  21.2 us (16%)
  starting transfers between devices  11.9 us (9%)
  Pallas kernels  9.37 us (7%)
  local copies, waits for them, and re-layouts  1.6 us (1%)
    all_to_all x6, blocking collectives, exchange(): return lax.all_to_all(x, axis, split_axis=0, concat_axis=0, tiled=True)  85.8 us
    all_to_all x2, waiting for transfers between devices, exchange(): return lax.all_to_all(x, axis, split_axis=0, concat_axis=0, tiled=True)  21.2 us
    all_to_all x2, starting transfers between devices, exchange(): return lax.all_to_all(x, axis, split_axis=0, concat_axis=0, tiled=True)  11.9 us
    pallas_call x11, Pallas kernels, call(): pl.pallas_call(kernel, out_shape=shapes if many else shapes[0], in_specs=...  9.37 us
  transfers between devices with their start and end apart: 2, of which 2 were waited for; matrix products, arithmetic and copies ran while one was open for 0% of the time, Pallas kernels for 2%

profile of v7, /device:TPU:2, one launch (start us, length us, event | category | flops | bytes accessed | tf_op | source)
XLA Modules:
  0.0 130.8 jit_solution(4974998642965765625)
XLA Ops:
  0.6 2.2 %send_kernel.1 = bf16[16,144,128]{2,1,0:T(8,128)(2,1)} custom-call(s32[4,128]{1,0:T(4,128)} %bitcast.12, bf16[32,3,2,512]{3,2,1,0:T(2,128)(2,1)} %bitcast.14, bf16[16,2,16,512]{3,2,1,0:T(8,128)(2,1)} %pages.1), custom_call_target="tpu_custom_call" | custom-call | bytes 589824 | tf_op jit(solution)/shard_map/send_kernel/pallas_call | solution.py:517
  2.9 0.0 copy-start.14
  2.9 0.0 copy-start.15
  2.9 0.0 copy-start.16
  2.9 0.0 copy-start.17
  2.9 0.0 copy-start.18
  2.9 0.0 copy-start.19
  2.9 0.0 copy-start.5
  3.0 7.3 %all-to-all-start = ((bf16[16,144,128]{2,1,0:T(8,128)(2,1)}), bf16[16,144,128]{2,1,0:T(8,128)(2,1)S(1)}, u32[]{:S(2)}, u32[]{:S(2)}) async-start(bf16[16,144,128]{2,1,0:T(8,128)(2,1)} %send_kernel.1), calls=%async_computation | async-start | bytes 1179648 | tf_op jit(solution)/shard_map/all_to_all | solution.py:530
  10.3 0.0 copy-start.11
  10.3 0.0 copy-start.12
  10.3 0.0 copy-start.13
  10.4 0.0 copy-done.14
  10.4 0.0 copy-done.15
  10.4 0.0 copy-done.16
  10.4 0.0 copy-done.17
  10.4 0.0 copy-done.18
  10.4 0.0 copy-done.19
  10.4 0.6 copy-done.11
  11.0 0.0 copy-done.12
  11.0 0.0 copy-done.13
  11.0 0.1 concatenate.3
  11.1 0.6 copy-done.7
  11.7 0.1 copy-done.6
  11.8 0.0 copy-done.8
  11.8 1.0 ready_kernel.1
  12.8 14.8 %all-to-all-done.recv = bf16[16,144,128]{2,1,0:T(8,128)(2,1)S(1)} async-done(((bf16[16,144,128]{2,1,0:T(8,128)(2,1)}), bf16[16,144,128]{2,1,0:T(8,128)(2,1)S(1)}, u32[]{:S(2)}, u32[]{:S(2)}) %all-to-all-start) | async-done | bytes 589856 | tf_op jit(solution)/shard_map/all_to_all | solution.py:530
  27.5 0.0 copy-done.2
  27.5 1.2 tail_kernel.1
  28.8 4.5 %all-to-all-start.1 = ((bf16[16,4,640]{2,1,0:T(4,128)(2,1)}), bf16[16,4,640]{2,1,0:T(4,128)(2,1)S(1)}, u32[]{:S(2)}, u32[]{:S(2)}) async-start(bf16[16,4,640]{2,1,0:T(4,128)(2,1)} %tail_kernel.1), calls=%async_computation.1 | async-start | bytes 163840 | tf_op jit(solution)/shard_map/all_to_all | solution.py:530
  33.3 0.1 copy.25
  33.5 1.4 %prefix_kernel.1 = (f32[64,640]{1,0:T(8,128)S(1)}, f32[8,8,256]{2,1,0:T(8,128)S(1)}, f32[8,8,128]{2,1,0:T(8,128)S(1)}) custom-call(bf16[64,1536]{1,0:T(8,128)(2,1)S(1)} %bitcast.9, bf16[16,144,128]{2,1,0:T(8,128)(2,1)S(1)} %all-to-all-done.recv, f32[64,256]{1,0:T(8,128)S(1)} %get-tuple-element.19.distance, f32[8,256]{1,0:T(8,128)S(1)} %get-tuple-element.20.vectors, ...), custom_call_target="tpu_custom_call" | custom-call | bytes 2957312 | tf_op jit(solution)/shard_map/prefix_kernel/pallas_call | solution.py:517
  34.9 6.5 %all-to-all-done.1.recv = bf16[16,4,640]{2,1,0:T(4,128)(2,1)S(1)} async-done(((bf16[16,4,640]{2,1,0:T(4,128)(2,1)}), bf16[16,4,640]{2,1,0:T(4,128)(2,1)S(1)}, u32[]{:S(2)}, u32[]{:S(2)}) %all-to-all-start.1) | async-done | bytes 81952 | tf_op jit(solution)/shard_map/all_to_all | solution.py:530
  41.4 0.5 join_kernel.1
  42.0 0.0 copy-start.4
  42.0 29.6 %all_to_all.40.recv = bf16[8,72,512]{2,1,0:T(8,128)(2,1)S(1)} all-to-all(bf16[8,72,512]{2,1,0:T(8,128)(2,1)S(1)} %join_kernel.1), channel_id=1, replica_groups=mesh['pages'=16,'row'=8,'col'=4] {'row'}, dimensions={0} | all-to-all | bytes 1179648 | tf_op jit(solution)/shard_map/all_to_all | solution.py:530
  71.6 0.5 out_kernel.1
  72.1 9.1 %all_to_all.41.recv = bf16[4,64,256]{2,1,0:T(8,128)(2,1)S(1)} all-to-all(bf16[4,64,256]{2,1,0:T(8,128)(2,1)S(1)} %out_kernel.1), channel_id=1, replica_groups=mesh['pages'=16,'row'=8,'col'=4] {'col'}, dimensions={0} | all-to-all | bytes 262144 | tf_op jit(solution)/shard_map/all_to_all | solution.py:530
  81.2 0.5 up_kernel.1
  81.8 0.0 copy-start.3
  81.8 13.5 %all_to_all.42.recv = bf16[8,72,256]{2,1,0:T(8,128)(2,1)S(1)} all-to-all(bf16[8,72,256]{2,1,0:T(8,128)(2,1)S(1)} %get-tuple-element.25), channel_id=1, replica_groups=mesh['pages'=16,'row'=8,'col'=4] {'row'}, dimensions={0} | all-to-all | bytes 589824 | tf_op jit(solution)/shard_map/all_to_all | solution.py:530
  95.2 0.2 hidden_kernel.1
  95.5 12.9 %all_to_all.43.recv = bf16[8,64,256]{2,1,0:T(8,128)(2,1)S(1)} all-to-all(bf16[8,64,256]{2,1,0:T(8,128)(2,1)S(1)} %hidden_kernel.1), channel_id=1, replica_groups=mesh['pages'=16,'row'=8,'col'=4] {'row'}, dimensions={0} | all-to-all | bytes 524288 | tf_op jit(solution)/shard_map/all_to_all | solution.py:530
  108.4 0.3 down_kernel.1
  108.7 8.4 %all_to_all.44.recv = bf16[4,64,256]{2,1,0:T(8,128)(2,1)S(1)} all-to-all(bf16[4,64,256]{2,1,0:T(8,128)(2,1)S(1)} %down_kernel.1), channel_id=1, replica_groups=mesh['pages'=16,'row'=8,'col'=4] {'col'}, dimensions={0} | all-to-all | bytes 262144 | tf_op jit(solution)/shard_map/all_to_all | solution.py:530
  117.0 0.6 next_kernel.1
  117.6 12.3 %all_to_all.45.recv = bf16[8,104,128]{2,1,0:T(8,128)(2,1)S(1)} all-to-all(bf16[8,104,128]{2,1,0:T(8,128)(2,1)S(1)} %get-tuple-element.28), channel_id=1, replica_groups=mesh['pages'=16,'row'=8,'col'=4] {'row'}, dimensions={0} | all-to-all | bytes 425984 | tf_op jit(solution)/shard_map/all_to_all | solution.py:530
  130.0 0.9 final_kernel.1
  (17 shorter events, 0.1 us)
Async XLA Ops:
  0.6 26.9 %copy-start.2 = (bf16[32,2,16,512]{3,2,1,0:T(8,128)(2,1)S(1)}, bf16[32,2,16,512]{3,2,1,0:T(8,128)(2,1)}, u32[]{:S(2)}) copy-start(bf16[32,2,16,512]{3,2,1,0:T(8,128)(2,1)} %tails.1) | copy-start | bytes 3145732
  2.9 7.5 %copy-start.14 = (bf16[256]{0:T(256)(128)(2,1)S(1)}, bf16[256]{0:T(256)(128)(2,1)}, u32[]{:S(2)}) copy-start(bf16[256]{0:T(256)(128)(2,1)} %param.38) | copy-start | bytes 1540
  2.9 7.5 %copy-start.15 = (bf16[256]{0:T(256)(128)(2,1)S(1)}, bf16[256]{0:T(256)(128)(2,1)}, u32[]{:S(2)}) copy-start(bf16[256]{0:T(256)(128)(2,1)} %param.39) | copy-start | bytes 1540
  2.9 7.5 %copy-start.16 = (bf16[256]{0:T(256)(128)(2,1)S(1)}, bf16[256]{0:T(256)(128)(2,1)}, u32[]{:S(2)}) copy-start(bf16[256]{0:T(256)(128)(2,1)} %param.34) | copy-start | bytes 1540
  2.9 7.5 %copy-start.17 = (bf16[192]{0:T(256)(128)(2,1)S(1)}, bf16[192]{0:T(256)(128)(2,1)}, u32[]{:S(2)}) copy-start(bf16[192]{0:T(256)(128)(2,1)} %param.41) | copy-start | bytes 1156
  2.9 7.5 %copy-start.18 = (bf16[64]{0:T(256)(128)(2,1)S(1)}, bf16[64]{0:T(256)(128)(2,1)}, u32[]{:S(2)}) copy-start(bf16[64]{0:T(256)(128)(2,1)} %param.30) | copy-start | bytes 388
  2.9 7.5 %copy-start.19 = (bf16[64]{0:T(256)(128)(2,1)S(1)}, bf16[64]{0:T(256)(128)(2,1)}, u32[]{:S(2)}) copy-start(bf16[64]{0:T(256)(128)(2,1)} %param.36) | copy-start | bytes 388
  2.9 8.2 %copy-start.5 = (bf16[32,2,64]{2,1,0:T(2,128)(2,1)S(1)}, bf16[32,2,64]{2,1,0:T(2,128)(2,1)}, u32[]{:S(2)}) copy-start(bf16[32,2,64]{2,1,0:T(2,128)(2,1)} %param.21) | copy-start | bytes 24580
  3.0 24.6 %all-to-all-start = ((bf16[16,144,128]{2,1,0:T(8,128)(2,1)}), bf16[16,144,128]{2,1,0:T(8,128)(2,1)S(1)}, u32[]{:S(2)}, u32[]{:S(2)}) async-start(bf16[16,144,128]{2,1,0:T(8,128)(2,1)} %send_kernel.1), calls=%async_computation | async-start | bytes 1179648 | tf_op jit(solution)/shard_map/all_to_all | solution.py:530
  10.3 0.7 copy-start.11
  10.3 0.7 copy-start.12
  10.3 0.7 copy-start.13
  11.0 0.7 copy-start.7
  11.1 0.7 copy-start.6
  11.1 0.7 copy-start.8
  11.1 0.7 copy-start.9
  27.5 5.8 %copy-start.10 = (bf16[32,2,3,512]{3,1,2,0:T(2,128)(2,1)S(1)}, bf16[32,2,3,512]{3,1,2,0:T(2,128)(2,1)}, u32[]{:S(2)}) copy-start(bf16[32,2,3,512]{3,1,2,0:T(2,128)(2,1)} %param.22) | copy-start | bytes 589828
  27.5 6.0 %copy-start = (bf16[256,2048]{1,0:T(8,128)(2,1)S(1)}, bf16[256,2048]{1,0:T(8,128)(2,1)}, u32[]{:S(2)}) copy-start(bf16[256,2048]{1,0:T(8,128)(2,1)} %weight.5) | copy-start | bytes 3145732
  28.8 4.7 %copy-start.1 = (bf16[256,1536]{1,0:T(8,128)(2,1)S(1)}, bf16[256,1536]{1,0:T(8,128)(2,1)}, u32[]{:S(2)}) copy-start(bf16[256,1536]{1,0:T(8,128)(2,1)} %weight.7) | copy-start | bytes 2359300
  28.8 12.7 %all-to-all-start.1 = ((bf16[16,4,640]{2,1,0:T(4,128)(2,1)}), bf16[16,4,640]{2,1,0:T(4,128)(2,1)S(1)}, u32[]{:S(2)}, u32[]{:S(2)}) async-start(bf16[16,4,640]{2,1,0:T(4,128)(2,1)} %tail_kernel.1), calls=%async_computation.1 | async-start | bytes 163840 | tf_op jit(solution)/shard_map/all_to_all | solution.py:530
  42.0 29.6 %copy-start.4 = (bf16[512,256]{1,0:T(8,128)(2,1)S(1)}, bf16[512,256]{1,0:T(8,128)(2,1)}, u32[]{:S(2)}) copy-start(bf16[512,256]{1,0:T(8,128)(2,1)} %weight.4) | copy-start | bytes 786436
  81.8 26.6 %copy-start.3 = (bf16[2048,256]{1,0:T(8,128)(2,1)S(1)}, bf16[2048,256]{1,0:T(8,128)(2,1)}, u32[]{:S(2)}) copy-start(bf16[2048,256]{1,0:T(8,128)(2,1)} %weight.6) | copy-start | bytes 3145732
